TPU v7x, 256 devices: a whole 4x4x8 slice. The times are simulated.
256 devices in a mesh: layer: 16 (over z_hi, x, core), sub: 16 (over y, z_lo).
Axes of the slice: x: 4, y: 4, z: 8 (z_hi: 2, z_lo: 4; z = z_hi * 4 + z_lo), core: 2. Of those that a mesh axis runs over, the one named last changes fastest.
Arguments:
- screens: float32 [16, 7, 2048, 640], P('layer', None, None, 'sub'), may hold values from -4 to 4
- new_columns: float32 [10, 16, 2048, 8], P(None, 'layer'), may hold values from -4 to 4
- col_block: int32 [10, 16], P(None, 'layer'), may hold values from 240 to 319
- shift_x: int32 [10, 16, 6], P(None, 'layer'), may hold values from -40 to 40, as said below
- shift_y: int32 [10, 16, 6], P(None, 'layer'), may hold values from -40 to 40, as said below
- valid: int32 [80, 80], P('layer', 'sub'), may hold values 0 or 1
- recon: bfloat16 [6, 2, 80, 80, 5376], P(None, None, 'layer', 'sub'), may hold values from -0.0234375 to 0.0234375
Outputs:
- slopes: float32 [10, 6, 2, 80, 80], P(None, None, None, 'layer', 'sub')
- commands: float32 [10, 5376], replicated
Inputs may be any that keep to these rules, and one draw needn't show every extreme that they name: `shift_x`: column shifts reach both -40 and 40 in every draw. `shift_y`: row shifts reach both -40 and 40 in every draw.
All inputs are finite; a program needn't handle non-finite values. No bound on the sum of `valid` on one device may be relied on, other than what follows from the above.
Results may differ from a plain program's by a relative error of at most 0.0029.
Values sent between devices are 32-bit elements; how exact they have to be, the bound alone decides.
No kernel may reach another device: no remote copies, remote signals or barrier semaphores. Data moves between devices by JAX's collectives and lax.ppermute only.
A program may use at most 64 MiB of HBM per device.

v0:
```python
import math

import jax
import jax.numpy as jnp
from jax import lax
from jax.sharding import PartitionSpec as P

FFT_LEN = 16
ACTS = 5376
HALO = 40
NEW_COLS = 8
PUP = 640
PUP_TURN = 3
ROW0 = 704


def extended_2(block, sides, width):
    for axis, dim in sides:
        count = lax.axis_size(axis)
        forward = [(i, i + 1) for i in range(count - 1)]
        forward.append((count - 1, 0))
        backward = [(target, source) for source, target in forward]
        low = lax.ppermute(
            lax.slice_in_dim(block, block.shape[dim] - width, None, axis=dim), axis, forward
        )
        high = lax.ppermute(lax.slice_in_dim(block, 0, width, axis=dim), axis, backward)
        block = jnp.concatenate([low, block, high], axis=dim)
    return block


def lenslet_slopes(phase, valid, fft_len):
    stars, rows, cols = phase.shape
    subs_r, subs_c = valid.shape
    pix = rows // subs_r
    tiles = phase.reshape(stars, subs_r, pix, subs_c, pix)
    tiles = jnp.transpose(tiles, (2, 4, 0, 1, 3)).reshape(pix, pix, stars * subs_r * subs_c)
    freq = jnp.arange(fft_len).astype(jnp.float32)
    place = jnp.arange(pix).astype(jnp.float32)
    angle = 2.0 * math.pi / fft_len * freq[:, None] * place[None, :]
    cosine = jnp.cos(angle)
    sine = -jnp.sin(angle)
    real_part = jnp.cos(tiles)
    imag_part = jnp.sin(tiles)
    highest = lax.Precision.HIGHEST

    def along_rows(mat, field):
        return jnp.einsum("kn,nms->kms", mat, field, precision=highest)

    def along_cols(field, mat):
        return jnp.einsum("kms,qm->kqs", field, mat, precision=highest)

    first_re = along_rows(cosine, real_part) - along_rows(sine, imag_part)
    first_im = along_rows(cosine, imag_part) + along_rows(sine, real_part)
    spot_re = along_cols(first_re, cosine) - along_cols(first_im, sine)
    spot_im = along_cols(first_re, sine) + along_cols(first_im, cosine)
    power = spot_re * spot_re + spot_im * spot_im
    centred = ((jnp.arange(fft_len) + fft_len // 2) % fft_len - fft_len // 2).astype(jnp.float32)
    total = jnp.sum(power, axis=(0, 1))
    along_x = jnp.sum(power * centred[None, :, None], axis=(0, 1)) / total
    along_y = jnp.sum(power * centred[:, None, None], axis=(0, 1)) / total
    result = jnp.stack([along_x, along_y]).reshape(2, stars, subs_r, subs_c)
    return jnp.transpose(result, (1, 0, 2, 3)) * valid.astype(jnp.float32)[None, None]


def place_columns(strips, fresh, block, owner, width):
    column = block * NEW_COLS
    turn = column // PUP
    start = column % PUP - owner * width
    inside = (start >= 0) & (start < width)
    offset = jnp.clip(start, 0, width - NEW_COLS)
    placed = lax.dynamic_update_slice(strips, fresh[None], (turn, jnp.int32(0), offset))
    return jnp.where(inside, placed, strips)


def cut_window(extended, step_x, step_y, width):
    return lax.dynamic_slice(extended, (HALO + step_y, HALO + step_x), (PUP, width))


def local(screens, new_columns, col_block, shift_x, shift_y, valid, recon):
    width = screens.shape[3]
    owner = lax.axis_index("sub")
    last = lax.axis_size("sub") - 1
    matrix = recon.reshape(-1, ACTS)

    def advance(strips, inputs):
        fresh, blocks, step_x, step_y = inputs
        strips = jax.vmap(lambda s, f, b: place_columns(s, f, b, owner, width))(
            strips, fresh, blocks
        )
        band = strips[:, PUP_TURN - 1 : PUP_TURN + 2, ROW0 - HALO : ROW0 + PUP + HALO, :]
        before = band[:, 0]
        core = band[:, 1]
        after = band[:, 2]
        tail_cols = jnp.where(owner == last, before, core)
        head_cols = jnp.where(owner == 0, after, core)
        rims = jnp.concatenate([head_cols, tail_cols], axis=2)
        padded = extended_2(rims, (("sub", 2),), HALO)
        extended = jnp.concatenate(
            [padded[:, :, :HALO], core, padded[:, :, padded.shape[2] - HALO :]], axis=2
        )
        window = jax.vmap(
            jax.vmap(lambda e, x, y: cut_window(e, x, y, width), in_axes=(None, 0, 0))
        )(extended, step_x, step_y)
        summed = lax.all_to_all(window, "layer", split_axis=2, concat_axis=0, tiled=True)
        phase = jnp.sum(summed, axis=0)
        slopes = lenslet_slopes(phase, valid, FFT_LEN)
        flat = slopes.astype(jnp.bfloat16).reshape(-1)
        partial_cmd = jnp.dot(flat, matrix, preferred_element_type=jnp.float32)
        command = lax.psum(partial_cmd, ("layer", "sub"))
        return (strips, (slopes, command))

    final, (slopes, commands) = lax.scan(
        advance, screens, (new_columns, col_block, shift_x, shift_y)
    )
    return (slopes, commands)


def solution(mesh):
    return jax.shard_map(
        local,
        mesh=mesh,
        in_specs=(
            P("layer", None, None, "sub"),
            P(None, "layer", None, None),
            P(None, "layer"),
            P(None, "layer", None),
            P(None, "layer", None),
            P("layer", "sub"),
            P(None, None, "layer", "sub", None),
        ),
        out_specs=(P(None, None, None, "layer", "sub"), P()),
        check_vma=False,
    )
```

profile of v0, /device:TPU:1, one launch (start us, length us, event | category | flops | bytes accessed | tf_op | source)
XLA Modules:
  0.0 1927.7 jit_solution(1306856155262718636)
XLA Ops:
  5.4 7.2 reshape.421
  17.1 1908.5 %while.21 = (s32[]{:T(128)}, f32[1,7,2048,40]{3,2,1,0:T(8,128)}, f32[10,6,2,5,5]{1,2,4,3,0:T(2,128)}, f32[10,5376]{1,0:T(8,128)}, s32[10,1]{0,1:T(1,128)S(1)}, /...) while((s32[]{:T(128)}, f32[1,7,2048,40]{3,2,1,0:T(8,128)}, ...), condition=%wide.region_7.8_spmd, body=%wide.region_0.7_spmd.sunk | while | flops 26182216 | bytes 32231552 | solution.py:112
  27.7 7.2 select_n.167
  50.5 8.9 collective-permute-done.1
  60.6 12.9 while.22
  87.0 10.3 all-to-all-start
  97.3 18.9 all-to-all-done
  137.5 75.3 %psum.12 = f32[1,5376]{1,0:T(1,128)S(1)} all-reduce(f32[1,5376]{1,0:T(1,128)S(1)} %fusion.108), channel_id=1, replica_groups=mesh['layer'=16,'sub'=16] {'layer','sub'}, use_global_device_ids=true, to_apply=%region_6.6 | all-reduce | flops 5376 | bytes 43008 | tf_op jit(solution)/shard_map/while/body/eval_jaxpr/psum | solution.py:109
  225.7 7.2 select_n.167
  244.0 7.8 collective-permute-done.1
  253.0 12.9 while.22
  285.7 15.2 all-to-all-done
  322.2 80.5 %psum.12 = f32[1,5376]{1,0:T(1,128)S(1)} all-reduce(f32[1,5376]{1,0:T(1,128)S(1)} %fusion.108), channel_id=1, replica_groups=mesh['layer'=16,'sub'=16] {'layer','sub'}, use_global_device_ids=true, to_apply=%region_6.6 | all-reduce | flops 5376 | bytes 43008 | tf_op jit(solution)/shard_map/while/body/eval_jaxpr/psum | solution.py:109
  415.6 7.2 select_n.167
  433.7 9.0 collective-permute-done.1
  443.9 12.9 while.22
  476.2 15.4 all-to-all-done
  512.9 80.4 %psum.12 = f32[1,5376]{1,0:T(1,128)S(1)} all-reduce(f32[1,5376]{1,0:T(1,128)S(1)} %fusion.108), channel_id=1, replica_groups=mesh['layer'=16,'sub'=16] {'layer','sub'}, use_global_device_ids=true, to_apply=%region_6.6 | all-reduce | flops 5376 | bytes 43008 | tf_op jit(solution)/shard_map/while/body/eval_jaxpr/psum | solution.py:109
  606.3 7.2 select_n.167
  624.3 8.5 collective-permute-done.1
  634.0 12.9 while.22
  666.3 15.7 all-to-all-done
  703.3 80.2 %psum.12 = f32[1,5376]{1,0:T(1,128)S(1)} all-reduce(f32[1,5376]{1,0:T(1,128)S(1)} %fusion.108), channel_id=1, replica_groups=mesh['layer'=16,'sub'=16] {'layer','sub'}, use_global_device_ids=true, to_apply=%region_6.6 | all-reduce | flops 5376 | bytes 43008 | tf_op jit(solution)/shard_map/while/body/eval_jaxpr/psum | solution.py:109
  814.4 8.3 collective-permute-done.1
  824.0 12.9 while.22
  856.3 15.7 all-to-all-done
  893.2 80.1 %psum.12 = f32[1,5376]{1,0:T(1,128)S(1)} all-reduce(f32[1,5376]{1,0:T(1,128)S(1)} %fusion.108), channel_id=1, replica_groups=mesh['layer'=16,'sub'=16] {'layer','sub'}, use_global_device_ids=true, to_apply=%region_6.6 | all-reduce | flops 5376 | bytes 43008 | tf_op jit(solution)/shard_map/while/body/eval_jaxpr/psum | solution.py:109
  997.4 8.3 collective-permute-done
  1013.9 12.9 while.22
  1046.3 15.7 all-to-all-done
  1083.2 80.2 %psum.12 = f32[1,5376]{1,0:T(1,128)S(1)} all-reduce(f32[1,5376]{1,0:T(1,128)S(1)} %fusion.108), channel_id=1, replica_groups=mesh['layer'=16,'sub'=16] {'layer','sub'}, use_global_device_ids=true, to_apply=%region_6.6 | all-reduce | flops 5376 | bytes 43008 | tf_op jit(solution)/shard_map/while/body/eval_jaxpr/psum | solution.py:109
  1194.3 7.4 collective-permute-done.1
  1203.0 12.9 while.22
  1236.3 15.7 all-to-all-done
  1273.2 80.2 %psum.12 = f32[1,5376]{1,0:T(1,128)S(1)} all-reduce(f32[1,5376]{1,0:T(1,128)S(1)} %fusion.108), channel_id=1, replica_groups=mesh['layer'=16,'sub'=16] {'layer','sub'}, use_global_device_ids=true, to_apply=%region_6.6 | all-reduce | flops 5376 | bytes 43008 | tf_op jit(solution)/shard_map/while/body/eval_jaxpr/psum | solution.py:109
  1384.3 8.4 collective-permute-done.1
  1394.0 12.9 while.22
  1426.3 15.7 all-to-all-done
  1463.2 80.2 %psum.12 = f32[1,5376]{1,0:T(1,128)S(1)} all-reduce(f32[1,5376]{1,0:T(1,128)S(1)} %fusion.108), channel_id=1, replica_groups=mesh['layer'=16,'sub'=16] {'layer','sub'}, use_global_device_ids=true, to_apply=%region_6.6 | all-reduce | flops 5376 | bytes 43008 | tf_op jit(solution)/shard_map/while/body/eval_jaxpr/psum | solution.py:109
  1567.4 8.3 collective-permute-done
  1583.9 12.9 while.22
  1616.3 15.7 all-to-all-done
  1653.2 80.2 %psum.12 = f32[1,5376]{1,0:T(1,128)S(1)} all-reduce(f32[1,5376]{1,0:T(1,128)S(1)} %fusion.108), channel_id=1, replica_groups=mesh['layer'=16,'sub'=16] {'layer','sub'}, use_global_device_ids=true, to_apply=%region_6.6 | all-reduce | flops 5376 | bytes 43008 | tf_op jit(solution)/shard_map/while/body/eval_jaxpr/psum | solution.py:109
  1757.4 7.4 collective-permute-done
  1764.8 7.8 collective-permute-done.1
  1773.9 12.9 while.22
  1806.3 15.7 all-to-all-done
  1843.2 80.1 %psum.12 = f32[1,5376]{1,0:T(1,128)S(1)} all-reduce(f32[1,5376]{1,0:T(1,128)S(1)} %fusion.108), channel_id=1, replica_groups=mesh['layer'=16,'sub'=16] {'layer','sub'}, use_global_device_ids=true, to_apply=%region_6.6 | all-reduce | flops 5376 | bytes 43008 | tf_op jit(solution)/shard_map/while/body/eval_jaxpr/psum | solution.py:109
  (786 shorter events, 810.2 us)
Async XLA Ops:
  5.4 7.2 copy-start.1
  12.6 4.3 copy-start.5
  12.6 4.4 copy-start.6
  12.6 4.5 copy-start.4
  12.6 4.5 copy-start.2
  12.6 4.5 copy-start.3
  12.7 4.5 copy-start.7
  36.2 14.2 collective-permute-start
  43.1 16.2 collective-permute-start.1
  87.0 29.2 %all-to-all-start = ((f32[16,1,9600]{2,1,0:T(1,128)}), f32[16,1,9600]{2,1,0:T(1,128)S(1)}, u32[]{:S(2)}, u32[]{:S(2)}) async-start(f32[16,1,9600]{2,1,0:T(1,128)} %reshape.457), calls=%async_computation | async-start | bytes 1228800 | tf_op jit(solution)/shard_map/while/body/eval_jaxpr/all_to_all | solution.py:104
  127.2 9.8 copy-start
  234.2 9.8 collective-permute-start
  235.6 16.2 collective-permute-start.1
  279.5 21.5 %all-to-all-start = ((f32[16,1,9600]{2,1,0:T(1,128)}), f32[16,1,9600]{2,1,0:T(1,128)S(1)}, u32[]{:S(2)}, u32[]{:S(2)}) async-start(f32[16,1,9600]{2,1,0:T(1,128)} %reshape.457), calls=%async_computation | async-start | bytes 1228800 | tf_op jit(solution)/shard_map/while/body/eval_jaxpr/all_to_all | solution.py:104
  311.9 9.8 copy-start
  424.1 9.5 collective-permute-start
  426.3 16.4 collective-permute-start.1
  470.3 21.3 %all-to-all-start = ((f32[16,1,9600]{2,1,0:T(1,128)}), f32[16,1,9600]{2,1,0:T(1,128)S(1)}, u32[]{:S(2)}, u32[]{:S(2)}) async-start(f32[16,1,9600]{2,1,0:T(1,128)} %reshape.457), calls=%async_computation | async-start | bytes 1228800 | tf_op jit(solution)/shard_map/while/body/eval_jaxpr/all_to_all | solution.py:104
  502.6 9.8 copy-start
  614.8 9.5 collective-permute-start
  616.4 16.4 collective-permute-start.1
  660.4 21.6 %all-to-all-start = ((f32[16,1,9600]{2,1,0:T(1,128)}), f32[16,1,9600]{2,1,0:T(1,128)S(1)}, u32[]{:S(2)}, u32[]{:S(2)}) async-start(f32[16,1,9600]{2,1,0:T(1,128)} %reshape.457), calls=%async_computation | async-start | bytes 1228800 | tf_op jit(solution)/shard_map/while/body/eval_jaxpr/all_to_all | solution.py:104
  692.9 9.8 copy-start
  804.9 9.5 collective-permute-start
  806.4 16.3 collective-permute-start.1
  850.4 21.6 %all-to-all-start = ((f32[16,1,9600]{2,1,0:T(1,128)}), f32[16,1,9600]{2,1,0:T(1,128)S(1)}, u32[]{:S(2)}, u32[]{:S(2)}) async-start(f32[16,1,9600]{2,1,0:T(1,128)} %reshape.457), calls=%async_computation | async-start | bytes 1228800 | tf_op jit(solution)/shard_map/while/body/eval_jaxpr/all_to_all | solution.py:104
  882.9 9.8 copy-start
  994.8 11.0 collective-permute-start
  996.4 16.3 collective-permute-start.1
  1040.3 21.6 %all-to-all-start = ((f32[16,1,9600]{2,1,0:T(1,128)}), f32[16,1,9600]{2,1,0:T(1,128)S(1)}, u32[]{:S(2)}, u32[]{:S(2)}) async-start(f32[16,1,9600]{2,1,0:T(1,128)} %reshape.457), calls=%async_computation | async-start | bytes 1228800 | tf_op jit(solution)/shard_map/while/body/eval_jaxpr/all_to_all | solution.py:104
  1072.9 9.8 copy-start
  1184.8 9.5 collective-permute-start
  1186.3 15.4 collective-permute-start.1
  1229.4 22.5 %all-to-all-start = ((f32[16,1,9600]{2,1,0:T(1,128)}), f32[16,1,9600]{2,1,0:T(1,128)S(1)}, u32[]{:S(2)}, u32[]{:S(2)}) async-start(f32[16,1,9600]{2,1,0:T(1,128)} %reshape.457), calls=%async_computation | async-start | bytes 1228800 | tf_op jit(solution)/shard_map/while/body/eval_jaxpr/all_to_all | solution.py:104
  1262.9 9.8 copy-start
  1374.8 9.5 collective-permute-start
  1376.4 16.4 collective-permute-start.1
  1420.4 21.6 %all-to-all-start = ((f32[16,1,9600]{2,1,0:T(1,128)}), f32[16,1,9600]{2,1,0:T(1,128)S(1)}, u32[]{:S(2)}, u32[]{:S(2)}) async-start(f32[16,1,9600]{2,1,0:T(1,128)} %reshape.457), calls=%async_computation | async-start | bytes 1228800 | tf_op jit(solution)/shard_map/while/body/eval_jaxpr/all_to_all | solution.py:104
  1452.9 9.8 copy-start
  1564.8 11.0 collective-permute-start
  1566.4 16.3 collective-permute-start.1
  1610.4 21.6 %all-to-all-start = ((f32[16,1,9600]{2,1,0:T(1,128)}), f32[16,1,9600]{2,1,0:T(1,128)S(1)}, u32[]{:S(2)}, u32[]{:S(2)}) async-start(f32[16,1,9600]{2,1,0:T(1,128)} %reshape.457), calls=%async_computation | async-start | bytes 1228800 | tf_op jit(solution)/shard_map/while/body/eval_jaxpr/all_to_all | solution.py:104
  1642.9 9.8 copy-start
  1754.8 10.1 collective-permute-start
  1756.3 16.3 collective-permute-start.1
  1800.3 21.7 %all-to-all-start = ((f32[16,1,9600]{2,1,0:T(1,128)}), f32[16,1,9600]{2,1,0:T(1,128)S(1)}, u32[]{:S(2)}, u32[]{:S(2)}) async-start(f32[16,1,9600]{2,1,0:T(1,128)} %reshape.457), calls=%async_computation | async-start | bytes 1228800 | tf_op jit(solution)/shard_map/while/body/eval_jaxpr/all_to_all | solution.py:104
  1832.9 9.8 copy-start
where the time goes:
time: 1940 us; the launch traced here: 1930 us
  blocking collectives  797 us (41%)
  local copies, waits for them, and re-layouts  469 us (24%)
  waiting for transfers between devices  310 us (16%)
  other arithmetic  196 us (10%)
  starting transfers between devices  86.3 us (4%)
  matrix products  44.6 us (2%)
  loops' own time  23.6 us (1%)
    psum x10, blocking collectives, advance(): command = lax.psum(partial_cmd, ('layer', 'sub'))  797 us
    all_to_all x10, waiting for transfers between devices, advance(): lax.all_to_all(window, 'layer', split_axis=2, concat_axis=0, tiled=True)  159 us
    gather x180, local copies, waits for them, and re-layouts  127 us
    while x60, local copies, waits for them, and re-layouts  99.3 us
    ppermute x10, waiting for transfers between devices, extended_2(): lax.ppermute(lax.slice_in_dim(block, block.shape[dim] - width, None, axis...  79.8 us
    select_n x10, local copies, waits for them, and re-layouts, place_columns(): return jnp.where(inside, placed, strips)  72.2 us
    ppermute x10, waiting for transfers between devices, extended_2(): lax.ppermute(lax.slice_in_dim(block, 0, width, axis=dim), axis, backward)  71.4 us
    while x20, other arithmetic  71.1 us
  transfers between devices with their start and end apart: 30, of which 30 were waited for; matrix products, arithmetic and copies ran while one was open for 1% of the time, Pallas kernels for 0%

commit v1 on v0

v1 whole, which is shorter than its diff:
```python
import math
import jax
import jax.numpy as jnp
import numpy as np
from jax import lax
from jax.experimental import pallas as pl
from jax.experimental.pallas import tpu as pltpu
from jax.sharding import PartitionSpec as P

ACTS = 5376
HALO = 40
NEW_COLS = 8
PUP = 640
PUP_TURN = 3
ROW0 = 704
STEPS = 10
STARS = 6
PIX = 8
LANES = 128
LANE0 = 640
KEPT = 768
FIRST = ROW0 - HALO - LANE0
WINDOW = 120
UPDATES = STEPS * NEW_COLS
META = WINDOW + UPDATES
PAYLOAD = META + 8
ROLL_AT = 64
SLAB_TILES = 3
SLAB_ROWS = 32
FLAT = 300
FLAT_PAD = 384
HIGHEST = lax.Precision.HIGHEST


def toeplitz():
    d = np.arange(PIX)[:, None] - np.arange(PIX)[None, :]
    safe = np.where(d == 0, 1, d)
    return np.where(d == 0, 0.0, -4.0 * (-1.0) ** d / np.tan(np.pi * safe / 16))


def sublane_table():
    t = toeplitz()
    x = np.arange(PIX)
    rows = [t[x, (x - d) % PIX] for d in range(1, PIX)]
    rows.append((-1.0) ** x)
    return np.repeat(np.concatenate(rows)[:, None], LANES, axis=1).astype(np.float32)


def lane_table():
    t = toeplitz()
    table = np.zeros((LANES, 3 * LANES))
    for lane in range(WINDOW):
        group, y = divmod(lane, PIX)
        for z in range(PIX):
            table[group * PIX + z, lane] = t[y, z]
        table[lane, LANES + group] = (-1.0) ** y
        table[lane, 2 * LANES + group] = 1.0 / 1024
    return table.astype(np.float32)


def order_table():
    table = np.zeros((FLAT_PAD, FLAT_PAD), np.float32)
    for s in range(2):
        for k in range(2):
            for b in range(5):
                for kk in range(3):
                    for a in range(5):
                        row = (s * 10 + k * 5 + b) * 16 + kk * 5 + a
                        table[row, (((3 * k + kk) * 5 + a) * 5 + b) * 2 + s] = 1.0
    return table


def lane_index(shape):
    return lax.broadcasted_iota(jnp.int32, shape, len(shape) - 1)


def pack_kernel(low, core, high, fresh, meta, out):
    lane = lane_index((40, LANES))

    def window(ref, rows, start):
        tile, shift = divmod(start, LANES)
        first = ref[rows, tile * LANES : (tile + 1) * LANES]
        if shift == 0:
            return first
        second = ref[rows, (tile + 1) * LANES : (tile + 2) * LANES]
        first = pltpu.roll(first, LANES - shift, 1)
        second = pltpu.roll(second, LANES - shift, 1)
        return jnp.where(lane < LANES - shift, first, second)

    whole = slice(0, 40)
    for i in range(16):
        start = FIRST + i * 40
        out[i, 0:40, :] = window(low, whole, start)
        out[i, 40:80, :] = window(core, whole, start)
        out[i, 80:120, :] = window(high, whole, start)
        out[i, 120:160, :] = window(fresh, slice(0, 40), start)
        out[i, 160:200, :] = window(fresh, slice(40, 80), start)
        out[i, 200:208, :] = meta[...]


def sincos(x):
    n = jnp.floor(x * (2.0 / math.pi) + 0.5)
    r = x - n * 1.5703125
    r = r - n * 4.8351287841796875e-4
    r = r - n * 3.13855707645416259765625e-7
    r = r - n * 6.0771005065061922e-11
    q = n.astype(jnp.int32)
    z = r * r
    s = r + r * z * (-1.6666654611e-1 + z * (8.3321608736e-3 + z * -1.9515295891e-4))
    c = 1.0 - 0.5 * z + z * z * (4.166664568298827e-2 + z * (-1.388731625493765e-3 + z * 2.443315711809948e-5))
    swap = (q & 1) == 1
    sine = jnp.where(swap, c, s)
    cosine = jnp.where(swap, s, c)
    sine = jnp.where((q & 2) == 2, -sine, sine)
    cosine = jnp.where(((q + 1) & 2) == 2, -cosine, cosine)
    return sine, cosine


def main_kernel(meta, recv, sub_tab, lane_tab, order_tab, mask, recon, out, flat_out, state, phase, groups):
    lane = lane_index((40, LANES))

    def begin(l, carry):
        state[l, 0:WINDOW, :] = recv[l, 0:WINDOW, :]
        return carry

    lax.fori_loop(0, 16, begin, 0)

    def step(t, carry):
        def layer(l, acc):
            dst = pl.multiple_of(meta[l, 6, t], NEW_COLS)
            src = pl.multiple_of(WINDOW + t * NEW_COLS, NEW_COLS)
            state[l, pl.ds(dst, NEW_COLS), :] = recv[l, pl.ds(src, NEW_COLS), :]
            return tuple(
                acc[g] + pltpu.roll(state[l, pl.ds(meta[l, g, t], 40), :], meta[l, g, ROLL_AT + t], 1)
                for g in range(STARS)
            )

        zero = jnp.zeros((40, LANES), jnp.float32)
        acc = lax.fori_loop(0, 16, layer, (zero,) * STARS)
        for k in range(2):
            one, two, three = acc[3 * k : 3 * k + 3]
            joined = jnp.where(lane < 40, one, jnp.where(lane < 80, pltpu.roll(two, 40, 1), pltpu.roll(three, 80, 1)))
            for b in range(5):
                row = pl.multiple_of(((k * 5 + b) * STEPS + t) * PIX, PIX)
                phase[pl.ds(row, PIX), :] = joined[b * PIX : (b + 1) * PIX, :]
        return carry

    lax.fori_loop(0, STEPS, step, 0)

    groups[...] = jnp.zeros_like(groups)
    size = STEPS * PIX

    def spots(kb, carry):
        sine, cosine = sincos(phase[pl.ds(pl.multiple_of(kb * size, PIX), size), :])
        both = jnp.concatenate([cosine, sine], axis=0)
        along = jnp.dot(both, lane_tab[:, : 2 * LANES], precision=HIGHEST, preferred_element_type=jnp.float32)
        s3 = sine.reshape(STEPS, PIX, LANES)
        c3 = cosine.reshape(STEPS, PIX, LANES)
        acc = jnp.zeros_like(c3)
        for d in range(1, PIX):
            acc = acc + sub_tab[(d - 1) * PIX : d * PIX, :][None] * pltpu.roll(c3, d, 1)
        sign = sub_tab[7 * PIX : 8 * PIX, :][None]
        alt_c = jnp.sum(sign * c3, axis=1)
        alt_s = jnp.sum(sign * s3, axis=1)
        num_x = 4.0 * jnp.sum(s3 * acc, axis=1) - 8.0 * (alt_c * alt_c + alt_s * alt_s)
        num_y = 4.0 * jnp.sum(s3 * along[:size, :LANES].reshape(STEPS, PIX, LANES), axis=1)
        alt = along[:, LANES:]
        alt = alt * alt
        alt = jnp.sum((alt[:size] + alt[size:]).reshape(STEPS, PIX, LANES), axis=1)
        grouper = lane_tab[:, 2 * LANES :]
        got_x = jnp.dot(num_x, grouper, precision=HIGHEST, preferred_element_type=jnp.float32)
        got_y = jnp.dot(num_y, grouper, precision=HIGHEST, preferred_element_type=jnp.float32) - alt * (8.0 / 1024)
        for s, got in ((0, got_x), (1, got_y)):
            unit = s * 10 + kb
            tile = unit // 8
            groups[tile, 0:STEPS, :] = groups[tile, 0:STEPS, :] + pltpu.roll(got, (unit % 8) * 16, 1)
        return carry

    lax.fori_loop(0, 10, spots, 0)

    flat = sum(
        jnp.dot(groups[i], order_tab[i * LANES : (i + 1) * LANES, :], precision=HIGHEST, preferred_element_type=jnp.float32)
        for i in range(3)
    )
    flat = flat * mask[...]
    flat_out[...] = flat
    rounded = flat[:, :FLAT].astype(jnp.bfloat16)
    out[...] = jnp.zeros_like(out)
    for i in range(ACTS // LANES):
        part = jnp.dot(rounded, recon[:, i * LANES : (i + 1) * LANES], preferred_element_type=jnp.float32)
        owner, place = divmod(i, SLAB_TILES)
        out[owner, place * STEPS : (place + 1) * STEPS, :] = part[:STEPS]


def vmem():
    return pl.BlockSpec(memory_space=pltpu.VMEM)


def smem():
    return pl.BlockSpec(memory_space=pltpu.SMEM)


def pack(low, core, high, fresh, meta):
    return pl.pallas_call(
        pack_kernel,
        out_shape=jax.ShapeDtypeStruct((16, PAYLOAD, LANES), jnp.float32),
        in_specs=[vmem()] * 5,
        out_specs=vmem(),
        compiler_params=pltpu.CompilerParams(vmem_limit_bytes=32 << 20),
    )(low, core, high, fresh, meta)


def slopes_and_products(meta, recv, mask, recon):
    return pl.pallas_call(
        main_kernel,
        out_shape=(
            jax.ShapeDtypeStruct((16, SLAB_ROWS, LANES), jnp.float32),
            jax.ShapeDtypeStruct((16, FLAT_PAD), jnp.float32),
        ),
        in_specs=[smem()] + [vmem()] * 6,
        out_specs=(vmem(), vmem()),
        scratch_shapes=[
            pltpu.VMEM((16, LANES, LANES), jnp.float32),
            pltpu.VMEM((100 * PIX, LANES), jnp.float32),
            pltpu.VMEM((3, 16, LANES), jnp.float32),
        ],
        compiler_params=pltpu.CompilerParams(vmem_limit_bytes=40 << 20),
    )(meta, recv, jnp.asarray(sublane_table()), jnp.asarray(lane_table()), jnp.asarray(order_table()), mask, recon)


def everywhere(slab, axis):
    return lax.all_to_all(jnp.broadcast_to(slab[None], (16,) + slab.shape), axis, 0, 0, tiled=True)


def local(screens, new_columns, col_block, shift_x, shift_y, valid, recon):
    owner = lax.axis_index("sub")
    count = lax.axis_size("sub")
    strips = jnp.transpose(screens[0], (0, 2, 1))
    fresh = jnp.transpose(new_columns[:, 0], (0, 2, 1))[:, :, LANE0 : LANE0 + KEPT].reshape(UPDATES, KEPT)

    def strip(turn):
        return lax.dynamic_slice(strips, (turn, 0, LANE0), (1, 40, KEPT))[0]

    core = strip(PUP_TURN)
    forward = [(i, (i + 1) % count) for i in range(count)]
    backward = [(target, source) for source, target in forward]
    low = lax.ppermute(strip(jnp.where(owner == count - 1, PUP_TURN - 1, PUP_TURN)), "sub", forward)
    high = lax.ppermute(strip(jnp.where(owner == 0, PUP_TURN + 1, PUP_TURN)), "sub", backward)

    start = jnp.transpose(shift_x[:, 0]) + HALO
    turn = (LANES - HALO - jnp.transpose(shift_y[:, 0])) % LANES
    block = jnp.transpose(col_block) - (PUP_TURN * PUP // NEW_COLS) - (owner * 5 - 5)
    block = jnp.where((block >= 0) & (block < WINDOW // NEW_COLS), block, WINDOW // NEW_COLS) * NEW_COLS
    meta = (
        jnp.pad(start, ((0, 2), (0, LANES - STEPS)))
        + jnp.pad(turn, ((0, 2), (ROLL_AT, LANES - ROLL_AT - STEPS)))
        + jnp.pad(block, ((6, 1), (0, LANES - STEPS)))
    ).astype(jnp.float32)

    payload = pack(low, core, high, fresh, meta)
    recv = lax.all_to_all(payload, "layer", 0, 0, tiled=True)
    numbers = recv[:, META:, :].astype(jnp.int32)

    matrix = jnp.transpose(recon, (0, 2, 3, 1, 4)).reshape(FLAT, ACTS)
    mask = jnp.broadcast_to(valid.astype(jnp.float32)[None, :, :, None], (STARS, 5, 5, 2)).reshape(1, FLAT)
    mask = jnp.pad(mask, ((0, 0), (0, FLAT_PAD - FLAT)))
    products, flat = slopes_and_products(numbers, recv, mask, matrix)

    part = jnp.sum(lax.all_to_all(products, "sub", 0, 0, tiled=True), axis=0)
    total = jnp.sum(everywhere(part, "layer"), axis=0)
    slabs = everywhere(total, "sub")[: ACTS // LANES // SLAB_TILES, : SLAB_TILES * STEPS]
    commands = jnp.transpose(slabs.reshape(ACTS // LANES, STEPS, LANES), (1, 0, 2)).reshape(STEPS, ACTS)
    slopes = jnp.transpose(flat[:STEPS, :FLAT].reshape(STEPS, STARS, 5, 5, 2), (0, 1, 4, 2, 3))
    return (slopes, commands)


def solution(mesh):
    return jax.shard_map(
        local,
        mesh=mesh,
        in_specs=(
            P("layer", None, None, "sub"),
            P(None, "layer", None, None),
            P(None, "layer"),
            P(None, "layer", None),
            P(None, "layer", None),
            P("layer", "sub"),
            P(None, None, "layer", "sub", None),
        ),
        out_specs=(P(None, None, None, "layer", "sub"), P()),
        check_vma=False,
    )
```

time: 1940 us -> 149 us (0.08)
  blocking collectives: 797 us -> 35.7 us
  local copies, waits for them, and re-layouts: 469 us -> 13.1 us
  waiting for transfers between devices: 310 us -> 43.4 us
  other arithmetic: 196 us -> 3.01 us
  starting transfers between devices: 86.3 us -> 23.2 us
  matrix products: 44.6 us -> 0 us
  Pallas kernels: 0 us -> 29.1 us
  loops' own time: 23.6 us -> 0 us
    psum x10 -> x0, blocking collectives: 797 us -> none  [advance(): command = lax.psum(partial_cmd, ('layer', 'sub'))]
    gather x200 -> x0, local copies, waits for them, and re-layouts: 160 us -> none
    ppermute x20 -> x2, waiting for transfers between devices: 151 us -> 3.63 us  [the longest x1 3.63 us: local(): lax.ppermute(strip(jnp.where(owner == count - 1, PUP_TURN - 1, PUP_TURN))...]
    all_to_all x10 -> x2, waiting for transfers between devices: 159 us -> 39.7 us  [the longest x1 30.9 us: local(): recv = lax.all_to_all(payload, 'layer', 0, 0, tiled=True)]
    while x63 -> x0, local copies, waits for them, and re-layouts: 104 us -> none
    select_n x10 -> x0, local copies, waits for them, and re-layouts: 72.2 us -> none  [place_columns(): return jnp.where(inside, placed, strips)]
    while x20 -> x0, other arithmetic: 71.1 us -> none
    all_to_all x10 -> x2, starting transfers between devices: 64.6 us -> 15.5 us  [the longest x1 10.3 us: local(): recv = lax.all_to_all(payload, 'layer', 0, 0, tiled=True)]
  transfers between devices with their start and end apart: 30 -> 4, of which waited for: 30 -> 3; matrix products, arithmetic and copies ran while one was open for 1% -> 8% of each run, Pallas kernels for 0% -> 0%
where the time goes in v1:
time: 149 us; the launch traced here: 148 us
  waiting for transfers between devices  43.4 us (29%)
  blocking collectives  35.7 us (24%)
  Pallas kernels  29.1 us (20%)
  starting transfers between devices  23.2 us (16%)
  local copies, waits for them, and re-layouts  13.1 us (9%)
  other arithmetic  3.01 us (2%)
    all_to_all x1, waiting for transfers between devices, local(): recv = lax.all_to_all(payload, 'layer', 0, 0, tiled=True)  30.9 us
    pallas_call x1, Pallas kernels, slopes_and_products(): pl.pallas_call(main_kernel, out_shape=(jax.ShapeDtypeStruct((16, SLAB_ROW...  27 us
    all_to_all x1, blocking collectives, everywhere(): lax.all_to_all(jnp.broadcast_to(slab[None], (16,) + slab.shape), axis, 0,...  18.4 us
    all_to_all x1, blocking collectives, local(): part = jnp.sum(lax.all_to_all(products, 'sub', 0, 0, tiled=True), axis=0)  17.3 us
    all_to_all x1, starting transfers between devices, local(): recv = lax.all_to_all(payload, 'layer', 0, 0, tiled=True)  10.3 us
    all_to_all x1, waiting for transfers between devices, everywhere(): lax.all_to_all(jnp.broadcast_to(slab[None], (16,) + slab.shape), axis, 0,...  8.78 us
    ppermute x1, starting transfers between devices, local(): lax.ppermute(strip(jnp.where(owner == 0, PUP_TURN + 1, PUP_TURN)), 'sub',...  7.7 us
    reshape x1, local copies, waits for them, and re-layouts, local(): matrix = jnp.transpose(recon, (0, 2, 3, 1, 4)).reshape(FLAT, ACTS)  6.37 us
  transfers between devices with their start and end apart: 4, of which 3 were waited for; matrix products, arithmetic and copies ran while one was open for 8% of the time, Pallas kernels for 0%

profile of v1, /device:TPU:1, one launch (start us, length us, event | category | flops | bytes accessed | tf_op | source)
XLA Modules:
  0.0 148.3 jit_solution(18080726827031166428)
XLA Ops:
  0.6 1.0 dynamic-slice_bitcast_fusion
  1.6 7.7 %collective-permute-start.1 = (f32[40,768]{1,0:T(8,128)S(1)}, f32[40,768]{1,0:T(8,128)S(1)}, u32[]{:S(2)}, u32[]{:S(2)}) collective-permute-start(f32[40,768]{1,0:T(8,128)S(1)} %get-tuple-element.6), channel_id=1, source_target_pairs={{1,0},{2,1},{3,2},{4,3},{5,4},{6,5},{7,6},{8,7},{9,8},{10,9},{11,1... | collective-permute-start | bytes 368648 | tf_op jit(solution)/shard_map/ppermute | solution.py:248
  9.3 0.0 collective-permute-start
  9.3 0.7 fusion.1
  10.0 0.7 add_select_fusion
  10.7 0.9 slice_bitcast_fusion.1.core
  11.6 1.0 slice_bitcast_fusion.fresh
  12.6 0.7 fusion.2
  13.3 0.1 add_convert_fusion.meta
  13.3 0.0 copy-start.3
  13.3 0.0 collective-permute-done.1.high
  13.3 3.6 %collective-permute-done.low = f32[40,768]{1,0:T(8,128)S(1)} collective-permute-done((f32[40,768]{1,0:T(8,128)S(1)}, f32[40,768]{1,0:T(8,128)S(1)}, u32[]{:S(2)}, u32[]{:S(2)}) %collective-permute-start) | collective-permute-done | bytes 122912 | tf_op jit(solution)/shard_map/ppermute | solution.py:247
  17.0 2.0 %shard_map.113 = f32[16,208,128]{2,1,0:T(8,128)} custom-call(f32[40,768]{1,0:T(8,128)S(1)} %collective-permute-done.low, f32[40,768]{1,0:T(8,128)S(1)} %slice_bitcast_fusion.1.core, f32[40,768]{1,0:T(8,128)S(1)} %collective-permute-done.1.high, f32[80,768]{1,0:T(8,128)S(1)} %slice_bitcast_fusion.fresh, f32[8,128]{1,0:T(8,128)S(1)} %add_convert_fusion.meta), custom_call_target="tpu_custom_call" | custom-call | tf_op jit(solution)/shard_map/pallas_call | solution.py:204
  19.0 10.3 %all-to-all-start = ((f32[16,208,128]{2,1,0:T(8,128)}), f32[16,208,128]{2,1,0:T(8,128)}, u32[]{:S(2)}, u32[]{:S(2)}) async-start(f32[16,208,128]{2,1,0:T(8,128)} %shard_map.113), calls=%async_computation | async-start | bytes 3407872 | tf_op jit(solution)/shard_map/all_to_all | solution.py:261
  29.4 0.0 copy-done.3
  29.4 0.1 broadcast_in_dim.8
  29.4 0.1 reshape.78
  29.6 0.0 copy-start.1
  29.6 0.0 copy-start.2
  29.6 6.4 %reshape.79.recon = bf16[300,5376]{1,0:T(8,128)(2,1)S(1)} reshape(bf16[6,5,5,2,5376]{4,3,2,1,0:T(2,128)(2,1)} %bitcast.44) | data formatting | bytes 6451200 | tf_op jit(solution)/shard_map/reshape | solution.py:264
  36.0 30.9 %all-to-all-done.recv = f32[16,208,128]{2,1,0:T(8,128)} async-done(((f32[16,208,128]{2,1,0:T(8,128)}), f32[16,208,128]{2,1,0:T(8,128)}, u32[]{:S(2)}, u32[]{:S(2)}) %all-to-all-start) | async-done | bytes 1703968 | tf_op jit(solution)/shard_map/all_to_all | solution.py:261
  67.0 0.8 slice_convert_fusion.meta
  67.8 0.0 copy-done.1
  67.8 0.0 copy-done.2
  67.8 0.0 copy-start
  67.8 1.1 copy-done
  68.9 27.0 %shard_map.114 = (f32[16,32,128]{2,1,0:T(8,128)S(1)}, f32[16,384]{1,0:T(8,128)S(1)}) custom-call(s32[16,8,128]{2,1,0:T(8,128)S(1)} %slice_convert_fusion.meta, f32[16,208,128]{2,1,0:T(8,128)} %all-to-all-done.recv, f32[64,128]{1,0:T(8,128)S(1)} %copy-done.2, f32[128,384]{1,0:T(8,128)S(1)} %copy-done.1, f32[384,384]{1,0:T(8,128)S(1)} %copy-done, ...), custom_call_target="tpu_custom_call" | custom-call | tf_op jit(solution)/shard_map/pallas_call | solution.py:214
  95.9 17.3 %all_to_all.20 = f32[16,32,128]{2,1,0:T(8,128)S(1)} all-to-all(f32[16,32,128]{2,1,0:T(8,128)S(1)} %get-tuple-element.5), channel_id=1, replica_groups=mesh['layer'=16,'sub'=16] {'sub'}, dimensions={0} | all-to-all | bytes 524288 | tf_op jit(solution)/shard_map/all_to_all | solution.py:269
  113.3 18.4 %all_to_all.21 = f32[16,32,128]{2,1,0:T(8,128)S(1)} all-to-all(f32[16,32,128]{2,1,0:T(8,128)S(1)} %broadcast_in_dim.9), channel_id=1, replica_groups=mesh['layer'=16,'sub'=16] {'layer'}, dimensions={0} | all-to-all | bytes 524288 | tf_op jit(solution)/shard_map/all_to_all | solution.py:232
  131.7 0.7 broadcast_in_dim.10
  132.5 5.2 %all-to-all-start.3 = ((f32[16,32,128]{2,1,0:T(8,128)}), f32[16,32,128]{2,1,0:T(8,128)S(1)}, u32[]{:S(2)}, u32[]{:S(2)}) async-start(f32[16,32,128]{2,1,0:T(8,128)} %broadcast_in_dim.10), calls=%async_computation.3 | async-start | bytes 524288 | tf_op jit(solution)/shard_map/all_to_all | solution.py:232
  137.7 0.1 copy.24
  137.8 0.8 reshape.80
  138.5 8.8 %all-to-all-done.3 = f32[16,32,128]{2,1,0:T(8,128)S(1)} async-done(((f32[16,32,128]{2,1,0:T(8,128)}), f32[16,32,128]{2,1,0:T(8,128)S(1)}, u32[]{:S(2)}, u32[]{:S(2)}) %all-to-all-start.3) | async-done | bytes 262176 | tf_op jit(solution)/shard_map/all_to_all | solution.py:232
  147.4 0.1 copy.25
  147.5 0.8 copy.26
  (8 shorter events, 0.1 us)
Async XLA Ops:
  1.6 11.7 %collective-permute-start.1 = (f32[40,768]{1,0:T(8,128)S(1)}, f32[40,768]{1,0:T(8,128)S(1)}, u32[]{:S(2)}, u32[]{:S(2)}) collective-permute-start(f32[40,768]{1,0:T(8,128)S(1)} %get-tuple-element.6), channel_id=1, source_target_pairs={{1,0},{2,1},{3,2},{4,3},{5,4},{6,5},{7,6},{8,7},{9,8},{10,9},{11,1... | collective-permute-start | bytes 368648 | tf_op jit(solution)/shard_map/ppermute | solution.py:248
  9.3 7.6 %collective-permute-start = (f32[40,768]{1,0:T(8,128)S(1)}, f32[40,768]{1,0:T(8,128)S(1)}, u32[]{:S(2)}, u32[]{:S(2)}) collective-permute-start(f32[40,768]{1,0:T(8,128)S(1)} %get-tuple-element.7), channel_id=1, source_target_pairs={{0,1},{1,2},{2,3},{3,4},{4,5},{5,6},{6,7},{7,8},{8,9},{9,10},{10,1... | collective-permute-start | bytes 368648 | tf_op jit(solution)/shard_map/ppermute | solution.py:247
  13.3 16.0 %copy-start.3 = (s32[5,5]{1,0:T(8,128)S(1)}, s32[5,5]{1,0:T(8,128)}, u32[]{:S(2)}) copy-start(s32[5,5]{1,0:T(8,128)} %param.15) | copy-start | bytes 304
  19.0 47.9 %all-to-all-start = ((f32[16,208,128]{2,1,0:T(8,128)}), f32[16,208,128]{2,1,0:T(8,128)}, u32[]{:S(2)}, u32[]{:S(2)}) async-start(f32[16,208,128]{2,1,0:T(8,128)} %shard_map.113), calls=%async_computation | async-start | bytes 3407872 | tf_op jit(solution)/shard_map/all_to_all | solution.py:261
  29.6 38.2 %copy-start.1 = (f32[128,384]{1,0:T(8,128)S(1)}, f32[128,384]{1,0:T(8,128)}, u32[]{:S(2)}) copy-start(f32[128,384]{1,0:T(8,128)} %constant.60.clone.lane_tab) | copy-start | bytes 589828
  29.6 38.2 %copy-start.2 = (f32[64,128]{1,0:T(8,128)S(1)}, f32[64,128]{1,0:T(8,128)}, u32[]{:S(2)}) copy-start(f32[64,128]{1,0:T(8,128)} %constant.59.clone.sub_tab) | copy-start | bytes 98308
  67.8 1.1 copy-start
  132.5 14.8 %all-to-all-start.3 = ((f32[16,32,128]{2,1,0:T(8,128)}), f32[16,32,128]{2,1,0:T(8,128)S(1)}, u32[]{:S(2)}, u32[]{:S(2)}) async-start(f32[16,32,128]{2,1,0:T(8,128)} %broadcast_in_dim.10), calls=%async_computation.3 | async-start | bytes 524288 | tf_op jit(solution)/shard_map/all_to_all | solution.py:232

commit v2 on v1

--- a/solution.py
+++ b/solution.py
@@ -22,11 +22,18 @@
 FIRST = ROW0 - HALO - LANE0
 WINDOW = 120
 UPDATES = STEPS * NEW_COLS
-META = WINDOW + UPDATES
+COLS = WINDOW + UPDATES
+REST = 56
+META = COLS + REST
 PAYLOAD = META + 8
+CHIPS = 8
+CHIP_ROWS = 80
+REST_LANES = 32
 ROLL_AT = 64
-SLAB_TILES = 3
-SLAB_ROWS = 32
+HALF_TILES = 21
+SLABS = 16
+SLAB_USED = 14
+SLAB_ROWS = 16
 FLAT = 300
 FLAT_PAD = 384
 HIGHEST = lax.Precision.HIGHEST
@@ -75,27 +82,40 @@
 
 
 def pack_kernel(low, core, high, fresh, meta, out):
-    lane = lane_index((40, LANES))
-
-    def window(ref, rows, start):
+    def window(ref, first, count, start):
         tile, shift = divmod(start, LANES)
-        first = ref[rows, tile * LANES : (tile + 1) * LANES]
+        rows = slice(first, first + count)
+        left = ref[rows, tile * LANES : (tile + 1) * LANES]
         if shift == 0:
-            return first
-        second = ref[rows, (tile + 1) * LANES : (tile + 2) * LANES]
-        first = pltpu.roll(first, LANES - shift, 1)
-        second = pltpu.roll(second, LANES - shift, 1)
-        return jnp.where(lane < LANES - shift, first, second)
-
-    whole = slice(0, 40)
-    for i in range(16):
-        start = FIRST + i * 40
-        out[i, 0:40, :] = window(low, whole, start)
-        out[i, 40:80, :] = window(core, whole, start)
-        out[i, 80:120, :] = window(high, whole, start)
-        out[i, 120:160, :] = window(fresh, slice(0, 40), start)
-        out[i, 160:200, :] = window(fresh, slice(40, 80), start)
-        out[i, 200:208, :] = meta[...]
+            return left
+        left = pltpu.roll(left, LANES - shift, 1)
+        if (tile + 2) * LANES > KEPT:
+            return left
+        right = pltpu.roll(ref[rows, (tile + 1) * LANES : (tile + 2) * LANES], LANES - shift, 1)
+        return jnp.where(lane_index(left.shape) < LANES - shift, left, right)
+
+    parts = ((low, 0), (core, 40), (high, 80), (fresh, 120))
+
+    def columns(first, start):
+        ref, base = [part for part in parts if part[1] <= first][-1]
+        return window(ref, first - base, PIX, start)
+
+    lane = lane_index((PIX, LANES))
+    for m in range(CHIPS):
+        start = FIRST + m * CHIP_ROWS
+        for ref, base in parts:
+            count = UPDATES if base == WINDOW else 40
+            out[m, base : base + count, :] = window(ref, 0, count, start)
+        for r in range(REST // PIX):
+            joined = None
+            for q in range(4):
+                first = q * REST + r * PIX
+                if first >= COLS:
+                    continue
+                piece = columns(first, start + LANES - q * REST_LANES)
+                joined = piece if joined is None else jnp.where(lane < q * REST_LANES, joined, piece)
+            out[m, COLS + r * PIX : COLS + (r + 1) * PIX, :] = joined
+        out[m, META:PAYLOAD, :] = meta[...]
 
 
 def sincos(x):
@@ -116,27 +136,47 @@
     return sine, cosine
 
 
-def main_kernel(meta, recv, sub_tab, lane_tab, order_tab, mask, recon, out, flat_out, state, phase, groups):
+def main_kernel(
+    core, mine, other, sub_tab, lane_tab, order_tab, mask, recon,
+    keep, send, flat_out,
+    state, phase, groups, numbers, meta, arrived,
+):
     lane = lane_index((40, LANES))
-
-    def begin(l, carry):
-        state[l, 0:WINDOW, :] = recv[l, 0:WINDOW, :]
+    side = core[0]
+    for p in range(CHIPS):
+        numbers[p] = mine[p, META:, :].astype(jnp.int32)
+        numbers[CHIPS + p] = other[p, META:, :].astype(jnp.int32)
+    copy = pltpu.make_async_copy(numbers, meta, arrived)
+    copy.start()
+
+    cut = LANES - 40 * side
+    turn = lax.rem(cut, LANES)
+
+    def begin(p, carry):
+        for base, ref in ((0, mine), (CHIPS, other)):
+            for q in range(4):
+                first = q * REST
+                count = min(REST, COLS - first)
+                left = pltpu.roll(ref[p, first : first + count, :], turn, 1)
+                right = pltpu.roll(ref[p, COLS : COLS + count, :], (88 - REST_LANES * q) % LANES, 1)
+                state[base + p, first : first + count, :] = jnp.where(lane_index(left.shape) < cut, left, right)
         return carry
 
-    lax.fori_loop(0, 16, begin, 0)
+    lax.fori_loop(0, CHIPS, begin, 0)
+    copy.wait()
 
     def step(t, carry):
         def layer(l, acc):
             dst = pl.multiple_of(meta[l, 6, t], NEW_COLS)
             src = pl.multiple_of(WINDOW + t * NEW_COLS, NEW_COLS)
-            state[l, pl.ds(dst, NEW_COLS), :] = recv[l, pl.ds(src, NEW_COLS), :]
+            state[l, pl.ds(dst, NEW_COLS), :] = state[l, pl.ds(src, NEW_COLS), :]
             return tuple(
                 acc[g] + pltpu.roll(state[l, pl.ds(meta[l, g, t], 40), :], meta[l, g, ROLL_AT + t], 1)
                 for g in range(STARS)
             )
 
         zero = jnp.zeros((40, LANES), jnp.float32)
-        acc = lax.fori_loop(0, 16, layer, (zero,) * STARS)
+        acc = lax.fori_loop(0, 2 * CHIPS, layer, (zero,) * STARS, unroll=8)
         for k in range(2):
             one, two, three = acc[3 * k : 3 * k + 3]
             joined = jnp.where(lane < 40, one, jnp.where(lane < 80, pltpu.roll(two, 40, 1), pltpu.roll(three, 80, 1)))
@@ -185,11 +225,32 @@
     flat = flat * mask[...]
     flat_out[...] = flat
     rounded = flat[:, :FLAT].astype(jnp.bfloat16)
-    out[...] = jnp.zeros_like(out)
-    for i in range(ACTS // LANES):
-        part = jnp.dot(rounded, recon[:, i * LANES : (i + 1) * LANES], preferred_element_type=jnp.float32)
-        owner, place = divmod(i, SLAB_TILES)
-        out[owner, place * STEPS : (place + 1) * STEPS, :] = part[:STEPS]
+    for out, half in ((keep, side), (send, 1 - side)):
+        out[...] = jnp.zeros_like(out)
+        for i in range(HALF_TILES):
+            column = pl.multiple_of((half * HALF_TILES + i) * LANES, LANES)
+            part = jnp.dot(rounded, recon[:, pl.ds(column, LANES)], preferred_element_type=jnp.float32)
+            for slab, row, first, count in pieces(i):
+                out[slab, row : row + count, :] = part[first : first + count]
+
+
+def pieces(i):
+    found = []
+    first = 0
+    while first < STEPS:
+        slab, row = divmod(i * STEPS + first, SLAB_USED)
+        count = min(STEPS - first, SLAB_USED - row)
+        found.append((slab, row, first, count))
+        first += count
+    return found
+
+
+def finish_kernel(core, mine, other, out):
+    for ref, half in ((mine, core[0]), (other, 1 - core[0])):
+        for i in range(HALF_TILES):
+            column = pl.multiple_of((half * HALF_TILES + i) * LANES, LANES)
+            for slab, row, first, count in pieces(i):
+                out[first : first + count, pl.ds(column, LANES)] = ref[slab, row : row + count, :]
 
 
 def vmem():
@@ -203,33 +264,59 @@
 def pack(low, core, high, fresh, meta):
     return pl.pallas_call(
         pack_kernel,
-        out_shape=jax.ShapeDtypeStruct((16, PAYLOAD, LANES), jnp.float32),
+        out_shape=jax.ShapeDtypeStruct((CHIPS, PAYLOAD, LANES), jnp.float32),
         in_specs=[vmem()] * 5,
         out_specs=vmem(),
         compiler_params=pltpu.CompilerParams(vmem_limit_bytes=32 << 20),
     )(low, core, high, fresh, meta)
 
 
-def slopes_and_products(meta, recv, mask, recon):
+def slopes_and_products(core, mine, other, mask, recon):
+    slab = jax.ShapeDtypeStruct((SLABS, SLAB_ROWS, LANES), jnp.float32)
     return pl.pallas_call(
         main_kernel,
-        out_shape=(
-            jax.ShapeDtypeStruct((16, SLAB_ROWS, LANES), jnp.float32),
-            jax.ShapeDtypeStruct((16, FLAT_PAD), jnp.float32),
-        ),
-        in_specs=[smem()] + [vmem()] * 6,
-        out_specs=(vmem(), vmem()),
+        out_shape=(slab, slab, jax.ShapeDtypeStruct((16, FLAT_PAD), jnp.float32)),
+        in_specs=[smem()] + [vmem()] * 7,
+        out_specs=(vmem(),) * 3,
         scratch_shapes=[
-            pltpu.VMEM((16, LANES, LANES), jnp.float32),
+            pltpu.VMEM((2 * CHIPS, COLS + NEW_COLS, LANES), jnp.float32),
             pltpu.VMEM((100 * PIX, LANES), jnp.float32),
             pltpu.VMEM((3, 16, LANES), jnp.float32),
+            pltpu.VMEM((2 * CHIPS, 8, LANES), jnp.int32),
+            pltpu.SMEM((2 * CHIPS, 8, LANES), jnp.int32),
+            pltpu.SemaphoreType.DMA(()),
         ],
         compiler_params=pltpu.CompilerParams(vmem_limit_bytes=40 << 20),
-    )(meta, recv, jnp.asarray(sublane_table()), jnp.asarray(lane_table()), jnp.asarray(order_table()), mask, recon)
-
-
-def everywhere(slab, axis):
-    return lax.all_to_all(jnp.broadcast_to(slab[None], (16,) + slab.shape), axis, 0, 0, tiled=True)
+    )(core, mine, other, jnp.asarray(sublane_table()), jnp.asarray(lane_table()), jnp.asarray(order_table()), mask, recon)
+
+
+def finish(core, mine, other):
+    return pl.pallas_call(
+        finish_kernel,
+        out_shape=jax.ShapeDtypeStruct((STEPS, ACTS), jnp.float32),
+        in_specs=[smem(), vmem(), vmem()],
+        out_specs=vmem(),
+    )(core, mine, other)
+
+
+def groups_by(key):
+    found = {}
+    for device in range(256):
+        layer, sub = divmod(device, 16)
+        found.setdefault(key(layer // 8, layer // 2 % 4, layer % 2, sub // 4, sub % 4), []).append(device)
+    return [found[name] for name in sorted(found)]
+
+
+def exchange(blocks, groups):
+    return lax.all_to_all(blocks, ("layer", "sub"), 0, 0, tiled=True, axis_index_groups=groups)
+
+
+def to_all(block, groups):
+    return exchange(jnp.broadcast_to(block[None], (len(groups[0]),) + block.shape), groups)
+
+
+def to_other_core(block):
+    return lax.ppermute(block, "layer", [(i, i ^ 1) for i in range(16)])
 
 
 def local(screens, new_columns, col_block, shift_x, shift_y, valid, recon):
@@ -250,26 +337,27 @@
     start = jnp.transpose(shift_x[:, 0]) + HALO
     turn = (LANES - HALO - jnp.transpose(shift_y[:, 0])) % LANES
     block = jnp.transpose(col_block) - (PUP_TURN * PUP // NEW_COLS) - (owner * 5 - 5)
-    block = jnp.where((block >= 0) & (block < WINDOW // NEW_COLS), block, WINDOW // NEW_COLS) * NEW_COLS
+    block = jnp.where((block >= 0) & (block < WINDOW // NEW_COLS), block, COLS // NEW_COLS) * NEW_COLS
     meta = (
         jnp.pad(start, ((0, 2), (0, LANES - STEPS)))
         + jnp.pad(turn, ((0, 2), (ROLL_AT, LANES - ROLL_AT - STEPS)))
         + jnp.pad(block, ((6, 1), (0, LANES - STEPS)))
     ).astype(jnp.float32)
 
-    payload = pack(low, core, high, fresh, meta)
-    recv = lax.all_to_all(payload, "layer", 0, 0, tiled=True)
-    numbers = recv[:, META:, :].astype(jnp.int32)
+    side = (lax.axis_index("layer") % 2).astype(jnp.int32).reshape(1)
+    mine = exchange(pack(low, core, high, fresh, meta), groups_by(lambda zh, x, c, y, zl: (c, y, zl)))
+    other = to_other_core(mine)
 
     matrix = jnp.transpose(recon, (0, 2, 3, 1, 4)).reshape(FLAT, ACTS)
     mask = jnp.broadcast_to(valid.astype(jnp.float32)[None, :, :, None], (STARS, 5, 5, 2)).reshape(1, FLAT)
     mask = jnp.pad(mask, ((0, 0), (0, FLAT_PAD - FLAT)))
-    products, flat = slopes_and_products(numbers, recv, mask, matrix)
-
-    part = jnp.sum(lax.all_to_all(products, "sub", 0, 0, tiled=True), axis=0)
-    total = jnp.sum(everywhere(part, "layer"), axis=0)
-    slabs = everywhere(total, "sub")[: ACTS // LANES // SLAB_TILES, : SLAB_TILES * STEPS]
-    commands = jnp.transpose(slabs.reshape(ACTS // LANES, STEPS, LANES), (1, 0, 2)).reshape(STEPS, ACTS)
+    keep, send, flat = slopes_and_products(side, mine, other, mask, matrix)
+
+    plane = groups_by(lambda zh, x, c, y, zl: (c, zh, zl))
+    column = groups_by(lambda zh, x, c, y, zl: (c, x, y))
+    part = jnp.sum(exchange(keep + to_other_core(send), plane), axis=0)
+    total = to_all(jnp.sum(to_all(part, column), axis=0), plane)
+    commands = finish(side, total, to_other_core(total))
     slopes = jnp.transpose(flat[:STEPS, :FLAT].reshape(STEPS, STARS, 5, 5, 2), (0, 1, 4, 2, 3))
     return (slopes, commands)
 

time: 149 us -> 123 us (0.83)
  waiting for transfers between devices: 43.4 us -> 5.07 us
  blocking collectives: 35.7 us -> 67 us
  starting transfers between devices: 23.2 us -> 12.8 us
  Pallas kernels: 29.1 us -> 22.7 us
    all_to_all x2 -> x0, waiting for transfers between devices: 39.7 us -> none  [the longest x1 30.9 us: local(): recv = lax.all_to_all(payload, 'layer', 0, 0, tiled=True)]
    all_to_all x2 -> x4, blocking collectives: 35.7 us -> 67 us  [exchange(): lax.all_to_all(blocks, ('layer', 'sub'), 0, 0, tiled=True, axis_index_gro...]
    all_to_all x2 -> x0, starting transfers between devices: 15.5 us -> none  [the longest x1 10.3 us: local(): recv = lax.all_to_all(payload, 'layer', 0, 0, tiled=True)]
    pallas_call x2 -> x3, Pallas kernels: 29.1 us -> 22.7 us  [the longest x1 20.1 us: slopes_and_products(): pl.pallas_call(main_kernel, out_shape=(slab, slab, jax.ShapeDtypeStruct((...]
    ppermute x0 -> x3, starting transfers between devices: none -> 5.08 us  [to_other_core(): return lax.ppermute(block, 'layer', [(i, i ^ 1) for i in range(16)])]
  transfers between devices with their start and end apart: 4 -> 5, of which waited for: 3 -> 3; matrix products, arithmetic and copies ran while one was open for 8% -> 9% of each run, Pallas kernels for 0% -> 0%
where the time goes in v2:
time: 123 us
  blocking collectives  67 us (54%)
  Pallas kernels  22.7 us (18%)
  starting transfers between devices  12.8 us (10%)
  local copies, waits for them, and re-layouts  12.1 us (10%)
  waiting for transfers between devices  5.07 us (4%)
  other arithmetic  2.17 us (2%)
    all_to_all x4, blocking collectives, exchange(): lax.all_to_all(blocks, ('layer', 'sub'), 0, 0, tiled=True, axis_index_gro...  67 us
    pallas_call x1, Pallas kernels, slopes_and_products(): pl.pallas_call(main_kernel, out_shape=(slab, slab, jax.ShapeDtypeStruct((...  20.1 us
    ppermute x1, starting transfers between devices, local(): lax.ppermute(strip(jnp.where(owner == 0, PUP_TURN + 1, PUP_TURN)), 'sub',...  7.7 us
    reshape x1, local copies, waits for them, and re-layouts, local(): matrix = jnp.transpose(recon, (0, 2, 3, 1, 4)).reshape(FLAT, ACTS)  6.37 us
    ppermute x3, starting transfers between devices, to_other_core(): return lax.ppermute(block, 'layer', [(i, i ^ 1) for i in range(16)])  5.08 us
    ppermute x1, waiting for transfers between devices, local(): lax.ppermute(strip(jnp.where(owner == count - 1, PUP_TURN - 1, PUP_TURN))...  3.62 us
  transfers between devices with their start and end apart: 5, of which 3 were waited for; matrix products, arithmetic and copies ran while one was open for 9% of the time, Pallas kernels for 0%

profile of v2, /device:TPU:1, one launch (start us, length us, event | category | flops | bytes accessed | tf_op | source)
XLA Modules:
  0.0 122.6 jit_solution(14305951224556847749)
XLA Ops:
  0.6 1.0 dynamic-slice_bitcast_fusion
  1.6 7.7 %collective-permute-start.1 = (f32[40,768]{1,0:T(8,128)S(1)}, f32[40,768]{1,0:T(8,128)S(1)}, u32[]{:S(2)}, u32[]{:S(2)}) collective-permute-start(f32[40,768]{1,0:T(8,128)S(1)} %get-tuple-element.8), channel_id=1, source_target_pairs={{1,0},{2,1},{3,2},{4,3},{5,4},{6,5},{7,6},{8,7},{9,8},{10,9},{11,1... | collective-permute-start | bytes 368648 | tf_op jit(solution)/shard_map/ppermute | solution.py:335
  9.3 0.0 collective-permute-start
  9.3 0.7 fusion.1
  10.0 0.7 add_select_fusion
  10.7 0.0 copy-start.5
  10.7 0.9 slice_bitcast_fusion.1.core
  11.6 1.0 slice_bitcast_fusion.fresh
  12.6 0.7 fusion.2
  13.3 0.1 add_convert_fusion.meta
  13.3 0.0 collective-permute-done.1.high
  13.4 3.6 %collective-permute-done.low = f32[40,768]{1,0:T(8,128)S(1)} collective-permute-done((f32[40,768]{1,0:T(8,128)S(1)}, f32[40,768]{1,0:T(8,128)S(1)}, u32[]{:S(2)}, u32[]{:S(2)}) %collective-permute-start) | collective-permute-done | bytes 122912 | tf_op jit(solution)/shard_map/ppermute | solution.py:334
  17.0 0.9 shard_map.113
  17.9 32.6 %all_to_all.20.mine = f32[8,264,128]{2,1,0:T(8,128)} all-to-all(f32[8,264,128]{2,1,0:T(8,128)S(1)} %shard_map.113), channel_id=1, replica_groups={{0,32,64,96,128,160,192,224},{1,33,65,97,129,161,193,225},{2,34,66,98,1..., dimensions={0} | all-to-all | bytes 2162688 | tf_op jit(solution)/shard_map/all_to_all | solution.py:311
  50.5 0.8 collective-permute-start.2
  51.3 0.0 copy-done.5
  51.3 0.1 broadcast_in_dim.11
  51.4 0.1 reshape.76
  51.6 0.0 copy-start.1
  51.6 0.0 copy-start.2
  51.6 6.4 %reshape.77.recon = bf16[300,5376]{1,0:T(8,128)(2,1)S(1)} reshape(bf16[6,5,5,2,5376]{4,3,2,1,0:T(2,128)(2,1)} %bitcast.41) | data formatting | bytes 6451200 | tf_op jit(solution)/shard_map/reshape | solution.py:351
  58.0 0.0 collective-permute-done.2.other
  58.0 0.0 copy-done.1
  58.0 0.0 copy-done.2
  58.0 0.0 copy-start
  58.0 1.1 copy-done
  59.1 20.1 %shard_map.114 = (f32[16,16,128]{2,1,0:T(8,128)S(1)}, f32[16,16,128]{2,1,0:T(8,128)S(1)}, f32[16,384]{1,0:T(8,128)S(1)}) custom-call(s32[1]{0:T(128)} %bitcast.core, f32[8,264,128]{2,1,0:T(8,128)} %all_to_all.20.mine, f32[8,264,128]{2,1,0:T(8,128)} %collective-permute-done.2.other, f32[64,128]{1,0:T(8,128)S(1)} %copy-done.2, f32[128,384]{1,0:T(8,128)S(1)} %copy-done.1, ...), custom_call_target="tpu_custom_call" | custom-call | tf_op jit(solution)/shard_map/pallas_call | solution.py:276
  79.2 0.1 collective-permute-start.3
  79.3 1.3 %collective-permute-done.3 = f32[16,16,128]{2,1,0:T(8,128)S(1)} collective-permute-done((f32[16,16,128]{2,1,0:T(8,128)S(1)}, f32[16,16,128]{2,1,0:T(8,128)S(1)}, u32[]{:S(2)}, u32[]{:S(2)}) %collective-permute-start.3) | collective-permute-done | bytes 131104 | tf_op jit(solution)/shard_map/ppermute | solution.py:319
  80.6 13.4 %all_to_all.21 = f32[16,16,128]{2,1,0:T(8,128)S(1)} all-to-all(f32[16,16,128]{2,1,0:T(8,128)S(1)} %add.60), channel_id=1, replica_groups={{0,4,8,12,32,36,40,44,64,68,72,76,96,100,104,108},{1,5,9,13,33,37,41,45..., dimensions={0} | all-to-all | bytes 262144 | tf_op jit(solution)/shard_map/all_to_all | solution.py:311
  94.0 11.1 %all_to_all.22 = f32[8,16,128]{2,1,0:T(8,128)S(1)} all-to-all(f32[8,16,128]{2,1,0:T(8,128)S(1)} %broadcast_in_dim.12), channel_id=1, replica_groups={{0,1,2,3,128,129,130,131},{4,5,6,7,132,133,134,135},{8,9,10,11,136,137,..., dimensions={0} | all-to-all | bytes 131072 | tf_op jit(solution)/shard_map/all_to_all | solution.py:311
  105.1 9.9 %all_to_all.23.mine = f32[16,16,128]{2,1,0:T(8,128)S(1)} all-to-all(f32[16,16,128]{2,1,0:T(8,128)S(1)} %broadcast_in_dim.13), channel_id=1, replica_groups={{0,4,8,12,32,36,40,44,64,68,72,76,96,100,104,108},{1,5,9,13,33,37,41,45..., dimensions={0} | all-to-all | bytes 262144 | tf_op jit(solution)/shard_map/all_to_all | solution.py:311
  115.1 0.0 copy-start.3
  115.1 4.2 %collective-permute-start.4 = (f32[16,16,128]{2,1,0:T(8,128)S(1)}, f32[16,16,128]{2,1,0:T(8,128)S(1)}, u32[]{:S(2)}, u32[]{:S(2)}) collective-permute-start(f32[16,16,128]{2,1,0:T(8,128)S(1)} %all_to_all.23.mine), channel_id=1, source_target_pairs={{0,16},{16,0},{32,48},{48,32},{64,80},{80,64},{96,112},{112,96},{1... | collective-permute-start | bytes 393224 | tf_op jit(solution)/shard_map/ppermute | solution.py:319
  119.2 0.1 copy.20
  119.3 0.8 reshape.78
  120.1 0.1 collective-permute-done.4.other
  120.2 0.0 copy-done.3
  120.2 0.0 copy-start.4
  120.2 0.7 copy-done.4
  120.9 1.7 %shard_map.115 = f32[10,5376]{1,0:T(8,128)} custom-call(s32[1]{0:T(128)} %bitcast.core, f32[16,16,128]{2,1,0:T(8,128)} %copy-done.3, f32[16,16,128]{2,1,0:T(8,128)} %copy-done.4), custom_call_target="tpu_custom_call" | custom-call | tf_op jit(solution)/shard_map/pallas_call | solution.py:294
  (7 shorter events, 0.1 us)
Async XLA Ops:
  1.6 11.7 %collective-permute-start.1 = (f32[40,768]{1,0:T(8,128)S(1)}, f32[40,768]{1,0:T(8,128)S(1)}, u32[]{:S(2)}, u32[]{:S(2)}) collective-permute-start(f32[40,768]{1,0:T(8,128)S(1)} %get-tuple-element.8), channel_id=1, source_target_pairs={{1,0},{2,1},{3,2},{4,3},{5,4},{6,5},{7,6},{8,7},{9,8},{10,9},{11,1... | collective-permute-start | bytes 368648 | tf_op jit(solution)/shard_map/ppermute | solution.py:335
  9.3 7.6 %collective-permute-start = (f32[40,768]{1,0:T(8,128)S(1)}, f32[40,768]{1,0:T(8,128)S(1)}, u32[]{:S(2)}, u32[]{:S(2)}) collective-permute-start(f32[40,768]{1,0:T(8,128)S(1)} %get-tuple-element.9), channel_id=1, source_target_pairs={{0,1},{1,2},{2,3},{3,4},{4,5},{5,6},{6,7},{7,8},{8,9},{9,10},{10,1... | collective-permute-start | bytes 368648 | tf_op jit(solution)/shard_map/ppermute | solution.py:334
  10.7 40.6 %copy-start.5 = (s32[5,5]{1,0:T(8,128)S(1)}, s32[5,5]{1,0:T(8,128)}, u32[]{:S(2)}) copy-start(s32[5,5]{1,0:T(8,128)} %param.15) | copy-start | bytes 304
  50.5 7.5 %collective-permute-start.2 = (f32[8,264,128]{2,1,0:T(8,128)}, f32[8,264,128]{2,1,0:T(8,128)}, u32[]{:S(2)}, u32[]{:S(2)}) collective-permute-start(f32[8,264,128]{2,1,0:T(8,128)} %all_to_all.20.mine), channel_id=1, source_target_pairs={{0,16},{16,0},{32,48},{48,32},{64,80},{80,64},{96,112},{112,96},{1... | collective-permute-start | bytes 3244040 | tf_op jit(solution)/shard_map/ppermute | solution.py:319
  51.6 6.4 %copy-start.1 = (f32[128,384]{1,0:T(8,128)S(1)}, f32[128,384]{1,0:T(8,128)}, u32[]{:S(2)}) copy-start(f32[128,384]{1,0:T(8,128)} %constant.75.clone.lane_tab) | copy-start | bytes 589828
  51.6 6.4 %copy-start.2 = (f32[64,128]{1,0:T(8,128)S(1)}, f32[64,128]{1,0:T(8,128)}, u32[]{:S(2)}) copy-start(f32[64,128]{1,0:T(8,128)} %constant.74.clone.sub_tab) | copy-start | bytes 98308
  58.0 1.1 copy-start
  79.2 1.4 %collective-permute-start.3 = (f32[16,16,128]{2,1,0:T(8,128)S(1)}, f32[16,16,128]{2,1,0:T(8,128)S(1)}, u32[]{:S(2)}, u32[]{:S(2)}) collective-permute-start(f32[16,16,128]{2,1,0:T(8,128)S(1)} %get-tuple-element.7), channel_id=1, source_target_pairs={{0,16},{16,0},{32,48},{48,32},{64,80},{80,64},{96,112},{112,96},{1... | collective-permute-start | bytes 393224 | tf_op jit(solution)/shard_map/ppermute | solution.py:319
  115.1 5.1 %copy-start.3 = (f32[16,16,128]{2,1,0:T(8,128)}, f32[16,16,128]{2,1,0:T(8,128)S(1)}, u32[]{:S(2)}) copy-start(f32[16,16,128]{2,1,0:T(8,128)S(1)} %all_to_all.23.mine) | copy-start | bytes 393220
  115.1 5.1 %collective-permute-start.4 = (f32[16,16,128]{2,1,0:T(8,128)S(1)}, f32[16,16,128]{2,1,0:T(8,128)S(1)}, u32[]{:S(2)}, u32[]{:S(2)}) collective-permute-start(f32[16,16,128]{2,1,0:T(8,128)S(1)} %all_to_all.23.mine), channel_id=1, source_target_pairs={{0,16},{16,0},{32,48},{48,32},{64,80},{80,64},{96,112},{112,96},{1... | collective-permute-start | bytes 393224 | tf_op jit(solution)/shard_map/ppermute | solution.py:319
  120.2 0.7 copy-start.4

commit v3 on v2

--- a/solution.py
+++ b/solution.py
@@ -36,7 +36,6 @@
 SLAB_ROWS = 16
 FLAT = 300
 FLAT_PAD = 384
-HIGHEST = lax.Precision.HIGHEST
 
 
 def toeplitz():
@@ -45,28 +44,47 @@
     return np.where(d == 0, 0.0, -4.0 * (-1.0) ** d / np.tan(np.pi * safe / 16))
 
 
+def parts(value, count):
+    found = []
+    rest = value
+    for _ in range(count):
+        found.append(rest.astype(jnp.bfloat16))
+        rest = rest - found[-1].astype(jnp.float32)
+    return found
+
+
 def sublane_table():
     t = toeplitz()
     x = np.arange(PIX)
-    rows = [t[x, (x - d) % PIX] for d in range(1, PIX)]
-    rows.append((-1.0) ** x)
+    rows = [(2.0 if d == 4 else 4.0) * t[x, (x - d) % PIX] for d in range(1, 5)]
     return np.repeat(np.concatenate(rows)[:, None], LANES, axis=1).astype(np.float32)
 
 
 def lane_table():
     t = toeplitz()
-    table = np.zeros((LANES, 3 * LANES))
-    for lane in range(WINDOW):
-        group, y = divmod(lane, PIX)
-        for z in range(PIX):
-            table[group * PIX + z, lane] = t[y, z]
-        table[lane, LANES + group] = (-1.0) ** y
-        table[lane, 2 * LANES + group] = 1.0 / 1024
-    return table.astype(np.float32)
+    table = np.zeros((2 * LANES, 2 * LANES))
+    y = np.arange(PIX)
+    sign = (-1.0) ** (y[:, None] - y[None, :])
+    for group in range(WINDOW // PIX):
+        rows = slice(group * PIX, (group + 1) * PIX)
+        after = slice(LANES + group * PIX, LANES + (group + 1) * PIX)
+        table[rows, rows] = 4.0 * t.T
+        table[after, rows] = -8.0 * sign
+        table[rows, after] = -8.0 * sign
+    first = table.astype(jnp.bfloat16)
+    second = (table - first.astype(np.float64)).astype(jnp.bfloat16)
+    return np.concatenate([first, second])
+
+
+def group_table():
+    table = np.zeros((LANES, LANES))
+    lane = np.arange(WINDOW)
+    table[lane, lane // PIX] = 1.0 / 1024
+    return table.astype(jnp.bfloat16)
 
 
 def order_table():
-    table = np.zeros((FLAT_PAD, FLAT_PAD), np.float32)
+    table = np.zeros((FLAT_PAD, FLAT_PAD))
     for s in range(2):
         for k in range(2):
             for b in range(5):
@@ -74,7 +92,7 @@
                     for a in range(5):
                         row = (s * 10 + k * 5 + b) * 16 + kk * 5 + a
                         table[row, (((3 * k + kk) * 5 + a) * 5 + b) * 2 + s] = 1.0
-    return table
+    return table.astype(jnp.bfloat16)
 
 
 def lane_index(shape):
@@ -94,16 +112,16 @@
         right = pltpu.roll(ref[rows, (tile + 1) * LANES : (tile + 2) * LANES], LANES - shift, 1)
         return jnp.where(lane_index(left.shape) < LANES - shift, left, right)
 
-    parts = ((low, 0), (core, 40), (high, 80), (fresh, 120))
+    sources = ((low, 0), (core, 40), (high, 80), (fresh, 120))
 
     def columns(first, start):
-        ref, base = [part for part in parts if part[1] <= first][-1]
+        ref, base = [source for source in sources if source[1] <= first][-1]
         return window(ref, first - base, PIX, start)
 
     lane = lane_index((PIX, LANES))
     for m in range(CHIPS):
         start = FIRST + m * CHIP_ROWS
-        for ref, base in parts:
+        for ref, base in sources:
             count = UPDATES if base == WINDOW else 40
             out[m, base : base + count, :] = window(ref, 0, count, start)
         for r in range(REST // PIX):
@@ -137,17 +155,22 @@
 
 
 def main_kernel(
-    core, mine, other, sub_tab, lane_tab, order_tab, mask, recon,
+    core, mine, other, sub_hbm, lane_hbm, group_hbm, order_hbm, mask, recon,
     keep, send, flat_out,
-    state, phase, groups, numbers, meta, arrived,
+    state, phase, sums, numbers, sub_tab, lane_tab, group_tab, order_tab, meta, arrived,
 ):
     lane = lane_index((40, LANES))
     side = core[0]
     for p in range(CHIPS):
         numbers[p] = mine[p, META:, :].astype(jnp.int32)
         numbers[CHIPS + p] = other[p, META:, :].astype(jnp.int32)
-    copy = pltpu.make_async_copy(numbers, meta, arrived)
+    copy = pltpu.make_async_copy(numbers, meta, arrived.at[0])
     copy.start()
+    tables = ((sub_hbm, sub_tab), (lane_hbm, lane_tab), (group_hbm, group_tab), (order_hbm, order_tab))
+    fetches = [pltpu.make_async_copy(source, target, arrived.at[1 + i]) for i, (source, target) in enumerate(tables)]
+    for fetch in fetches:
+        fetch.start()
+    sums[...] = jnp.zeros_like(sums)
 
     cut = LANES - 40 * side
     turn = lax.rem(cut, LANES)
@@ -165,7 +188,7 @@
     lax.fori_loop(0, CHIPS, begin, 0)
     copy.wait()
 
-    def step(t, carry):
+    def cut_and_add(t):
         def layer(l, acc):
             dst = pl.multiple_of(meta[l, 6, t], NEW_COLS)
             src = pl.multiple_of(WINDOW + t * NEW_COLS, NEW_COLS)
@@ -175,53 +198,68 @@
                 for g in range(STARS)
             )
 
-        zero = jnp.zeros((40, LANES), jnp.float32)
-        acc = lax.fori_loop(0, 2 * CHIPS, layer, (zero,) * STARS, unroll=8)
+        acc = (jnp.zeros((40, LANES), jnp.float32),) * STARS
+        for l in range(2 * CHIPS):
+            acc = layer(l, acc)
         for k in range(2):
             one, two, three = acc[3 * k : 3 * k + 3]
             joined = jnp.where(lane < 40, one, jnp.where(lane < 80, pltpu.roll(two, 40, 1), pltpu.roll(three, 80, 1)))
-            for b in range(5):
-                row = pl.multiple_of(((k * 5 + b) * STEPS + t) * PIX, PIX)
-                phase[pl.ds(row, PIX), :] = joined[b * PIX : (b + 1) * PIX, :]
+            phase[lax.rem(t, 2), k * 40 : (k + 1) * 40, :] = joined
+
+    def spots(t):
+        sine, cosine = sincos(phase[lax.rem(t, 2)])
+        c1, c2 = parts(cosine, 2)
+        s1, s2 = parts(sine, 2)
+        head = jnp.concatenate([c1, s1], axis=1)
+        tail = jnp.concatenate([c2, s2], axis=1)
+        first = jnp.dot(jnp.concatenate([head, tail]), lane_tab[: 2 * LANES], preferred_element_type=jnp.float32)
+        second = jnp.dot(head, lane_tab[2 * LANES :], preferred_element_type=jnp.float32)
+        along = first[:80] + first[80:] + second
+        z_y = sine * along[:, :LANES] + cosine * along[:, LANES:]
+
+        c3 = cosine.reshape(10, PIX, LANES)
+        s3 = sine.reshape(10, PIX, LANES)
+        by_sine = -8.0 * s3
+        by_cosine = -8.0 * c3
+        for d in range(1, 5):
+            weight = sub_tab[(d - 1) * PIX : d * PIX, :][None]
+            even = -8.0 if d == 4 else 16.0 * (-1.0) ** (d + 1)
+            c_d = pltpu.roll(c3, d, 1)
+            s_d = pltpu.roll(s3, d, 1)
+            by_sine = by_sine + (weight * c_d + even * s_d)
+            by_cosine = by_cosine + (even * c_d - weight * s_d)
+        z_x = jnp.sum(s3 * by_sine + c3 * by_cosine, axis=1)
+        z_y = jnp.sum(z_y.reshape(10, PIX, LANES), axis=1)
+        for unit in range(10):
+            sums[unit, pl.ds(t, 1), :] = z_x[unit : unit + 1]
+            sums[10 + unit, pl.ds(t, 1), :] = z_y[unit : unit + 1]
+
+    cut_and_add(0)
+    for fetch in fetches:
+        fetch.wait()
+
+    def step(t, carry):
+        cut_and_add(t)
+        spots(t - 1)
         return carry
 
-    lax.fori_loop(0, STEPS, step, 0)
-
-    groups[...] = jnp.zeros_like(groups)
-    size = STEPS * PIX
-
-    def spots(kb, carry):
-        sine, cosine = sincos(phase[pl.ds(pl.multiple_of(kb * size, PIX), size), :])
-        both = jnp.concatenate([cosine, sine], axis=0)
-        along = jnp.dot(both, lane_tab[:, : 2 * LANES], precision=HIGHEST, preferred_element_type=jnp.float32)
-        s3 = sine.reshape(STEPS, PIX, LANES)
-        c3 = cosine.reshape(STEPS, PIX, LANES)
-        acc = jnp.zeros_like(c3)
-        for d in range(1, PIX):
-            acc = acc + sub_tab[(d - 1) * PIX : d * PIX, :][None] * pltpu.roll(c3, d, 1)
-        sign = sub_tab[7 * PIX : 8 * PIX, :][None]
-        alt_c = jnp.sum(sign * c3, axis=1)
-        alt_s = jnp.sum(sign * s3, axis=1)
-        num_x = 4.0 * jnp.sum(s3 * acc, axis=1) - 8.0 * (alt_c * alt_c + alt_s * alt_s)
-        num_y = 4.0 * jnp.sum(s3 * along[:size, :LANES].reshape(STEPS, PIX, LANES), axis=1)
-        alt = along[:, LANES:]
-        alt = alt * alt
-        alt = jnp.sum((alt[:size] + alt[size:]).reshape(STEPS, PIX, LANES), axis=1)
-        grouper = lane_tab[:, 2 * LANES :]
-        got_x = jnp.dot(num_x, grouper, precision=HIGHEST, preferred_element_type=jnp.float32)
-        got_y = jnp.dot(num_y, grouper, precision=HIGHEST, preferred_element_type=jnp.float32) - alt * (8.0 / 1024)
-        for s, got in ((0, got_x), (1, got_y)):
-            unit = s * 10 + kb
-            tile = unit // 8
-            groups[tile, 0:STEPS, :] = groups[tile, 0:STEPS, :] + pltpu.roll(got, (unit % 8) * 16, 1)
-        return carry
-
-    lax.fori_loop(0, 10, spots, 0)
-
-    flat = sum(
-        jnp.dot(groups[i], order_tab[i * LANES : (i + 1) * LANES, :], precision=HIGHEST, preferred_element_type=jnp.float32)
-        for i in range(3)
-    )
+    lax.fori_loop(1, STEPS, step, 0)
+    spots(STEPS - 1)
+
+    units = 20
+    stacked = jnp.concatenate(parts(sums[...].reshape(units * 16, LANES), 3))
+    got = jnp.dot(stacked, group_tab[...], preferred_element_type=jnp.float32)
+    size = units * 16
+    got = (got[:size] + got[size : 2 * size]) + got[2 * size :]
+    tiles = [jnp.zeros((16, LANES), jnp.float32) for _ in range(3)]
+    for unit in range(units):
+        tiles[unit // 8] = tiles[unit // 8] + pltpu.roll(got[unit * 16 : (unit + 1) * 16], (unit % 8) * 16, 1)
+    flat = jnp.zeros((16, FLAT_PAD), jnp.float32)
+    for i in range(3):
+        moved = jnp.dot(
+            jnp.concatenate(parts(tiles[i], 3)), order_tab[i * LANES : (i + 1) * LANES, :], preferred_element_type=jnp.float32
+        )
+        flat = flat + ((moved[:16] + moved[16:32]) + moved[32:])
     flat = flat * mask[...]
     flat_out[...] = flat
     rounded = flat[:, :FLAT].astype(jnp.bfloat16)
@@ -276,18 +314,25 @@
     return pl.pallas_call(
         main_kernel,
         out_shape=(slab, slab, jax.ShapeDtypeStruct((16, FLAT_PAD), jnp.float32)),
-        in_specs=[smem()] + [vmem()] * 7,
+        in_specs=[smem()] + [vmem()] * 2 + [pl.BlockSpec(memory_space=pltpu.HBM)] * 4 + [vmem()] * 2,
         out_specs=(vmem(),) * 3,
         scratch_shapes=[
             pltpu.VMEM((2 * CHIPS, COLS + NEW_COLS, LANES), jnp.float32),
-            pltpu.VMEM((100 * PIX, LANES), jnp.float32),
-            pltpu.VMEM((3, 16, LANES), jnp.float32),
+            pltpu.VMEM((2, 10 * PIX, LANES), jnp.float32),
+            pltpu.VMEM((20, 16, LANES), jnp.float32),
             pltpu.VMEM((2 * CHIPS, 8, LANES), jnp.int32),
+            pltpu.VMEM((4 * PIX, LANES), jnp.float32),
+            pltpu.VMEM((4 * LANES, 2 * LANES), jnp.bfloat16),
+            pltpu.VMEM((LANES, LANES), jnp.bfloat16),
+            pltpu.VMEM((FLAT_PAD, FLAT_PAD), jnp.bfloat16),
             pltpu.SMEM((2 * CHIPS, 8, LANES), jnp.int32),
-            pltpu.SemaphoreType.DMA(()),
+            pltpu.SemaphoreType.DMA((5,)),
         ],
         compiler_params=pltpu.CompilerParams(vmem_limit_bytes=40 << 20),
-    )(core, mine, other, jnp.asarray(sublane_table()), jnp.asarray(lane_table()), jnp.asarray(order_table()), mask, recon)
+    )(
+        core, mine, other, jnp.asarray(sublane_table()), jnp.asarray(lane_table()), jnp.asarray(group_table()),
+        jnp.asarray(order_table()), mask, recon,
+    )
 
 
 def finish(core, mine, other):
@@ -346,9 +391,10 @@
 
     side = (lax.axis_index("layer") % 2).astype(jnp.int32).reshape(1)
     mine = exchange(pack(low, core, high, fresh, meta), groups_by(lambda zh, x, c, y, zl: (c, y, zl)))
+    matrix = jnp.transpose(recon, (0, 2, 3, 1, 4)).reshape(FLAT, ACTS)
+    mine, matrix = lax.optimization_barrier((mine, matrix))
     other = to_other_core(mine)
 
-    matrix = jnp.transpose(recon, (0, 2, 3, 1, 4)).reshape(FLAT, ACTS)
     mask = jnp.broadcast_to(valid.astype(jnp.float32)[None, :, :, None], (STARS, 5, 5, 2)).reshape(1, FLAT)
     mask = jnp.pad(mask, ((0, 0), (0, FLAT_PAD - FLAT)))
     keep, send, flat = slopes_and_products(side, mine, other, mask, matrix)

time: 123 us -> 115 us (0.935)
  blocking collectives: 67 us -> 36.5 us
  waiting for transfers between devices: 5.07 us -> 21.8 us
  starting transfers between devices: 12.8 us -> 21 us
  Pallas kernels: 22.7 us -> 17.4 us
  local copies, waits for them, and re-layouts: 12.1 us -> 15 us
    all_to_all x4 -> x3, blocking collectives: 67 us -> 36.5 us  [exchange(): lax.all_to_all(blocks, ('layer', 'sub'), 0, 0, tiled=True, axis_index_gro...]
    all_to_all x0 -> x1, waiting for transfers between devices: none -> 16.2 us  [exchange(): lax.all_to_all(blocks, ('layer', 'sub'), 0, 0, tiled=True, axis_index_gro...]
    all_to_all x0 -> x1, starting transfers between devices: none -> 7.95 us  [exchange(): lax.all_to_all(blocks, ('layer', 'sub'), 0, 0, tiled=True, axis_index_gro...]
    pallas_call x1, Pallas kernels: 20.1 us -> 13.7 us  [slopes_and_products(): pl.pallas_call(main_kernel, out_shape=(slab, slab, jax.ShapeDtypeStruct((...]
    unnamed x12 -> x14, local copies, waits for them, and re-layouts: 1.74 us -> 3.12 us
  transfers between devices with their start and end apart: 5 -> 6, of which waited for: 3 -> 5; matrix products, arithmetic and copies ran while one was open for 9% -> 11% of each run, Pallas kernels for 0% -> 0%
where the time goes in v3:
time: 115 us
  blocking collectives  36.5 us (32%)
  waiting for transfers between devices  21.8 us (19%)
  starting transfers between devices  21 us (18%)
  Pallas kernels  17.4 us (15%)
  local copies, waits for them, and re-layouts  15 us (13%)
  other arithmetic  2.17 us (2%)
    all_to_all x3, blocking collectives, exchange(): lax.all_to_all(blocks, ('layer', 'sub'), 0, 0, tiled=True, axis_index_gro...  36.5 us
    all_to_all x1, waiting for transfers between devices, exchange(): lax.all_to_all(blocks, ('layer', 'sub'), 0, 0, tiled=True, axis_index_gro...  16.2 us
    pallas_call x1, Pallas kernels, slopes_and_products(): pl.pallas_call(main_kernel, out_shape=(slab, slab, jax.ShapeDtypeStruct((...  13.7 us
    all_to_all x1, starting transfers between devices, exchange(): lax.all_to_all(blocks, ('layer', 'sub'), 0, 0, tiled=True, axis_index_gro...  7.95 us
    ppermute x1, starting transfers between devices, local(): lax.ppermute(strip(jnp.where(owner == 0, PUP_TURN + 1, PUP_TURN)), 'sub',...  7.7 us
    reshape x1, local copies, waits for them, and re-layouts, local(): matrix = jnp.transpose(recon, (0, 2, 3, 1, 4)).reshape(FLAT, ACTS)  6.38 us
    ppermute x3, starting transfers between devices, to_other_core(): return lax.ppermute(block, 'layer', [(i, i ^ 1) for i in range(16)])  5.36 us
    ppermute x1, waiting for transfers between devices, local(): lax.ppermute(strip(jnp.where(owner == count - 1, PUP_TURN - 1, PUP_TURN))...  3.63 us
  transfers between devices with their start and end apart: 6, of which 5 were waited for; matrix products, arithmetic and copies ran while one was open for 11% of the time, Pallas kernels for 0%

profile of v3, /device:TPU:1, one launch (start us, length us, event | category | flops | bytes accessed | tf_op | source)
XLA Modules:
  0.0 114.6 jit_solution(12231115176479536554)
XLA Ops:
  0.6 1.0 dynamic-slice_bitcast_fusion
  1.6 7.7 %collective-permute-start.1 = (f32[40,768]{1,0:T(8,128)S(1)}, f32[40,768]{1,0:T(8,128)S(1)}, u32[]{:S(2)}, u32[]{:S(2)}) collective-permute-start(f32[40,768]{1,0:T(8,128)S(1)} %get-tuple-element.12), channel_id=1, source_target_pairs={{1,0},{2,1},{3,2},{4,3},{5,4},{6,5},{7,6},{8,7},{9,8},{10,9},{11,1... | collective-permute-start | bytes 368648 | tf_op jit(solution)/shard_map/ppermute | solution.py:380
  9.3 0.0 collective-permute-start
  9.3 0.7 fusion.1
  10.0 0.7 add_select_fusion
  10.7 0.9 slice_bitcast_fusion.1.core
  11.6 1.0 slice_bitcast_fusion.fresh
  12.6 0.7 fusion.2
  13.3 0.1 add_convert_fusion.meta
  13.3 0.0 collective-permute-done.1.high
  13.3 3.6 %collective-permute-done.low = f32[40,768]{1,0:T(8,128)S(1)} collective-permute-done((f32[40,768]{1,0:T(8,128)S(1)}, f32[40,768]{1,0:T(8,128)S(1)}, u32[]{:S(2)}, u32[]{:S(2)}) %collective-permute-start) | collective-permute-done | bytes 122912 | tf_op jit(solution)/shard_map/ppermute | solution.py:379
  17.0 1.9 %shard_map.122 = f32[8,264,128]{2,1,0:T(8,128)} custom-call(f32[40,768]{1,0:T(8,128)S(1)} %collective-permute-done.low, f32[40,768]{1,0:T(8,128)S(1)} %slice_bitcast_fusion.1.core, f32[40,768]{1,0:T(8,128)S(1)} %collective-permute-done.1.high, f32[80,768]{1,0:T(8,128)S(1)} %slice_bitcast_fusion.fresh, f32[8,128]{1,0:T(8,128)S(1)} %add_convert_fusion.meta), custom_call_target="tpu_custom_call" | custom-call | tf_op jit(solution)/shard_map/pallas_call | solution.py:303
  18.9 7.9 %all-to-all-start = ((f32[8,264,128]{2,1,0:T(8,128)}), f32[8,264,128]{2,1,0:T(8,128)}, u32[]{:S(2)}, u32[]{:S(2)}) async-start(f32[8,264,128]{2,1,0:T(8,128)} %shard_map.122), calls=%async_computation | async-start | bytes 2162688 | tf_op jit(solution)/shard_map/all_to_all | solution.py:356
  26.8 0.0 copy-start.6
  26.8 0.0 copy-start.1
  26.8 6.4 %reshape.76.recon = bf16[300,5376]{1,0:T(8,128)(2,1)S(1)} reshape(bf16[6,5,5,2,5376]{4,3,2,1,0:T(2,128)(2,1)} %bitcast.41) | data formatting | bytes 6451200 | tf_op jit(solution)/shard_map/reshape | solution.py:394
  33.2 16.2 %all-to-all-done.mine = f32[8,264,128]{2,1,0:T(8,128)} async-done(((f32[8,264,128]{2,1,0:T(8,128)}), f32[8,264,128]{2,1,0:T(8,128)}, u32[]{:S(2)}, u32[]{:S(2)}) %all-to-all-start) | async-done | bytes 1081376 | tf_op jit(solution)/shard_map/all_to_all | solution.py:356
  49.4 0.6 collective-permute-start.2
  50.1 0.0 copy-done.6
  50.1 0.7 broadcast_in_dim.11
  50.8 1.0 reshape.77
  51.9 0.9 collective-permute-done.2.other
  52.7 0.0 copy-done.1
  52.7 0.0 copy-start
  52.7 1.0 copy-done
  53.7 0.0 copy-start.2
  53.7 0.8 copy-done.2
  54.5 0.0 copy-start.3
  54.5 0.7 copy-done.3
  55.2 13.7 %shard_map.123 = (f32[16,16,128]{2,1,0:T(8,128)S(1)}, f32[16,16,128]{2,1,0:T(8,128)S(1)}, f32[16,384]{1,0:T(8,128)S(1)}) custom-call(s32[1]{0:T(128)} %bitcast.core, f32[8,264,128]{2,1,0:T(8,128)} %all-to-all-done.mine, f32[8,264,128]{2,1,0:T(8,128)} %collective-permute-done.2.other, f32[32,128]{1,0:T(8,128)S(1)} %copy-done.3, ...), custom_call_target="tpu_custom_call" | custom-call | tf_op jit(solution)/shard_map/pallas_call | solution.py:314
  68.9 0.5 collective-permute-start.3
  69.4 1.0 collective-permute-done.3
  70.4 13.5 %all_to_all.20 = f32[16,16,128]{2,1,0:T(8,128)S(1)} all-to-all(f32[16,16,128]{2,1,0:T(8,128)S(1)} %add.60), channel_id=1, replica_groups={{0,4,8,12,32,36,40,44,64,68,72,76,96,100,104,108},{1,5,9,13,33,37,41,45..., dimensions={0} | all-to-all | bytes 262144 | tf_op jit(solution)/shard_map/all_to_all | solution.py:356
  83.9 12.8 %all_to_all.21 = f32[8,16,128]{2,1,0:T(8,128)S(1)} all-to-all(f32[8,16,128]{2,1,0:T(8,128)S(1)} %broadcast_in_dim.12), channel_id=1, replica_groups={{0,1,2,3,128,129,130,131},{4,5,6,7,132,133,134,135},{8,9,10,11,136,137,..., dimensions={0} | all-to-all | bytes 131072 | tf_op jit(solution)/shard_map/all_to_all | solution.py:356
  96.7 10.2 %all_to_all.22.mine = f32[16,16,128]{2,1,0:T(8,128)S(1)} all-to-all(f32[16,16,128]{2,1,0:T(8,128)S(1)} %broadcast_in_dim.13), channel_id=1, replica_groups={{0,4,8,12,32,36,40,44,64,68,72,76,96,100,104,108},{1,5,9,13,33,37,41,45..., dimensions={0} | all-to-all | bytes 262144 | tf_op jit(solution)/shard_map/all_to_all | solution.py:356
  106.9 0.0 copy-start.4
  106.9 4.3 %collective-permute-start.4 = (f32[16,16,128]{2,1,0:T(8,128)S(1)}, f32[16,16,128]{2,1,0:T(8,128)S(1)}, u32[]{:S(2)}, u32[]{:S(2)}) collective-permute-start(f32[16,16,128]{2,1,0:T(8,128)S(1)} %all_to_all.22.mine), channel_id=1, source_target_pairs={{0,16},{16,0},{32,48},{48,32},{64,80},{80,64},{96,112},{112,96},{1... | collective-permute-start | bytes 393224 | tf_op jit(solution)/shard_map/ppermute | solution.py:364
  111.2 0.1 copy.21
  111.3 0.8 reshape.78
  112.0 0.1 collective-permute-done.4.other
  112.2 0.0 copy-done.4
  112.2 0.0 copy-start.5
  112.2 0.7 copy-done.5
  112.8 1.7 %shard_map.124 = f32[10,5376]{1,0:T(8,128)} custom-call(s32[1]{0:T(128)} %bitcast.core, f32[16,16,128]{2,1,0:T(8,128)} %copy-done.4, f32[16,16,128]{2,1,0:T(8,128)} %copy-done.5), custom_call_target="tpu_custom_call" | custom-call | tf_op jit(solution)/shard_map/pallas_call | solution.py:339
  (7 shorter events, 0.1 us)
Async XLA Ops:
  1.6 11.7 %collective-permute-start.1 = (f32[40,768]{1,0:T(8,128)S(1)}, f32[40,768]{1,0:T(8,128)S(1)}, u32[]{:S(2)}, u32[]{:S(2)}) collective-permute-start(f32[40,768]{1,0:T(8,128)S(1)} %get-tuple-element.12), channel_id=1, source_target_pairs={{1,0},{2,1},{3,2},{4,3},{5,4},{6,5},{7,6},{8,7},{9,8},{10,9},{11,1... | collective-permute-start | bytes 368648 | tf_op jit(solution)/shard_map/ppermute | solution.py:380
  9.3 7.6 %collective-permute-start = (f32[40,768]{1,0:T(8,128)S(1)}, f32[40,768]{1,0:T(8,128)S(1)}, u32[]{:S(2)}, u32[]{:S(2)}) collective-permute-start(f32[40,768]{1,0:T(8,128)S(1)} %get-tuple-element.13), channel_id=1, source_target_pairs={{0,1},{1,2},{2,3},{3,4},{4,5},{5,6},{6,7},{7,8},{8,9},{9,10},{10,1... | collective-permute-start | bytes 368648 | tf_op jit(solution)/shard_map/ppermute | solution.py:379
  18.9 30.6 %all-to-all-start = ((f32[8,264,128]{2,1,0:T(8,128)}), f32[8,264,128]{2,1,0:T(8,128)}, u32[]{:S(2)}, u32[]{:S(2)}) async-start(f32[8,264,128]{2,1,0:T(8,128)} %shard_map.122), calls=%async_computation | async-start | bytes 2162688 | tf_op jit(solution)/shard_map/all_to_all | solution.py:356
  26.8 23.2 %copy-start.6 = (s32[5,5]{1,0:T(8,128)S(1)}, s32[5,5]{1,0:T(8,128)}, u32[]{:S(2)}) copy-start(s32[5,5]{1,0:T(8,128)} %param.16) | copy-start | bytes 304
  26.8 25.9 %copy-start.1 = (bf16[512,256]{1,0:T(8,128)(2,1)S(1)}, bf16[512,256]{1,0:T(8,128)(2,1)}, u32[]{:S(2)}) copy-start(bf16[512,256]{1,0:T(8,128)(2,1)} %constant.77.clone.lane_hbm) | copy-start | bytes 786436
  49.4 3.3 %collective-permute-start.2 = (f32[8,264,128]{2,1,0:T(8,128)}, f32[8,264,128]{2,1,0:T(8,128)}, u32[]{:S(2)}, u32[]{:S(2)}) collective-permute-start(f32[8,264,128]{2,1,0:T(8,128)} %all-to-all-done.mine), channel_id=1, source_target_pairs={{0,16},{16,0},{32,48},{48,32},{64,80},{80,64},{96,112},{112,96},{1... | collective-permute-start | bytes 3244040 | tf_op jit(solution)/shard_map/ppermute | solution.py:364
  52.7 1.0 copy-start
  53.7 0.8 copy-start.2
  54.5 0.7 copy-start.3
  68.9 1.5 %collective-permute-start.3 = (f32[16,16,128]{2,1,0:T(8,128)S(1)}, f32[16,16,128]{2,1,0:T(8,128)S(1)}, u32[]{:S(2)}, u32[]{:S(2)}) collective-permute-start(f32[16,16,128]{2,1,0:T(8,128)S(1)} %get-tuple-element.11), channel_id=1, source_target_pairs={{0,16},{16,0},{32,48},{48,32},{64,80},{80,64},{96,112},{112,96},{1... | collective-permute-start | bytes 393224 | tf_op jit(solution)/shard_map/ppermute | solution.py:364
  106.9 5.2 %copy-start.4 = (f32[16,16,128]{2,1,0:T(8,128)}, f32[16,16,128]{2,1,0:T(8,128)S(1)}, u32[]{:S(2)}) copy-start(f32[16,16,128]{2,1,0:T(8,128)S(1)} %all_to_all.22.mine) | copy-start | bytes 393220
  106.9 5.2 %collective-permute-start.4 = (f32[16,16,128]{2,1,0:T(8,128)S(1)}, f32[16,16,128]{2,1,0:T(8,128)S(1)}, u32[]{:S(2)}, u32[]{:S(2)}) collective-permute-start(f32[16,16,128]{2,1,0:T(8,128)S(1)} %all_to_all.22.mine), channel_id=1, source_target_pairs={{0,16},{16,0},{32,48},{48,32},{64,80},{80,64},{96,112},{112,96},{1... | collective-permute-start | bytes 393224 | tf_op jit(solution)/shard_map/ppermute | solution.py:364
  112.2 0.7 copy-start.5

commit v4 on v3

--- a/solution.py
+++ b/solution.py
@@ -53,11 +53,13 @@
     return found
 
 
-def sublane_table():
+def ahead(d):
     t = toeplitz()
-    x = np.arange(PIX)
-    rows = [(2.0 if d == 4 else 4.0) * t[x, (x - d) % PIX] for d in range(1, 5)]
-    return np.repeat(np.concatenate(rows)[:, None], LANES, axis=1).astype(np.float32)
+    x = lax.broadcasted_iota(jnp.int32, (PIX, LANES), 0)
+    weight = jnp.zeros((PIX, LANES), jnp.float32)
+    for i in range(PIX):
+        weight = jnp.where(x == i, jnp.float32((2.0 if d == 4 else 4.0) * t[i, (i - d) % PIX]), weight)
+    return weight
 
 
 def lane_table():
@@ -77,22 +79,42 @@
 
 
 def group_table():
-    table = np.zeros((LANES, LANES))
-    lane = np.arange(WINDOW)
-    table[lane, lane // PIX] = 1.0 / 1024
-    return table.astype(jnp.bfloat16)
-
-
-def order_table():
-    table = np.zeros((FLAT_PAD, FLAT_PAD))
-    for s in range(2):
-        for k in range(2):
-            for b in range(5):
-                for kk in range(3):
-                    for a in range(5):
-                        row = (s * 10 + k * 5 + b) * 16 + kk * 5 + a
-                        table[row, (((3 * k + kk) * 5 + a) * 5 + b) * 2 + s] = 1.0
-    return table.astype(jnp.bfloat16)
+    lane = lax.broadcasted_iota(jnp.int32, (LANES, LANES), 0)
+    group = lax.broadcasted_iota(jnp.int32, (LANES, LANES), 1)
+    first = group * PIX
+    return jnp.where((lane >= first) & (lane < first + PIX) & (lane < WINDOW), 1.0 / 1024, 0.0).astype(jnp.bfloat16)
+
+
+def multiple(value, step, count):
+    found = jnp.zeros_like(value)
+    for i in range(1, count + 1):
+        found = found + (value >= step * i).astype(jnp.int32)
+    return found
+
+
+def order_table(tile):
+    row = lax.broadcasted_iota(jnp.int32, (LANES, LANES), 0) + tile * LANES
+    column = lax.broadcasted_iota(jnp.int32, (LANES, LANES), 1)
+    unit = lax.shift_right_logical(row, 4)
+    place = row & 15
+    s = multiple(unit, 10, 1)
+    k = multiple(unit - 10 * s, 5, 1)
+    b = unit - 10 * s - 5 * k
+    kk = multiple(place, 5, 2)
+    target = (((3 * k + kk) * 5 + place - 5 * kk) * 5 + b) * 2 + s
+    target = jnp.where((place < 15) & (unit < 20), target, -1)
+    blocks = [(target == column + i * LANES).astype(jnp.float32).astype(jnp.bfloat16) for i in range(FLAT_PAD // LANES)]
+    return jnp.concatenate(blocks, axis=1)
+
+
+def lit(flags):
+    place = lax.shift_right_logical(lax.broadcasted_iota(jnp.int32, (8, FLAT_PAD), 1), 1)
+    place = place - 25 * multiple(place, 25, 7)
+    found = jnp.zeros((8, FLAT_PAD), jnp.float32)
+    for a in range(5):
+        for b in range(5):
+            found = jnp.where(place == a * 5 + b, flags[1 + a * 5 + b].astype(jnp.float32), found)
+    return found
 
 
 def lane_index(shape):
@@ -155,21 +177,17 @@
 
 
 def main_kernel(
-    core, mine, other, sub_hbm, lane_hbm, group_hbm, order_hbm, mask, recon,
+    flags, mine, other, lane_tab, recon,
     keep, send, flat_out,
-    state, phase, sums, numbers, sub_tab, lane_tab, group_tab, order_tab, meta, arrived,
+    state, phase, sums, numbers, meta, arrived,
 ):
     lane = lane_index((40, LANES))
-    side = core[0]
+    side = flags[0]
     for p in range(CHIPS):
         numbers[p] = mine[p, META:, :].astype(jnp.int32)
         numbers[CHIPS + p] = other[p, META:, :].astype(jnp.int32)
-    copy = pltpu.make_async_copy(numbers, meta, arrived.at[0])
+    copy = pltpu.make_async_copy(numbers, meta, arrived)
     copy.start()
-    tables = ((sub_hbm, sub_tab), (lane_hbm, lane_tab), (group_hbm, group_tab), (order_hbm, order_tab))
-    fetches = [pltpu.make_async_copy(source, target, arrived.at[1 + i]) for i, (source, target) in enumerate(tables)]
-    for fetch in fetches:
-        fetch.start()
     sums[...] = jnp.zeros_like(sums)
 
     cut = LANES - 40 * side
@@ -189,18 +207,16 @@
     copy.wait()
 
     def cut_and_add(t):
-        def layer(l, acc):
+        for l in range(2 * CHIPS):
             dst = pl.multiple_of(meta[l, 6, t], NEW_COLS)
             src = pl.multiple_of(WINDOW + t * NEW_COLS, NEW_COLS)
             state[l, pl.ds(dst, NEW_COLS), :] = state[l, pl.ds(src, NEW_COLS), :]
-            return tuple(
-                acc[g] + pltpu.roll(state[l, pl.ds(meta[l, g, t], 40), :], meta[l, g, ROLL_AT + t], 1)
-                for g in range(STARS)
-            )
-
-        acc = (jnp.zeros((40, LANES), jnp.float32),) * STARS
-        for l in range(2 * CHIPS):
-            acc = layer(l, acc)
+        acc = []
+        for g in range(STARS):
+            total = jnp.zeros((40, LANES), jnp.float32)
+            for l in range(2 * CHIPS):
+                total = total + pltpu.roll(state[l, pl.ds(meta[l, g, t], 40), :], meta[l, g, ROLL_AT + t], 1)
+            acc.append(total)
         for k in range(2):
             one, two, three = acc[3 * k : 3 * k + 3]
             joined = jnp.where(lane < 40, one, jnp.where(lane < 80, pltpu.roll(two, 40, 1), pltpu.roll(three, 80, 1)))
@@ -222,7 +238,7 @@
         by_sine = -8.0 * s3
         by_cosine = -8.0 * c3
         for d in range(1, 5):
-            weight = sub_tab[(d - 1) * PIX : d * PIX, :][None]
+            weight = weights[d - 1][None]
             even = -8.0 if d == 4 else 16.0 * (-1.0) ** (d + 1)
             c_d = pltpu.roll(c3, d, 1)
             s_d = pltpu.roll(s3, d, 1)
@@ -234,9 +250,8 @@
             sums[unit, pl.ds(t, 1), :] = z_x[unit : unit + 1]
             sums[10 + unit, pl.ds(t, 1), :] = z_y[unit : unit + 1]
 
+    weights = [ahead(d) for d in range(1, 5)]
     cut_and_add(0)
-    for fetch in fetches:
-        fetch.wait()
 
     def step(t, carry):
         cut_and_add(t)
@@ -248,7 +263,7 @@
 
     units = 20
     stacked = jnp.concatenate(parts(sums[...].reshape(units * 16, LANES), 3))
-    got = jnp.dot(stacked, group_tab[...], preferred_element_type=jnp.float32)
+    got = jnp.dot(stacked, group_table(), preferred_element_type=jnp.float32)
     size = units * 16
     got = (got[:size] + got[size : 2 * size]) + got[2 * size :]
     tiles = [jnp.zeros((16, LANES), jnp.float32) for _ in range(3)]
@@ -257,10 +272,11 @@
     flat = jnp.zeros((16, FLAT_PAD), jnp.float32)
     for i in range(3):
         moved = jnp.dot(
-            jnp.concatenate(parts(tiles[i], 3)), order_tab[i * LANES : (i + 1) * LANES, :], preferred_element_type=jnp.float32
+            jnp.concatenate(parts(tiles[i], 3)), order_table(i), preferred_element_type=jnp.float32
         )
         flat = flat + ((moved[:16] + moved[16:32]) + moved[32:])
-    flat = flat * mask[...]
+    shown = lit(flags)
+    flat = flat * jnp.concatenate([shown, shown])
     flat_out[...] = flat
     rounded = flat[:, :FLAT].astype(jnp.bfloat16)
     for out, half in ((keep, side), (send, 1 - side)):
@@ -305,34 +321,27 @@
         out_shape=jax.ShapeDtypeStruct((CHIPS, PAYLOAD, LANES), jnp.float32),
         in_specs=[vmem()] * 5,
         out_specs=vmem(),
-        compiler_params=pltpu.CompilerParams(vmem_limit_bytes=32 << 20),
+        compiler_params=pltpu.CompilerParams(vmem_limit_bytes=16 << 20),
     )(low, core, high, fresh, meta)
 
 
-def slopes_and_products(core, mine, other, mask, recon):
+def slopes_and_products(flags, mine, other, recon):
     slab = jax.ShapeDtypeStruct((SLABS, SLAB_ROWS, LANES), jnp.float32)
     return pl.pallas_call(
         main_kernel,
         out_shape=(slab, slab, jax.ShapeDtypeStruct((16, FLAT_PAD), jnp.float32)),
-        in_specs=[smem()] + [vmem()] * 2 + [pl.BlockSpec(memory_space=pltpu.HBM)] * 4 + [vmem()] * 2,
+        in_specs=[smem()] + [vmem()] * 4,
         out_specs=(vmem(),) * 3,
         scratch_shapes=[
             pltpu.VMEM((2 * CHIPS, COLS + NEW_COLS, LANES), jnp.float32),
             pltpu.VMEM((2, 10 * PIX, LANES), jnp.float32),
             pltpu.VMEM((20, 16, LANES), jnp.float32),
             pltpu.VMEM((2 * CHIPS, 8, LANES), jnp.int32),
-            pltpu.VMEM((4 * PIX, LANES), jnp.float32),
-            pltpu.VMEM((4 * LANES, 2 * LANES), jnp.bfloat16),
-            pltpu.VMEM((LANES, LANES), jnp.bfloat16),
-            pltpu.VMEM((FLAT_PAD, FLAT_PAD), jnp.bfloat16),
             pltpu.SMEM((2 * CHIPS, 8, LANES), jnp.int32),
-            pltpu.SemaphoreType.DMA((5,)),
+            pltpu.SemaphoreType.DMA(()),
         ],
-        compiler_params=pltpu.CompilerParams(vmem_limit_bytes=40 << 20),
-    )(
-        core, mine, other, jnp.asarray(sublane_table()), jnp.asarray(lane_table()), jnp.asarray(group_table()),
-        jnp.asarray(order_table()), mask, recon,
-    )
+        compiler_params=pltpu.CompilerParams(vmem_limit_bytes=20 << 20),
+    )(flags, mine, other, jnp.asarray(lane_table()), recon)
 
 
 def finish(core, mine, other):
@@ -341,6 +350,7 @@
         out_shape=jax.ShapeDtypeStruct((STEPS, ACTS), jnp.float32),
         in_specs=[smem(), vmem(), vmem()],
         out_specs=vmem(),
+        compiler_params=pltpu.CompilerParams(vmem_limit_bytes=8 << 20),
     )(core, mine, other)
 
 
@@ -392,12 +402,11 @@
     side = (lax.axis_index("layer") % 2).astype(jnp.int32).reshape(1)
     mine = exchange(pack(low, core, high, fresh, meta), groups_by(lambda zh, x, c, y, zl: (c, y, zl)))
     matrix = jnp.transpose(recon, (0, 2, 3, 1, 4)).reshape(FLAT, ACTS)
-    mine, matrix = lax.optimization_barrier((mine, matrix))
+    flags = jnp.concatenate([side, valid.reshape(-1)])
+    mine, matrix, flags = lax.optimization_barrier((mine, matrix, flags))
     other = to_other_core(mine)
 
-    mask = jnp.broadcast_to(valid.astype(jnp.float32)[None, :, :, None], (STARS, 5, 5, 2)).reshape(1, FLAT)
-    mask = jnp.pad(mask, ((0, 0), (0, FLAT_PAD - FLAT)))
-    keep, send, flat = slopes_and_products(side, mine, other, mask, matrix)
+    keep, send, flat = slopes_and_products(flags, mine, other, matrix)
 
     plane = groups_by(lambda zh, x, c, y, zl: (c, zh, zl))
     column = groups_by(lambda zh, x, c, y, zl: (c, x, y))

time: 115 us -> 111 us (0.965)
  local copies, waits for them, and re-layouts: 15 us -> 10.9 us
  Pallas kernels: 17.4 us -> 15.7 us
    unnamed x14 -> x6, local copies, waits for them, and re-layouts: 3.12 us -> 0.66 us
    ppermute x3, waiting for transfers between devices: 1.98 us -> 3.65 us  [to_other_core(): return lax.ppermute(block, 'layer', [(i, i ^ 1) for i in range(16)])]
where the time goes in v4:
time: 111 us; the launch traced here: 110 us
  blocking collectives  36.4 us (33%)
  waiting for transfers between devices  22.8 us (21%)
  starting transfers between devices  21 us (19%)
  Pallas kernels  15.7 us (14%)
  local copies, waits for them, and re-layouts  10.9 us (10%)
  other arithmetic  2.75 us (2%)
    all_to_all x3, blocking collectives, exchange(): lax.all_to_all(blocks, ('layer', 'sub'), 0, 0, tiled=True, axis_index_gro...  36.4 us
    all_to_all x1, waiting for transfers between devices, exchange(): lax.all_to_all(blocks, ('layer', 'sub'), 0, 0, tiled=True, axis_index_gro...  15.6 us
    pallas_call x1, Pallas kernels, slopes_and_products(): pl.pallas_call(main_kernel, out_shape=(slab, slab, jax.ShapeDtypeStruct((...  13 us
    all_to_all x1, starting transfers between devices, exchange(): lax.all_to_all(blocks, ('layer', 'sub'), 0, 0, tiled=True, axis_index_gro...  7.95 us
    ppermute x1, starting transfers between devices, local(): lax.ppermute(strip(jnp.where(owner == 0, PUP_TURN + 1, PUP_TURN)), 'sub',...  7.7 us
    reshape x1, local copies, waits for them, and re-layouts, local(): matrix = jnp.transpose(recon, (0, 2, 3, 1, 4)).reshape(FLAT, ACTS)  6.37 us
    ppermute x3, starting transfers between devices, to_other_core(): return lax.ppermute(block, 'layer', [(i, i ^ 1) for i in range(16)])  5.36 us
    ppermute x3, waiting for transfers between devices, to_other_core(): return lax.ppermute(block, 'layer', [(i, i ^ 1) for i in range(16)])  3.65 us
  transfers between devices with their start and end apart: 6, of which 5 were waited for; matrix products, arithmetic and copies ran while one was open for 11% of the time, Pallas kernels for 0%

profile of v4, /device:TPU:1, one launch (start us, length us, event | category | flops | bytes accessed | tf_op | source)
XLA Modules:
  0.0 110.3 jit_solution(9369746616618785499)
XLA Ops:
  0.6 1.0 dynamic-slice_bitcast_fusion
  1.6 7.7 %collective-permute-start.1 = (f32[40,768]{1,0:T(8,128)S(1)}, f32[40,768]{1,0:T(8,128)S(1)}, u32[]{:S(2)}, u32[]{:S(2)}) collective-permute-start(f32[40,768]{1,0:T(8,128)S(1)} %get-tuple-element.14), channel_id=1, source_target_pairs={{1,0},{2,1},{3,2},{4,3},{5,4},{6,5},{7,6},{8,7},{9,8},{10,9},{11,1... | collective-permute-start | bytes 368648 | tf_op jit(solution)/shard_map/ppermute | solution.py:390
  9.3 0.0 collective-permute-start
  9.3 0.7 fusion.1
  10.0 0.7 add_select_fusion
  10.7 0.0 copy-start.2
  10.7 0.9 slice_bitcast_fusion.1.core
  11.6 1.0 slice_bitcast_fusion.fresh
  12.6 0.7 fusion.2
  13.3 0.1 add_convert_fusion.meta
  13.3 0.0 collective-permute-done.1.high
  13.4 3.6 %collective-permute-done.low = f32[40,768]{1,0:T(8,128)S(1)} collective-permute-done((f32[40,768]{1,0:T(8,128)S(1)}, f32[40,768]{1,0:T(8,128)S(1)}, u32[]{:S(2)}, u32[]{:S(2)}) %collective-permute-start) | collective-permute-done | bytes 122912 | tf_op jit(solution)/shard_map/ppermute | solution.py:389
  17.0 1.9 %shard_map.95 = f32[8,264,128]{2,1,0:T(8,128)} custom-call(f32[40,768]{1,0:T(8,128)S(1)} %collective-permute-done.low, f32[40,768]{1,0:T(8,128)S(1)} %slice_bitcast_fusion.1.core, f32[40,768]{1,0:T(8,128)S(1)} %collective-permute-done.1.high, f32[80,768]{1,0:T(8,128)S(1)} %slice_bitcast_fusion.fresh, f32[8,128]{1,0:T(8,128)S(1)} %add_convert_fusion.meta), custom_call_target="tpu_custom_call" | custom-call | tf_op jit(solution)/shard_map/pallas_call | solution.py:319
  18.9 7.9 %all-to-all-start = ((f32[8,264,128]{2,1,0:T(8,128)}), f32[8,264,128]{2,1,0:T(8,128)}, u32[]{:S(2)}, u32[]{:S(2)}) async-start(f32[8,264,128]{2,1,0:T(8,128)} %shard_map.95), calls=%async_computation | async-start | bytes 2162688 | tf_op jit(solution)/shard_map/all_to_all | solution.py:366
  26.8 0.0 copy-done.2
  26.8 0.1 reshape.76
  26.9 0.0 copy-start
  26.9 6.4 %reshape.74.recon = bf16[300,5376]{1,0:T(8,128)(2,1)S(1)} reshape(bf16[6,5,5,2,5376]{4,3,2,1,0:T(2,128)(2,1)} %bitcast.41) | data formatting | bytes 6451200 | tf_op jit(solution)/shard_map/reshape | solution.py:404
  33.3 0.6 pad_add_fusion.flags
  33.9 15.6 %all-to-all-done.mine = f32[8,264,128]{2,1,0:T(8,128)} async-done(((f32[8,264,128]{2,1,0:T(8,128)}), f32[8,264,128]{2,1,0:T(8,128)}, u32[]{:S(2)}, u32[]{:S(2)}) %all-to-all-start) | async-done | bytes 1081376 | tf_op jit(solution)/shard_map/all_to_all | solution.py:366
  49.5 0.6 collective-permute-start.2
  50.1 2.5 %collective-permute-done.2.other = f32[8,264,128]{2,1,0:T(8,128)S(1)} collective-permute-done((f32[8,264,128]{2,1,0:T(8,128)}, f32[8,264,128]{2,1,0:T(8,128)S(1)}, u32[]{:S(2)}, u32[]{:S(2)}) %collective-permute-start.2) | collective-permute-done | bytes 1081376 | tf_op jit(solution)/shard_map/ppermute | solution.py:374
  52.6 0.0 copy-done
  52.6 0.0 copy-start.1
  52.6 0.7 copy-done.1
  53.3 13.0 %shard_map.96 = (f32[16,16,128]{2,1,0:T(8,128)S(1)}, f32[16,16,128]{2,1,0:T(8,128)S(1)}, f32[16,384]{1,0:T(8,128)S(1)}) custom-call(s32[26]{0:T(128)S(1)} %copy-done.1, f32[8,264,128]{2,1,0:T(8,128)} %all-to-all-done.mine, f32[8,264,128]{2,1,0:T(8,128)S(1)} %collective-permute-done.2.other, bf16[512,256]{1,0:T(8,128)(2,1)S(1)} %copy-done, ...), custom_call_target="tpu_custom_call" | custom-call | tf_op jit(solution)/shard_map/pallas_call | solution.py:330
  66.3 0.5 collective-permute-start.3
  66.7 1.0 collective-permute-done.3
  67.7 13.5 %all_to_all.20 = f32[16,16,128]{2,1,0:T(8,128)S(1)} all-to-all(f32[16,16,128]{2,1,0:T(8,128)S(1)} %add.58), channel_id=1, replica_groups={{0,4,8,12,32,36,40,44,64,68,72,76,96,100,104,108},{1,5,9,13,33,37,41,45..., dimensions={0} | all-to-all | bytes 262144 | tf_op jit(solution)/shard_map/all_to_all | solution.py:366
  81.3 12.8 %all_to_all.21 = f32[8,16,128]{2,1,0:T(8,128)S(1)} all-to-all(f32[8,16,128]{2,1,0:T(8,128)S(1)} %broadcast_in_dim.9), channel_id=1, replica_groups={{0,1,2,3,128,129,130,131},{4,5,6,7,132,133,134,135},{8,9,10,11,136,137,..., dimensions={0} | all-to-all | bytes 131072 | tf_op jit(solution)/shard_map/all_to_all | solution.py:366
  94.0 10.2 %all_to_all.22.mine = f32[16,16,128]{2,1,0:T(8,128)S(1)} all-to-all(f32[16,16,128]{2,1,0:T(8,128)S(1)} %broadcast_in_dim.18), channel_id=1, replica_groups={{0,4,8,12,32,36,40,44,64,68,72,76,96,100,104,108},{1,5,9,13,33,37,41,45..., dimensions={0} | all-to-all | bytes 262144 | tf_op jit(solution)/shard_map/all_to_all | solution.py:366
  104.3 4.3 %collective-permute-start.4 = (f32[16,16,128]{2,1,0:T(8,128)S(1)}, f32[16,16,128]{2,1,0:T(8,128)S(1)}, u32[]{:S(2)}, u32[]{:S(2)}) collective-permute-start(f32[16,16,128]{2,1,0:T(8,128)S(1)} %all_to_all.22.mine), channel_id=1, source_target_pairs={{0,16},{16,0},{32,48},{48,32},{64,80},{80,64},{96,112},{112,96},{1... | collective-permute-start | bytes 393224 | tf_op jit(solution)/shard_map/ppermute | solution.py:374
  108.5 0.1 copy.18
  108.6 0.8 reshape.77
  109.4 0.1 collective-permute-done.4.other
  109.5 0.8 shard_map.97
  (5 shorter events, 0.1 us)
Async XLA Ops:
  1.6 11.7 %collective-permute-start.1 = (f32[40,768]{1,0:T(8,128)S(1)}, f32[40,768]{1,0:T(8,128)S(1)}, u32[]{:S(2)}, u32[]{:S(2)}) collective-permute-start(f32[40,768]{1,0:T(8,128)S(1)} %get-tuple-element.14), channel_id=1, source_target_pairs={{1,0},{2,1},{3,2},{4,3},{5,4},{6,5},{7,6},{8,7},{9,8},{10,9},{11,1... | collective-permute-start | bytes 368648 | tf_op jit(solution)/shard_map/ppermute | solution.py:390
  9.3 7.6 %collective-permute-start = (f32[40,768]{1,0:T(8,128)S(1)}, f32[40,768]{1,0:T(8,128)S(1)}, u32[]{:S(2)}, u32[]{:S(2)}) collective-permute-start(f32[40,768]{1,0:T(8,128)S(1)} %get-tuple-element.15), channel_id=1, source_target_pairs={{0,1},{1,2},{2,3},{3,4},{4,5},{5,6},{6,7},{7,8},{8,9},{9,10},{10,1... | collective-permute-start | bytes 368648 | tf_op jit(solution)/shard_map/ppermute | solution.py:389
  10.7 16.1 %copy-start.2 = (s32[5,5]{1,0:T(8,128)S(1)}, s32[5,5]{1,0:T(8,128)}, u32[]{:S(2)}) copy-start(s32[5,5]{1,0:T(8,128)} %param.13) | copy-start | bytes 304
  18.9 30.6 %all-to-all-start = ((f32[8,264,128]{2,1,0:T(8,128)}), f32[8,264,128]{2,1,0:T(8,128)}, u32[]{:S(2)}, u32[]{:S(2)}) async-start(f32[8,264,128]{2,1,0:T(8,128)} %shard_map.95), calls=%async_computation | async-start | bytes 2162688 | tf_op jit(solution)/shard_map/all_to_all | solution.py:366
  26.9 25.7 %copy-start = (bf16[512,256]{1,0:T(8,128)(2,1)S(1)}, bf16[512,256]{1,0:T(8,128)(2,1)}, u32[]{:S(2)}) copy-start(bf16[512,256]{1,0:T(8,128)(2,1)} %constant.69.clone.lane_tab) | copy-start | bytes 786436
  49.5 3.2 %collective-permute-start.2 = (f32[8,264,128]{2,1,0:T(8,128)}, f32[8,264,128]{2,1,0:T(8,128)S(1)}, u32[]{:S(2)}, u32[]{:S(2)}) collective-permute-start(f32[8,264,128]{2,1,0:T(8,128)} %all-to-all-done.mine), channel_id=1, source_target_pairs={{0,16},{16,0},{32,48},{48,32},{64,80},{80,64},{96,112},{112,96},{1... | collective-permute-start | bytes 3244040 | tf_op jit(solution)/shard_map/ppermute | solution.py:374
  52.6 0.7 copy-start.1
  66.3 1.4 %collective-permute-start.3 = (f32[16,16,128]{2,1,0:T(8,128)S(1)}, f32[16,16,128]{2,1,0:T(8,128)S(1)}, u32[]{:S(2)}, u32[]{:S(2)}) collective-permute-start(f32[16,16,128]{2,1,0:T(8,128)S(1)} %get-tuple-element.13), channel_id=1, source_target_pairs={{0,16},{16,0},{32,48},{48,32},{64,80},{80,64},{96,112},{112,96},{1... | collective-permute-start | bytes 393224 | tf_op jit(solution)/shard_map/ppermute | solution.py:374
  104.3 5.2 %collective-permute-start.4 = (f32[16,16,128]{2,1,0:T(8,128)S(1)}, f32[16,16,128]{2,1,0:T(8,128)S(1)}, u32[]{:S(2)}, u32[]{:S(2)}) collective-permute-start(f32[16,16,128]{2,1,0:T(8,128)S(1)} %all_to_all.22.mine), channel_id=1, source_target_pairs={{0,16},{16,0},{32,48},{48,32},{64,80},{80,64},{96,112},{112,96},{1... | collective-permute-start | bytes 393224 | tf_op jit(solution)/shard_map/ppermute | solution.py:374

commit v5 on v4

--- a/solution.py
+++ b/solution.py
@@ -24,12 +24,15 @@
 UPDATES = STEPS * NEW_COLS
 COLS = WINDOW + UPDATES
 REST = 56
-META = COLS + REST
-PAYLOAD = META + 8
+META = COLS + 32
+PAYLOAD = COLS + REST
+TILE = COLS + NEW_COLS
+META_LANE = 96
+TURN_LANE = 106
+BEHIND = 32
 CHIPS = 8
 CHIP_ROWS = 80
 REST_LANES = 32
-ROLL_AT = 64
 HALF_TILES = 21
 SLABS = 16
 SLAB_USED = 14
@@ -154,8 +157,9 @@
                     continue
                 piece = columns(first, start + LANES - q * REST_LANES)
                 joined = piece if joined is None else jnp.where(lane < q * REST_LANES, joined, piece)
+            if COLS + r * PIX == META:
+                joined = jnp.where(lane < META_LANE, joined, meta[...])
             out[m, COLS + r * PIX : COLS + (r + 1) * PIX, :] = joined
-        out[m, META:PAYLOAD, :] = meta[...]
 
 
 def sincos(x):
@@ -176,54 +180,62 @@
     return sine, cosine
 
 
-def main_kernel(
-    flags, mine, other, lane_tab, recon,
-    keep, send, flat_out,
-    state, phase, sums, numbers, meta, arrived,
-):
+def sum_kernel(core, mine, keep, send, state, numbers, meta, arrived):
     lane = lane_index((40, LANES))
-    side = flags[0]
+    side = core[0]
     for p in range(CHIPS):
-        numbers[p] = mine[p, META:, :].astype(jnp.int32)
-        numbers[CHIPS + p] = other[p, META:, :].astype(jnp.int32)
+        numbers[p] = mine[p, META : META + PIX, :].astype(jnp.int32)
     copy = pltpu.make_async_copy(numbers, meta, arrived)
     copy.start()
-    sums[...] = jnp.zeros_like(sums)
-
-    cut = LANES - 40 * side
-    turn = lax.rem(cut, LANES)
 
     def begin(p, carry):
-        for base, ref in ((0, mine), (CHIPS, other)):
-            for q in range(4):
-                first = q * REST
-                count = min(REST, COLS - first)
-                left = pltpu.roll(ref[p, first : first + count, :], turn, 1)
-                right = pltpu.roll(ref[p, COLS : COLS + count, :], (88 - REST_LANES * q) % LANES, 1)
-                state[base + p, first : first + count, :] = jnp.where(lane_index(left.shape) < cut, left, right)
+        for q in range(4):
+            first = q * REST
+            count = min(REST, COLS - first)
+            near = mine[p, first : first + count, :]
+            left = pltpu.roll(near, LANES - BEHIND, 1)
+            right = pltpu.roll(mine[p, COLS : COLS + count, :], (LANES - BEHIND - REST_LANES * q) % LANES, 1)
+            state[p, first : first + count, :] = near
+            state[p, TILE + first : TILE + first + count, :] = jnp.where(
+                lane_index(left.shape) < LANES - BEHIND, left, right
+            )
         return carry
 
     lax.fori_loop(0, CHIPS, begin, 0)
     copy.wait()
 
-    def cut_and_add(t):
-        for l in range(2 * CHIPS):
-            dst = pl.multiple_of(meta[l, 6, t], NEW_COLS)
+    def step(t, carry):
+        for l in range(CHIPS):
+            dst = pl.multiple_of(meta[l, 6, META_LANE + t], NEW_COLS)
             src = pl.multiple_of(WINDOW + t * NEW_COLS, NEW_COLS)
-            state[l, pl.ds(dst, NEW_COLS), :] = state[l, pl.ds(src, NEW_COLS), :]
+            for base in (0, TILE):
+                state[l, pl.ds(base + dst, NEW_COLS), :] = state[l, pl.ds(base + src, NEW_COLS), :]
         acc = []
         for g in range(STARS):
             total = jnp.zeros((40, LANES), jnp.float32)
-            for l in range(2 * CHIPS):
-                total = total + pltpu.roll(state[l, pl.ds(meta[l, g, t], 40), :], meta[l, g, ROLL_AT + t], 1)
+            for l in range(CHIPS):
+                window = state[l, pl.ds(meta[l, g, META_LANE + t], 40), :]
+                total = total + pltpu.roll(window, meta[l, g, TURN_LANE + t], 1)
             acc.append(total)
-        for k in range(2):
-            one, two, three = acc[3 * k : 3 * k + 3]
-            joined = jnp.where(lane < 40, one, jnp.where(lane < 80, pltpu.roll(two, 40, 1), pltpu.roll(three, 80, 1)))
-            phase[lax.rem(t, 2), k * 40 : (k + 1) * 40, :] = joined
+        for out, block in ((keep, side), (send, 1 - side)):
+            for k in range(2):
+                placed = [
+                    pltpu.roll(acc[3 * k + j], lax.rem(LANES + 40 * j - 40 * block, LANES), 1) for j in range(3)
+                ]
+                joined = jnp.where(lane < 40, placed[0], jnp.where(lane < 80, placed[1], placed[2]))
+                out[t, k * 40 : (k + 1) * 40, :] = joined
+        return carry
+
+    lax.fori_loop(0, STEPS, step, 0)
+
+
+def spot_kernel(flags, here, there, lane_tab, recon, keep, send, flat_out, sums):
+    side = flags[0]
+    sums[...] = jnp.zeros_like(sums)
+    weights = [ahead(d) for d in range(1, 5)]
 
     def spots(t):
-        sine, cosine = sincos(phase[lax.rem(t, 2)])
+        sine, cosine = sincos(here[t] + there[t])
         c1, c2 = parts(cosine, 2)
         s1, s2 = parts(sine, 2)
         head = jnp.concatenate([c1, s1], axis=1)
@@ -250,16 +262,11 @@
             sums[unit, pl.ds(t, 1), :] = z_x[unit : unit + 1]
             sums[10 + unit, pl.ds(t, 1), :] = z_y[unit : unit + 1]
 
-    weights = [ahead(d) for d in range(1, 5)]
-    cut_and_add(0)
-
     def step(t, carry):
-        cut_and_add(t)
-        spots(t - 1)
+        spots(t)
         return carry
 
-    lax.fori_loop(1, STEPS, step, 0)
-    spots(STEPS - 1)
+    lax.fori_loop(0, STEPS, step, 0, unroll=2)
 
     units = 20
     stacked = jnp.concatenate(parts(sums[...].reshape(units * 16, LANES), 3))
@@ -325,23 +332,33 @@
     )(low, core, high, fresh, meta)
 
 
-def slopes_and_products(flags, mine, other, recon):
+def partial_phases(core, mine):
+    half = jax.ShapeDtypeStruct((STEPS, 10 * PIX, LANES), jnp.float32)
+    return pl.pallas_call(
+        sum_kernel,
+        out_shape=(half, half),
+        in_specs=[smem(), vmem()],
+        out_specs=(vmem(), vmem()),
+        scratch_shapes=[
+            pltpu.VMEM((CHIPS, 2 * TILE, LANES), jnp.float32),
+            pltpu.VMEM((CHIPS, PIX, LANES), jnp.int32),
+            pltpu.SMEM((CHIPS, PIX, LANES), jnp.int32),
+            pltpu.SemaphoreType.DMA(()),
+        ],
+        compiler_params=pltpu.CompilerParams(vmem_limit_bytes=16 << 20),
+    )(core, mine)
+
+
+def slopes_and_products(flags, here, there, recon):
     slab = jax.ShapeDtypeStruct((SLABS, SLAB_ROWS, LANES), jnp.float32)
     return pl.pallas_call(
-        main_kernel,
+        spot_kernel,
         out_shape=(slab, slab, jax.ShapeDtypeStruct((16, FLAT_PAD), jnp.float32)),
         in_specs=[smem()] + [vmem()] * 4,
         out_specs=(vmem(),) * 3,
-        scratch_shapes=[
-            pltpu.VMEM((2 * CHIPS, COLS + NEW_COLS, LANES), jnp.float32),
-            pltpu.VMEM((2, 10 * PIX, LANES), jnp.float32),
-            pltpu.VMEM((20, 16, LANES), jnp.float32),
-            pltpu.VMEM((2 * CHIPS, 8, LANES), jnp.int32),
-            pltpu.SMEM((2 * CHIPS, 8, LANES), jnp.int32),
-            pltpu.SemaphoreType.DMA(()),
-        ],
-        compiler_params=pltpu.CompilerParams(vmem_limit_bytes=20 << 20),
-    )(flags, mine, other, jnp.asarray(lane_table()), recon)
+        scratch_shapes=[pltpu.VMEM((20, 16, LANES), jnp.float32)],
+        compiler_params=pltpu.CompilerParams(vmem_limit_bytes=16 << 20),
+    )(flags, here, there, jnp.asarray(lane_table()), recon)
 
 
 def finish(core, mine, other):
@@ -389,14 +406,16 @@
     low = lax.ppermute(strip(jnp.where(owner == count - 1, PUP_TURN - 1, PUP_TURN)), "sub", forward)
     high = lax.ppermute(strip(jnp.where(owner == 0, PUP_TURN + 1, PUP_TURN)), "sub", backward)
 
-    start = jnp.transpose(shift_x[:, 0]) + HALO
-    turn = (LANES - HALO - jnp.transpose(shift_y[:, 0])) % LANES
+    offset = jnp.transpose(shift_y[:, 0]) + HALO
+    behind = (offset > LANES - CHIP_ROWS).astype(jnp.int32)
+    start = jnp.transpose(shift_x[:, 0]) + HALO + behind * TILE
+    turn = (LANES - offset + behind * BEHIND) % LANES
     block = jnp.transpose(col_block) - (PUP_TURN * PUP // NEW_COLS) - (owner * 5 - 5)
     block = jnp.where((block >= 0) & (block < WINDOW // NEW_COLS), block, COLS // NEW_COLS) * NEW_COLS
     meta = (
-        jnp.pad(start, ((0, 2), (0, LANES - STEPS)))
-        + jnp.pad(turn, ((0, 2), (ROLL_AT, LANES - ROLL_AT - STEPS)))
-        + jnp.pad(block, ((6, 1), (0, LANES - STEPS)))
+        jnp.pad(start, ((0, 2), (META_LANE, LANES - META_LANE - STEPS)))
+        + jnp.pad(turn, ((0, 2), (TURN_LANE, LANES - TURN_LANE - STEPS)))
+        + jnp.pad(block, ((6, 1), (META_LANE, LANES - META_LANE - STEPS)))
     ).astype(jnp.float32)
 
     side = (lax.axis_index("layer") % 2).astype(jnp.int32).reshape(1)
@@ -404,9 +423,8 @@
     matrix = jnp.transpose(recon, (0, 2, 3, 1, 4)).reshape(FLAT, ACTS)
     flags = jnp.concatenate([side, valid.reshape(-1)])
     mine, matrix, flags = lax.optimization_barrier((mine, matrix, flags))
-    other = to_other_core(mine)
-
-    keep, send, flat = slopes_and_products(flags, mine, other, matrix)
+    here, there = partial_phases(side, mine)
+    keep, send, flat = slopes_and_products(flags, here, to_other_core(there), matrix)
 
     plane = groups_by(lambda zh, x, c, y, zl: (c, zh, zl))
     column = groups_by(lambda zh, x, c, y, zl: (c, x, y))

time: 111 us -> 107 us (0.964)
  Pallas kernels: 15.7 us -> 13.5 us
  waiting for transfers between devices: 22.8 us -> 21 us
    pallas_call x1 -> x2, Pallas kernels: 13 us -> 10.8 us  [the longest x1 6.91 us: partial_phases(): pl.pallas_call(sum_kernel, out_shape=(half, half), in_specs=[smem(), vmem...]
    ppermute x3, waiting for transfers between devices: 3.65 us -> 2.47 us  [to_other_core(): return lax.ppermute(block, 'layer', [(i, i ^ 1) for i in range(16)])]
where the time goes in v5:
time: 107 us; the launch traced here: 106 us
  blocking collectives  36.4 us (34%)
  starting transfers between devices  21.1 us (20%)
  waiting for transfers between devices  21 us (20%)
  Pallas kernels  13.5 us (13%)
  local copies, waits for them, and re-layouts  10.8 us (10%)
  other arithmetic  2.77 us (3%)
    all_to_all x3, blocking collectives, exchange(): lax.all_to_all(blocks, ('layer', 'sub'), 0, 0, tiled=True, axis_index_gro...  36.4 us
    all_to_all x1, waiting for transfers between devices, exchange(): lax.all_to_all(blocks, ('layer', 'sub'), 0, 0, tiled=True, axis_index_gro...  14.9 us
    all_to_all x1, starting transfers between devices, exchange(): lax.all_to_all(blocks, ('layer', 'sub'), 0, 0, tiled=True, axis_index_gro...  7.95 us
    ppermute x1, starting transfers between devices, local(): lax.ppermute(strip(jnp.where(owner == 0, PUP_TURN + 1, PUP_TURN)), 'sub',...  7.7 us
    pallas_call x1, Pallas kernels, partial_phases(): pl.pallas_call(sum_kernel, out_shape=(half, half), in_specs=[smem(), vmem...  6.91 us
    reshape x1, local copies, waits for them, and re-layouts, local(): matrix = jnp.transpose(recon, (0, 2, 3, 1, 4)).reshape(FLAT, ACTS)  6.37 us
    ppermute x3, starting transfers between devices, to_other_core(): return lax.ppermute(block, 'layer', [(i, i ^ 1) for i in range(16)])  5.45 us
    pallas_call x1, Pallas kernels, slopes_and_products(): pl.pallas_call(spot_kernel, out_shape=(slab, slab, jax.ShapeDtypeStruct((...  3.92 us
  transfers between devices with their start and end apart: 6, of which 5 were waited for; matrix products, arithmetic and copies ran while one was open for 11% of the time, Pallas kernels for 0%

profile of v5, /device:TPU:1, one launch (start us, length us, event | category | flops | bytes accessed | tf_op | source)
XLA Modules:
  0.0 106.4 jit_solution(8884362383596468106)
XLA Ops:
  0.6 1.0 dynamic-slice_bitcast_fusion
  1.6 0.0 copy-start.2
  1.6 7.7 %collective-permute-start.1 = (f32[40,768]{1,0:T(8,128)S(1)}, f32[40,768]{1,0:T(8,128)S(1)}, u32[]{:S(2)}, u32[]{:S(2)}) collective-permute-start(f32[40,768]{1,0:T(8,128)S(1)} %get-tuple-element.18), channel_id=1, source_target_pairs={{1,0},{2,1},{3,2},{4,3},{5,4},{6,5},{7,6},{8,7},{9,8},{10,9},{11,1... | collective-permute-start | bytes 368648 | tf_op jit(solution)/shard_map/ppermute | solution.py:407
  9.3 0.0 collective-permute-start
  9.3 0.7 add_select_fusion
  10.0 0.7 fusion.5
  10.7 0.9 slice_bitcast_fusion.1.core
  11.7 1.0 slice_bitcast_fusion.fresh
  12.6 0.7 fusion.6
  13.3 0.1 add_convert_fusion.meta
  13.4 0.0 collective-permute-done.1.high
  13.4 3.6 %collective-permute-done.low = f32[40,768]{1,0:T(8,128)S(1)} collective-permute-done((f32[40,768]{1,0:T(8,128)S(1)}, f32[40,768]{1,0:T(8,128)S(1)}, u32[]{:S(2)}, u32[]{:S(2)}) %collective-permute-start) | collective-permute-done | bytes 122912 | tf_op jit(solution)/shard_map/ppermute | solution.py:406
  17.0 1.9 %shard_map.95 = f32[8,256,128]{2,1,0:T(8,128)} custom-call(f32[40,768]{1,0:T(8,128)S(1)} %collective-permute-done.low, f32[40,768]{1,0:T(8,128)S(1)} %slice_bitcast_fusion.1.core, f32[40,768]{1,0:T(8,128)S(1)} %collective-permute-done.1.high, f32[80,768]{1,0:T(8,128)S(1)} %slice_bitcast_fusion.fresh, f32[8,128]{1,0:T(8,128)S(1)} %add_convert_fusion.meta), custom_call_target="tpu_custom_call" | custom-call | tf_op jit(solution)/shard_map/pallas_call | solution.py:326
  18.9 7.9 %all-to-all-start = ((f32[8,256,128]{2,1,0:T(8,128)}), f32[8,256,128]{2,1,0:T(8,128)}, u32[]{:S(2)}, u32[]{:S(2)}) async-start(f32[8,256,128]{2,1,0:T(8,128)} %shard_map.95), calls=%async_computation | async-start | bytes 2097152 | tf_op jit(solution)/shard_map/all_to_all | solution.py:383
  26.9 0.0 copy-done.2
  26.9 0.1 reshape.86
  26.9 0.0 copy-start
  26.9 6.4 %reshape.84.recon = bf16[300,5376]{1,0:T(8,128)(2,1)S(1)} reshape(bf16[6,5,5,2,5376]{4,3,2,1,0:T(2,128)(2,1)} %bitcast.41) | data formatting | bytes 6451200 | tf_op jit(solution)/shard_map/reshape | solution.py:423
  33.3 0.6 pad_add_fusion.flags
  33.9 14.9 %all-to-all-done.mine = f32[8,256,128]{2,1,0:T(8,128)} async-done(((f32[8,256,128]{2,1,0:T(8,128)}), f32[8,256,128]{2,1,0:T(8,128)}, u32[]{:S(2)}, u32[]{:S(2)}) %all-to-all-start) | async-done | bytes 1048608 | tf_op jit(solution)/shard_map/all_to_all | solution.py:383
  48.8 6.9 %shard_map.96 = (f32[10,80,128]{2,1,0:T(8,128)S(1)}, f32[10,80,128]{2,1,0:T(8,128)S(1)}) custom-call(s32[1]{0:T(128)} %bitcast.19.core, f32[8,256,128]{2,1,0:T(8,128)} %all-to-all-done.mine), custom_call_target="tpu_custom_call" | custom-call | tf_op jit(solution)/shard_map/pallas_call | solution.py:337
  55.7 0.7 collective-permute-start.2
  56.4 1.4 %collective-permute-done.2.there = f32[10,80,128]{2,1,0:T(8,128)S(1)} collective-permute-done((f32[10,80,128]{2,1,0:T(8,128)S(1)}, f32[10,80,128]{2,1,0:T(8,128)S(1)}, u32[]{:S(2)}, u32[]{:S(2)}) %collective-permute-start.2) | collective-permute-done | bytes 409632 | tf_op jit(solution)/shard_map/ppermute | solution.py:391
  57.8 0.0 copy-done
  57.8 0.0 copy-start.1
  57.8 0.7 copy-done.1
  58.5 3.9 %shard_map.97 = (f32[16,16,128]{2,1,0:T(8,128)S(1)}, f32[16,16,128]{2,1,0:T(8,128)S(1)}, f32[16,384]{1,0:T(8,128)S(1)}) custom-call(s32[26]{0:T(128)S(1)} %copy-done.1, f32[10,80,128]{2,1,0:T(8,128)S(1)} %get-tuple-element.12.here, f32[10,80,128]{2,1,0:T(8,128)S(1)} %collective-permute-done.2.there, bf16[512,256]{1,0:T(8,128)(2,1)S(1)} %copy-done, ...), custom_call_target="tpu_custom_call" | custom-call | tf_op jit(solution)/shard_map/pallas_call | solution.py:354
  62.4 0.5 collective-permute-start.3
  62.8 1.0 collective-permute-done.3
  63.8 13.5 %all_to_all.20 = f32[16,16,128]{2,1,0:T(8,128)S(1)} all-to-all(f32[16,16,128]{2,1,0:T(8,128)S(1)} %add.73), channel_id=1, replica_groups={{0,4,8,12,32,36,40,44,64,68,72,76,96,100,104,108},{1,5,9,13,33,37,41,45..., dimensions={0} | all-to-all | bytes 262144 | tf_op jit(solution)/shard_map/all_to_all | solution.py:383
  77.4 12.8 %all_to_all.21 = f32[8,16,128]{2,1,0:T(8,128)S(1)} all-to-all(f32[8,16,128]{2,1,0:T(8,128)S(1)} %broadcast_in_dim.9), channel_id=1, replica_groups={{0,1,2,3,128,129,130,131},{4,5,6,7,132,133,134,135},{8,9,10,11,136,137,..., dimensions={0} | all-to-all | bytes 131072 | tf_op jit(solution)/shard_map/all_to_all | solution.py:383
  90.1 10.2 %all_to_all.22.mine = f32[16,16,128]{2,1,0:T(8,128)S(1)} all-to-all(f32[16,16,128]{2,1,0:T(8,128)S(1)} %broadcast_in_dim.18), channel_id=1, replica_groups={{0,4,8,12,32,36,40,44,64,68,72,76,96,100,104,108},{1,5,9,13,33,37,41,45..., dimensions={0} | all-to-all | bytes 262144 | tf_op jit(solution)/shard_map/all_to_all | solution.py:383
  100.3 4.3 %collective-permute-start.4 = (f32[16,16,128]{2,1,0:T(8,128)S(1)}, f32[16,16,128]{2,1,0:T(8,128)S(1)}, u32[]{:S(2)}, u32[]{:S(2)}) collective-permute-start(f32[16,16,128]{2,1,0:T(8,128)S(1)} %all_to_all.22.mine), channel_id=1, source_target_pairs={{0,16},{16,0},{32,48},{48,32},{64,80},{80,64},{96,112},{112,96},{1... | collective-permute-start | bytes 393224 | tf_op jit(solution)/shard_map/ppermute | solution.py:391
  104.6 0.1 copy.18
  104.7 0.8 reshape.87
  105.5 0.1 collective-permute-done.4.other
  105.6 0.8 shard_map.98
  (5 shorter events, 0.1 us)
Async XLA Ops:
  1.6 25.2 %copy-start.2 = (s32[5,5]{1,0:T(8,128)S(1)}, s32[5,5]{1,0:T(8,128)}, u32[]{:S(2)}) copy-start(s32[5,5]{1,0:T(8,128)} %param.13) | copy-start | bytes 304
  1.6 11.7 %collective-permute-start.1 = (f32[40,768]{1,0:T(8,128)S(1)}, f32[40,768]{1,0:T(8,128)S(1)}, u32[]{:S(2)}, u32[]{:S(2)}) collective-permute-start(f32[40,768]{1,0:T(8,128)S(1)} %get-tuple-element.18), channel_id=1, source_target_pairs={{1,0},{2,1},{3,2},{4,3},{5,4},{6,5},{7,6},{8,7},{9,8},{10,9},{11,1... | collective-permute-start | bytes 368648 | tf_op jit(solution)/shard_map/ppermute | solution.py:407
  9.3 7.6 %collective-permute-start = (f32[40,768]{1,0:T(8,128)S(1)}, f32[40,768]{1,0:T(8,128)S(1)}, u32[]{:S(2)}, u32[]{:S(2)}) collective-permute-start(f32[40,768]{1,0:T(8,128)S(1)} %get-tuple-element.19), channel_id=1, source_target_pairs={{0,1},{1,2},{2,3},{3,4},{4,5},{5,6},{6,7},{7,8},{8,9},{9,10},{10,1... | collective-permute-start | bytes 368648 | tf_op jit(solution)/shard_map/ppermute | solution.py:406
  18.9 29.9 %all-to-all-start = ((f32[8,256,128]{2,1,0:T(8,128)}), f32[8,256,128]{2,1,0:T(8,128)}, u32[]{:S(2)}, u32[]{:S(2)}) async-start(f32[8,256,128]{2,1,0:T(8,128)} %shard_map.95), calls=%async_computation | async-start | bytes 2097152 | tf_op jit(solution)/shard_map/all_to_all | solution.py:383
  26.9 30.9 %copy-start = (bf16[512,256]{1,0:T(8,128)(2,1)S(1)}, bf16[512,256]{1,0:T(8,128)(2,1)}, u32[]{:S(2)}) copy-start(bf16[512,256]{1,0:T(8,128)(2,1)} %constant.76.clone.lane_tab) | copy-start | bytes 786436
  55.7 2.1 %collective-permute-start.2 = (f32[10,80,128]{2,1,0:T(8,128)S(1)}, f32[10,80,128]{2,1,0:T(8,128)S(1)}, u32[]{:S(2)}, u32[]{:S(2)}) collective-permute-start(f32[10,80,128]{2,1,0:T(8,128)S(1)} %get-tuple-element.13), channel_id=1, source_target_pairs={{0,16},{16,0},{32,48},{48,32},{64,80},{80,64},{96,112},{112,96},{1... | collective-permute-start | bytes 1228808 | tf_op jit(solution)/shard_map/ppermute | solution.py:391
  57.8 0.7 copy-start.1
  62.4 1.4 %collective-permute-start.3 = (f32[16,16,128]{2,1,0:T(8,128)S(1)}, f32[16,16,128]{2,1,0:T(8,128)S(1)}, u32[]{:S(2)}, u32[]{:S(2)}) collective-permute-start(f32[16,16,128]{2,1,0:T(8,128)S(1)} %get-tuple-element.17), channel_id=1, source_target_pairs={{0,16},{16,0},{32,48},{48,32},{64,80},{80,64},{96,112},{112,96},{1... | collective-permute-start | bytes 393224 | tf_op jit(solution)/shard_map/ppermute | solution.py:391
  100.3 5.2 %collective-permute-start.4 = (f32[16,16,128]{2,1,0:T(8,128)S(1)}, f32[16,16,128]{2,1,0:T(8,128)S(1)}, u32[]{:S(2)}, u32[]{:S(2)}) collective-permute-start(f32[16,16,128]{2,1,0:T(8,128)S(1)} %all_to_all.22.mine), channel_id=1, source_target_pairs={{0,16},{16,0},{32,48},{48,32},{64,80},{80,64},{96,112},{112,96},{1... | collective-permute-start | bytes 393224 | tf_op jit(solution)/shard_map/ppermute | solution.py:391

commit v6 on v5

--- a/solution.py
+++ b/solution.py
@@ -23,9 +23,12 @@
 WINDOW = 120
 UPDATES = STEPS * NEW_COLS
 COLS = WINDOW + UPDATES
-REST = 56
-META = COLS + 32
-PAYLOAD = COLS + REST
+REST = 32
+META = WINDOW + 24
+PAYLOAD = WINDOW + REST
+NEW_REST = 24
+NEW_PAYLOAD = UPDATES + NEW_REST
+HALF_LANES = 512
 TILE = COLS + NEW_COLS
 META_LANE = 96
 TURN_LANE = 106
@@ -124,7 +127,7 @@
     return lax.broadcasted_iota(jnp.int32, shape, len(shape) - 1)
 
 
-def pack_kernel(low, core, high, fresh, meta, out):
+def pack_kernel(low, core, high, meta, out):
     def window(ref, first, count, start):
         tile, shift = divmod(start, LANES)
         rows = slice(first, first + count)
@@ -137,7 +140,7 @@
         right = pltpu.roll(ref[rows, (tile + 1) * LANES : (tile + 2) * LANES], LANES - shift, 1)
         return jnp.where(lane_index(left.shape) < LANES - shift, left, right)
 
-    sources = ((low, 0), (core, 40), (high, 80), (fresh, 120))
+    sources = ((low, 0), (core, 40), (high, 80))
 
     def columns(first, start):
         ref, base = [source for source in sources if source[1] <= first][-1]
@@ -147,19 +150,47 @@
     for m in range(CHIPS):
         start = FIRST + m * CHIP_ROWS
         for ref, base in sources:
-            count = UPDATES if base == WINDOW else 40
-            out[m, base : base + count, :] = window(ref, 0, count, start)
+            out[m, base : base + 40, :] = window(ref, 0, 40, start)
         for r in range(REST // PIX):
             joined = None
             for q in range(4):
                 first = q * REST + r * PIX
-                if first >= COLS:
+                if first >= WINDOW:
                     continue
                 piece = columns(first, start + LANES - q * REST_LANES)
                 joined = piece if joined is None else jnp.where(lane < q * REST_LANES, joined, piece)
-            if COLS + r * PIX == META:
+            if WINDOW + r * PIX == META:
                 joined = jnp.where(lane < META_LANE, joined, meta[...])
-            out[m, COLS + r * PIX : COLS + (r + 1) * PIX, :] = joined
+            out[m, WINDOW + r * PIX : WINDOW + (r + 1) * PIX, :] = joined
+
+
+def hand_kernel(place, own, partner, *outs):
+    lane = lane_index((PIX, LANES))
+
+    def window(ref, first, count, start):
+        tile = lax.shift_right_logical(start, 7)
+        cut = LANES - (start & (LANES - 1))
+        turn = cut & (LANES - 1)
+        rows = slice(first, first + count)
+        after = jnp.minimum(tile + 1, HALF_LANES // LANES - 1)
+        left = pltpu.roll(ref[rows, pl.ds(pl.multiple_of(tile * LANES, LANES), LANES)], turn, 1)
+        right = pltpu.roll(ref[rows, pl.ds(pl.multiple_of(after * LANES, LANES), LANES)], turn, 1)
+        return jnp.where(lane_index(left.shape) < cut, left, right)
+
+    for d, out in enumerate(outs):
+        start = FIRST + 64 * place[2] + CHIP_ROWS * ((place[1] + d) & 3)
+        for w, ref in enumerate((own, partner)):
+            base = w * NEW_PAYLOAD
+            out[base : base + UPDATES, :] = window(ref, 0, UPDATES, start)
+            for r in range(NEW_REST // PIX):
+                joined = None
+                for q in range(4):
+                    first = q * NEW_REST + r * PIX
+                    if first >= UPDATES:
+                        continue
+                    piece = window(ref, first, PIX, start + LANES - q * REST_LANES)
+                    joined = piece if joined is None else jnp.where(lane < q * REST_LANES, joined, piece)
+                out[base + UPDATES + r * PIX : base + UPDATES + (r + 1) * PIX, :] = joined
 
 
 def sincos(x):
@@ -180,28 +211,41 @@
     return sine, cosine
 
 
-def sum_kernel(core, mine, keep, send, state, numbers, meta, arrived):
+def sum_kernel(place, mine, new_0, new_1, new_2, new_3, keep, send, state, numbers, meta, arrived):
     lane = lane_index((40, LANES))
-    side = core[0]
+    side = place[0]
     for p in range(CHIPS):
         numbers[p] = mine[p, META : META + PIX, :].astype(jnp.int32)
     copy = pltpu.make_async_copy(numbers, meta, arrived)
     copy.start()
 
+    def unpack(p, target, near, rest, q):
+        count = near.shape[0]
+        left = pltpu.roll(near, LANES - BEHIND, 1)
+        right = pltpu.roll(rest, (LANES - BEHIND - REST_LANES * q) % LANES, 1)
+        state[p, target : target + count, :] = near
+        state[p, TILE + target : TILE + target + count, :] = jnp.where(
+            lane_index(left.shape) < LANES - BEHIND, left, right
+        )
+
     def begin(p, carry):
         for q in range(4):
             first = q * REST
-            count = min(REST, COLS - first)
-            near = mine[p, first : first + count, :]
-            left = pltpu.roll(near, LANES - BEHIND, 1)
-            right = pltpu.roll(mine[p, COLS : COLS + count, :], (LANES - BEHIND - REST_LANES * q) % LANES, 1)
-            state[p, first : first + count, :] = near
-            state[p, TILE + first : TILE + first + count, :] = jnp.where(
-                lane_index(left.shape) < LANES - BEHIND, left, right
-            )
+            count = min(REST, WINDOW - first)
+            unpack(p, first, mine[p, first : first + count, :], mine[p, WINDOW : WINDOW + count, :], q)
         return carry
 
     lax.fori_loop(0, CHIPS, begin, 0)
+    for d, ref in enumerate((new_0, new_1, new_2, new_3)):
+        for w in range(2):
+            half = place[2] if w == 0 else 1 - place[2]
+            p = half * 4 + ((place[1] + 4 - d) & 3)
+            base = w * NEW_PAYLOAD
+            for q in range(4):
+                first = q * NEW_REST
+                count = min(NEW_REST, UPDATES - first)
+                near = ref[base + first : base + first + count, :]
+                unpack(p, WINDOW + first, near, ref[base + UPDATES : base + UPDATES + count, :], q)
     copy.wait()
 
     def step(t, carry):
@@ -322,22 +366,32 @@
     return pl.BlockSpec(memory_space=pltpu.SMEM)
 
 
-def pack(low, core, high, fresh, meta):
+def pack(low, core, high, meta):
     return pl.pallas_call(
         pack_kernel,
         out_shape=jax.ShapeDtypeStruct((CHIPS, PAYLOAD, LANES), jnp.float32),
-        in_specs=[vmem()] * 5,
+        in_specs=[vmem()] * 4,
         out_specs=vmem(),
         compiler_params=pltpu.CompilerParams(vmem_limit_bytes=16 << 20),
-    )(low, core, high, fresh, meta)
-
-
-def partial_phases(core, mine):
+    )(low, core, high, meta)
+
+
+def hand(place, own, partner):
+    return pl.pallas_call(
+        hand_kernel,
+        out_shape=(jax.ShapeDtypeStruct((2 * NEW_PAYLOAD, LANES), jnp.float32),) * 4,
+        in_specs=[smem(), vmem(), vmem()],
+        out_specs=(vmem(),) * 4,
+        compiler_params=pltpu.CompilerParams(vmem_limit_bytes=8 << 20),
+    )(place, own, partner)
+
+
+def partial_phases(place, mine, news):
     half = jax.ShapeDtypeStruct((STEPS, 10 * PIX, LANES), jnp.float32)
     return pl.pallas_call(
         sum_kernel,
         out_shape=(half, half),
-        in_specs=[smem(), vmem()],
+        in_specs=[smem()] + [vmem()] * 5,
         out_specs=(vmem(), vmem()),
         scratch_shapes=[
             pltpu.VMEM((CHIPS, 2 * TILE, LANES), jnp.float32),
@@ -346,7 +400,7 @@
             pltpu.SemaphoreType.DMA(()),
         ],
         compiler_params=pltpu.CompilerParams(vmem_limit_bytes=16 << 20),
-    )(core, mine)
+    )(place, mine, *news)
 
 
 def slopes_and_products(flags, here, there, recon):
@@ -395,7 +449,13 @@
     owner = lax.axis_index("sub")
     count = lax.axis_size("sub")
     strips = jnp.transpose(screens[0], (0, 2, 1))
-    fresh = jnp.transpose(new_columns[:, 0], (0, 2, 1))[:, :, LANE0 : LANE0 + KEPT].reshape(UPDATES, KEPT)
+    fresh = jnp.transpose(new_columns[:, 0], (0, 2, 1))
+    layer = lax.axis_index("layer").astype(jnp.int32)
+    half = layer // 8
+
+    def new_rows(part):
+        at = LANE0 + part * (KEPT - HALF_LANES)
+        return lax.dynamic_slice(fresh, (0, 0, at), (STEPS, NEW_COLS, HALF_LANES)).reshape(UPDATES, HALF_LANES)
 
     def strip(turn):
         return lax.dynamic_slice(strips, (turn, 0, LANE0), (1, 40, KEPT))[0]
@@ -405,6 +465,8 @@
     backward = [(target, source) for source, target in forward]
     low = lax.ppermute(strip(jnp.where(owner == count - 1, PUP_TURN - 1, PUP_TURN)), "sub", forward)
     high = lax.ppermute(strip(jnp.where(owner == 0, PUP_TURN + 1, PUP_TURN)), "sub", backward)
+
+    partner = lax.ppermute(new_rows(1 - half), "layer", [(i, i ^ 8) for i in range(16)])
 
     offset = jnp.transpose(shift_y[:, 0]) + HALO
     behind = (offset > LANES - CHIP_ROWS).astype(jnp.int32)
@@ -418,12 +480,18 @@
         + jnp.pad(block, ((6, 1), (META_LANE, LANES - META_LANE - STEPS)))
     ).astype(jnp.float32)
 
-    side = (lax.axis_index("layer") % 2).astype(jnp.int32).reshape(1)
-    mine = exchange(pack(low, core, high, fresh, meta), groups_by(lambda zh, x, c, y, zl: (c, y, zl)))
+    side = (layer % 2).reshape(1)
+    place = jnp.stack([layer % 2, layer // 2 % 4, half])
+    payload, partner = lax.optimization_barrier((pack(low, core, high, meta), partner))
+    mine = exchange(payload, groups_by(lambda zh, x, c, y, zl: (c, y, zl)))
+    *news, recon = lax.optimization_barrier((*hand(place, new_rows(half), partner), recon))
+    for d in range(1, 4):
+        along = [(i, i // 8 * 8 + (i % 8 + 2 * d) % 8) for i in range(16)]
+        news[d] = lax.ppermute(news[d], "layer", along)
     matrix = jnp.transpose(recon, (0, 2, 3, 1, 4)).reshape(FLAT, ACTS)
     flags = jnp.concatenate([side, valid.reshape(-1)])
     mine, matrix, flags = lax.optimization_barrier((mine, matrix, flags))
-    here, there = partial_phases(side, mine)
+    here, there = partial_phases(place, mine, news)
     keep, send, flat = slopes_and_products(flags, here, to_other_core(there), matrix)
 
     plane = groups_by(lambda zh, x, c, y, zl: (c, zh, zl))

time: 107 us -> 104 us (0.972)
  waiting for transfers between devices: 21 us -> 9.3 us
  starting transfers between devices: 21.1 us -> 29.7 us
  blocking collectives: 36.4 us -> 33.4 us
  local copies, waits for them, and re-layouts: 10.8 us -> 12.4 us
  Pallas kernels: 13.5 us -> 14.6 us
    all_to_all x1, waiting for transfers between devices: 14.9 us -> 0.01 us  [exchange(): lax.all_to_all(blocks, ('layer', 'sub'), 0, 0, tiled=True, axis_index_gro...]
    ppermute x0 -> x4, starting transfers between devices: none -> 9.33 us  [the longest x3 5.03 us: local(): news[d] = lax.ppermute(news[d], 'layer', along)]
    ppermute x0 -> x4, waiting for transfers between devices: none -> 3.8 us  [the longest x1 3.8 us: local(): lax.ppermute(new_rows(1 - half), 'layer', [(i, i ^ 8) for i in range(16)])]
    all_to_all x3, blocking collectives: 36.4 us -> 33.4 us  [exchange(): lax.all_to_all(blocks, ('layer', 'sub'), 0, 0, tiled=True, axis_index_gro...]
    all_to_all x1, starting transfers between devices: 7.95 us -> 5.18 us  [exchange(): lax.all_to_all(blocks, ('layer', 'sub'), 0, 0, tiled=True, axis_index_gro...]
    ppermute x3, starting transfers between devices: 5.45 us -> 7.52 us  [to_other_core(): return lax.ppermute(block, 'layer', [(i, i ^ 1) for i in range(16)])]
    pallas_call x1 -> x2, Pallas kernels: 6.91 us -> 8.45 us  [the longest x1 6.86 us: partial_phases(): pl.pallas_call(sum_kernel, out_shape=(half, half), in_specs=[smem()] + [v...]
    unnamed x6 -> x10, local copies, waits for them, and re-layouts: 0.67 us -> 2.15 us
  transfers between devices with their start and end apart: 6 -> 10, of which waited for: 5 -> 5; matrix products, arithmetic and copies ran while one was open for 11% -> 12% of each run, Pallas kernels for 0% -> 3%
where the time goes in v6:
time: 104 us; the launch traced here: 103 us
  blocking collectives  33.4 us (32%)
  starting transfers between devices  29.7 us (29%)
  Pallas kernels  14.6 us (14%)
  local copies, waits for them, and re-layouts  12.4 us (12%)
  waiting for transfers between devices  9.3 us (9%)
  other arithmetic  2.85 us (3%)
    all_to_all x3, blocking collectives, exchange(): lax.all_to_all(blocks, ('layer', 'sub'), 0, 0, tiled=True, axis_index_gro...  33.4 us
    ppermute x1, starting transfers between devices, local(): lax.ppermute(strip(jnp.where(owner == 0, PUP_TURN + 1, PUP_TURN)), 'sub',...  7.7 us
    ppermute x3, starting transfers between devices, to_other_core(): return lax.ppermute(block, 'layer', [(i, i ^ 1) for i in range(16)])  7.52 us
    pallas_call x1, Pallas kernels, partial_phases(): pl.pallas_call(sum_kernel, out_shape=(half, half), in_specs=[smem()] + [v...  6.86 us
    reshape x1, local copies, waits for them, and re-layouts, local(): matrix = jnp.transpose(recon, (0, 2, 3, 1, 4)).reshape(FLAT, ACTS)  6.37 us
    all_to_all x1, starting transfers between devices, exchange(): lax.all_to_all(blocks, ('layer', 'sub'), 0, 0, tiled=True, axis_index_gro...  5.18 us
    ppermute x3, starting transfers between devices, local(): news[d] = lax.ppermute(news[d], 'layer', along)  5.03 us
    ppermute x1, starting transfers between devices, local(): lax.ppermute(new_rows(1 - half), 'layer', [(i, i ^ 8) for i in range(16)])  4.3 us
  transfers between devices with their start and end apart: 10, of which 5 were waited for; matrix products, arithmetic and copies ran while one was open for 12% of the time, Pallas kernels for 3%

profile of v6, /device:TPU:1, one launch (start us, length us, event | category | flops | bytes accessed | tf_op | source)
XLA Modules:
  0.0 103.0 jit_solution(11672151238470161112)
XLA Ops:
  0.6 0.0 copy-start.4
  0.7 1.0 dynamic-slice_bitcast_fusion.2
  1.6 7.7 %collective-permute-start.1 = (f32[40,768]{1,0:T(8,128)S(1)}, f32[40,768]{1,0:T(8,128)S(1)}, u32[]{:S(2)}, u32[]{:S(2)}) collective-permute-start(f32[40,768]{1,0:T(8,128)S(1)} %get-tuple-element.40), channel_id=1, source_target_pairs={{1,0},{2,1},{3,2},{4,3},{5,4},{6,5},{7,6},{8,7},{9,8},{10,9},{11,1... | collective-permute-start | bytes 368648 | tf_op jit(solution)/shard_map/ppermute | solution.py:467
  9.3 0.0 collective-permute-start
  9.3 1.0 dynamic-slice_bitcast_fusion
  10.4 4.3 %collective-permute-start.2 = (f32[80,512]{1,0:T(8,128)S(1)}, f32[80,512]{1,0:T(8,128)S(1)}, u32[]{:S(2)}, u32[]{:S(2)}) collective-permute-start(f32[80,512]{1,0:T(8,128)S(1)} %get-tuple-element.43), channel_id=1, source_target_pairs={{0,128},{16,144},{32,160},{48,176},{64,192},{80,208},{96,224},{112... | collective-permute-start | bytes 491528 | tf_op jit(solution)/shard_map/ppermute | solution.py:469
  14.7 0.7 add_select_fusion
  15.4 0.7 fusion.5
  16.1 0.9 slice_bitcast_fusion.core
  17.0 0.7 fusion.6
  17.6 0.1 add_convert_fusion.meta
  17.7 0.0 collective-permute-done.1.high
  17.7 3.0 %collective-permute-done.low = f32[40,768]{1,0:T(8,128)S(1)} collective-permute-done((f32[40,768]{1,0:T(8,128)S(1)}, f32[40,768]{1,0:T(8,128)S(1)}, u32[]{:S(2)}, u32[]{:S(2)}) %collective-permute-start) | collective-permute-done | bytes 122912 | tf_op jit(solution)/shard_map/ppermute | solution.py:466
  20.7 1.4 %shard_map.95 = f32[8,152,128]{2,1,0:T(8,128)} custom-call(f32[40,768]{1,0:T(8,128)S(1)} %collective-permute-done.low, f32[40,768]{1,0:T(8,128)S(1)} %slice_bitcast_fusion.core, f32[40,768]{1,0:T(8,128)S(1)} %collective-permute-done.1.high, f32[8,128]{1,0:T(8,128)S(1)} %add_convert_fusion.meta), custom_call_target="tpu_custom_call" | custom-call | tf_op jit(solution)/shard_map/pallas_call | solution.py:370
  22.1 3.8 %collective-permute-done.2.partner = f32[80,512]{1,0:T(8,128)S(1)} collective-permute-done((f32[80,512]{1,0:T(8,128)S(1)}, f32[80,512]{1,0:T(8,128)S(1)}, u32[]{:S(2)}, u32[]{:S(2)}) %collective-permute-start.2) | collective-permute-done | bytes 163872 | tf_op jit(solution)/shard_map/ppermute | solution.py:469
  25.9 5.2 %all-to-all-start = ((f32[8,152,128]{2,1,0:T(8,128)}), f32[8,152,128]{2,1,0:T(8,128)}, u32[]{:S(2)}, u32[]{:S(2)}) async-start(f32[8,152,128]{2,1,0:T(8,128)} %shard_map.95), calls=%async_computation | async-start | bytes 1245184 | tf_op jit(solution)/shard_map/all_to_all | solution.py:437
  31.1 0.0 copy-done.4
  31.1 0.1 reshape.95
  31.2 0.1 pad_add_fusion.place
  31.3 1.6 %shard_map.96 = (f32[208,128]{1,0:T(8,128)S(1)}, f32[208,128]{1,0:T(8,128)}, f32[208,128]{1,0:T(8,128)}, f32[208,128]{1,0:T(8,128)}) custom-call(s32[3]{0:T(128)S(1)} %pad_add_fusion.place, f32[80,512]{1,0:T(8,128)S(1)} %get-tuple-element.42.own, f32[80,512]{1,0:T(8,128)S(1)} %collective-permute-done.2.partner), custom_call_target="tpu_custom_call" | custom-call | tf_op jit(solution)/shard_map/pallas_call | solution.py:380
  32.9 0.6 copy-done.1
  33.5 1.5 %collective-permute-start.3 = (f32[208,128]{1,0:T(8,128)}, f32[208,128]{1,0:T(8,128)}, u32[]{:S(2)}, u32[]{:S(2)}) collective-permute-start(f32[208,128]{1,0:T(8,128)} %get-tuple-element.31), channel_id=1, source_target_pairs={{0,32},{16,48},{32,64},{48,80},{64,96},{80,112},{96,0},{112,16},{1... | collective-permute-start | bytes 319496 | tf_op jit(solution)/shard_map/ppermute | solution.py:490
  35.0 2.4 %collective-permute-start.4 = (f32[208,128]{1,0:T(8,128)}, f32[208,128]{1,0:T(8,128)}, u32[]{:S(2)}, u32[]{:S(2)}) collective-permute-start(f32[208,128]{1,0:T(8,128)} %get-tuple-element.32), channel_id=1, source_target_pairs={{0,64},{16,80},{32,96},{48,112},{64,0},{80,16},{96,32},{112,48},{1... | collective-permute-start | bytes 319496 | tf_op jit(solution)/shard_map/ppermute | solution.py:490
  37.4 1.2 %collective-permute-start.5 = (f32[208,128]{1,0:T(8,128)}, f32[208,128]{1,0:T(8,128)}, u32[]{:S(2)}, u32[]{:S(2)}) collective-permute-start(f32[208,128]{1,0:T(8,128)} %get-tuple-element.33), channel_id=1, source_target_pairs={{0,96},{16,112},{32,0},{48,16},{64,32},{80,48},{96,64},{112,80},{1... | collective-permute-start | bytes 319496 | tf_op jit(solution)/shard_map/ppermute | solution.py:490
  38.5 0.6 pad_add_fusion.1.flags
  39.1 6.4 %reshape.94.recon = bf16[300,5376]{1,0:T(8,128)(2,1)S(1)} reshape(bf16[6,5,5,2,5376]{4,3,2,1,0:T(2,128)(2,1)} %bitcast.50) | data formatting | bytes 6451200 | tf_op jit(solution)/shard_map/reshape | solution.py:491
  45.5 0.0 all-to-all-done.mine
  45.5 0.0 collective-permute-done.3.new_1
  45.5 0.0 collective-permute-done.4.new_2
  45.5 0.0 collective-permute-done.5.new_3
  45.6 0.0 copy-start.2
  45.6 0.9 copy-done.2
  46.5 6.9 %shard_map.97 = (f32[10,80,128]{2,1,0:T(8,128)S(1)}, f32[10,80,128]{2,1,0:T(8,128)S(1)}) custom-call(s32[3]{0:T(128)S(1)} %pad_add_fusion.place, f32[8,152,128]{2,1,0:T(8,128)} %all-to-all-done.mine, f32[208,128]{1,0:T(8,128)S(1)} %copy-done.2, f32[208,128]{1,0:T(8,128)} %collective-permute-done.3.new_1, f32[208,128]{1,0:T(8,128)} %collective-permute-done.4.new_2, ...), custom_call_target="tpu_custom_call" | custom-call | tf_op jit(solution)/shard_map/pallas_call | solution.py:391
  53.3 2.8 %collective-permute-start.6 = (f32[10,80,128]{2,1,0:T(8,128)S(1)}, f32[10,80,128]{2,1,0:T(8,128)S(1)}, u32[]{:S(2)}, u32[]{:S(2)}) collective-permute-start(f32[10,80,128]{2,1,0:T(8,128)S(1)} %get-tuple-element.35), channel_id=1, source_target_pairs={{0,16},{16,0},{32,48},{48,32},{64,80},{80,64},{96,112},{112,96},{1... | collective-permute-start | bytes 1228808 | tf_op jit(solution)/shard_map/ppermute | solution.py:445
  56.1 1.4 %collective-permute-done.6.there = f32[10,80,128]{2,1,0:T(8,128)S(1)} collective-permute-done((f32[10,80,128]{2,1,0:T(8,128)S(1)}, f32[10,80,128]{2,1,0:T(8,128)S(1)}, u32[]{:S(2)}, u32[]{:S(2)}) %collective-permute-start.6) | collective-permute-done | bytes 409632 | tf_op jit(solution)/shard_map/ppermute | solution.py:445
  57.5 0.0 copy-done
  57.5 0.6 copy-done.3
  58.1 3.9 %shard_map.98 = (f32[16,16,128]{2,1,0:T(8,128)S(1)}, f32[16,16,128]{2,1,0:T(8,128)S(1)}, f32[16,384]{1,0:T(8,128)S(1)}) custom-call(s32[26]{0:T(128)S(1)} %copy-done.3, f32[10,80,128]{2,1,0:T(8,128)S(1)} %get-tuple-element.34.here, f32[10,80,128]{2,1,0:T(8,128)S(1)} %collective-permute-done.6.there, bf16[512,256]{1,0:T(8,128)(2,1)S(1)} %copy-done, ...), custom_call_target="tpu_custom_call" | custom-call | tf_op jit(solution)/shard_map/pallas_call | solution.py:408
  62.0 0.5 collective-permute-start.7
  62.5 1.0 collective-permute-done.7
  63.5 9.3 %all_to_all.20 = f32[16,16,128]{2,1,0:T(8,128)S(1)} all-to-all(f32[16,16,128]{2,1,0:T(8,128)S(1)} %add.100), channel_id=1, replica_groups={{0,4,8,12,32,36,40,44,64,68,72,76,96,100,104,108},{1,5,9,13,33,37,41,45..., dimensions={0} | all-to-all | bytes 262144 | tf_op jit(solution)/shard_map/all_to_all | solution.py:437
  72.8 14.0 %all_to_all.21 = f32[8,16,128]{2,1,0:T(8,128)S(1)} all-to-all(f32[8,16,128]{2,1,0:T(8,128)S(1)} %broadcast_in_dim.9), channel_id=1, replica_groups={{0,1,2,3,128,129,130,131},{4,5,6,7,132,133,134,135},{8,9,10,11,136,137,..., dimensions={0} | all-to-all | bytes 131072 | tf_op jit(solution)/shard_map/all_to_all | solution.py:437
  86.8 10.2 %all_to_all.22.mine = f32[16,16,128]{2,1,0:T(8,128)S(1)} all-to-all(f32[16,16,128]{2,1,0:T(8,128)S(1)} %broadcast_in_dim.18), channel_id=1, replica_groups={{0,4,8,12,32,36,40,44,64,68,72,76,96,100,104,108},{1,5,9,13,33,37,41,45..., dimensions={0} | all-to-all | bytes 262144 | tf_op jit(solution)/shard_map/all_to_all | solution.py:437
  97.0 4.3 %collective-permute-start.8 = (f32[16,16,128]{2,1,0:T(8,128)S(1)}, f32[16,16,128]{2,1,0:T(8,128)S(1)}, u32[]{:S(2)}, u32[]{:S(2)}) collective-permute-start(f32[16,16,128]{2,1,0:T(8,128)S(1)} %all_to_all.22.mine), channel_id=1, source_target_pairs={{0,16},{16,0},{32,48},{48,32},{64,80},{80,64},{96,112},{112,96},{1... | collective-permute-start | bytes 393224 | tf_op jit(solution)/shard_map/ppermute | solution.py:445
  101.3 0.1 copy.18
  101.4 0.8 reshape.96
  102.1 0.1 collective-permute-done.8.other
  102.2 0.8 shard_map.99
  (8 shorter events, 0.1 us)
Async XLA Ops:
  0.6 30.5 %copy-start.4 = (s32[5,5]{1,0:T(8,128)S(1)}, s32[5,5]{1,0:T(8,128)}, u32[]{:S(2)}) copy-start(s32[5,5]{1,0:T(8,128)} %param.13) | copy-start | bytes 304
  1.6 16.1 %collective-permute-start.1 = (f32[40,768]{1,0:T(8,128)S(1)}, f32[40,768]{1,0:T(8,128)S(1)}, u32[]{:S(2)}, u32[]{:S(2)}) collective-permute-start(f32[40,768]{1,0:T(8,128)S(1)} %get-tuple-element.40), channel_id=1, source_target_pairs={{1,0},{2,1},{3,2},{4,3},{5,4},{6,5},{7,6},{8,7},{9,8},{10,9},{11,1... | collective-permute-start | bytes 368648 | tf_op jit(solution)/shard_map/ppermute | solution.py:467
  9.3 11.4 %collective-permute-start = (f32[40,768]{1,0:T(8,128)S(1)}, f32[40,768]{1,0:T(8,128)S(1)}, u32[]{:S(2)}, u32[]{:S(2)}) collective-permute-start(f32[40,768]{1,0:T(8,128)S(1)} %get-tuple-element.41), channel_id=1, source_target_pairs={{0,1},{1,2},{2,3},{3,4},{4,5},{5,6},{6,7},{7,8},{8,9},{9,10},{10,1... | collective-permute-start | bytes 368648 | tf_op jit(solution)/shard_map/ppermute | solution.py:466
  10.4 15.6 %collective-permute-start.2 = (f32[80,512]{1,0:T(8,128)S(1)}, f32[80,512]{1,0:T(8,128)S(1)}, u32[]{:S(2)}, u32[]{:S(2)}) collective-permute-start(f32[80,512]{1,0:T(8,128)S(1)} %get-tuple-element.43), channel_id=1, source_target_pairs={{0,128},{16,144},{32,160},{48,176},{64,192},{80,208},{96,224},{112... | collective-permute-start | bytes 491528 | tf_op jit(solution)/shard_map/ppermute | solution.py:469
  25.9 19.6 %all-to-all-start = ((f32[8,152,128]{2,1,0:T(8,128)}), f32[8,152,128]{2,1,0:T(8,128)}, u32[]{:S(2)}, u32[]{:S(2)}) async-start(f32[8,152,128]{2,1,0:T(8,128)} %shard_map.95), calls=%async_computation | async-start | bytes 1245184 | tf_op jit(solution)/shard_map/all_to_all | solution.py:437
  32.9 0.6 copy-start.1
  33.5 12.0 %collective-permute-start.3 = (f32[208,128]{1,0:T(8,128)}, f32[208,128]{1,0:T(8,128)}, u32[]{:S(2)}, u32[]{:S(2)}) collective-permute-start(f32[208,128]{1,0:T(8,128)} %get-tuple-element.31), channel_id=1, source_target_pairs={{0,32},{16,48},{32,64},{48,80},{64,96},{80,112},{96,0},{112,16},{1... | collective-permute-start | bytes 319496 | tf_op jit(solution)/shard_map/ppermute | solution.py:490
  35.0 10.6 %collective-permute-start.4 = (f32[208,128]{1,0:T(8,128)}, f32[208,128]{1,0:T(8,128)}, u32[]{:S(2)}, u32[]{:S(2)}) collective-permute-start(f32[208,128]{1,0:T(8,128)} %get-tuple-element.32), channel_id=1, source_target_pairs={{0,64},{16,80},{32,96},{48,112},{64,0},{80,16},{96,32},{112,48},{1... | collective-permute-start | bytes 319496 | tf_op jit(solution)/shard_map/ppermute | solution.py:490
  37.4 8.2 %collective-permute-start.5 = (f32[208,128]{1,0:T(8,128)}, f32[208,128]{1,0:T(8,128)}, u32[]{:S(2)}, u32[]{:S(2)}) collective-permute-start(f32[208,128]{1,0:T(8,128)} %get-tuple-element.33), channel_id=1, source_target_pairs={{0,96},{16,112},{32,0},{48,16},{64,32},{80,48},{96,64},{112,80},{1... | collective-permute-start | bytes 319496 | tf_op jit(solution)/shard_map/ppermute | solution.py:490
  39.1 18.4 %copy-start = (bf16[512,256]{1,0:T(8,128)(2,1)S(1)}, bf16[512,256]{1,0:T(8,128)(2,1)}, u32[]{:S(2)}) copy-start(bf16[512,256]{1,0:T(8,128)(2,1)} %constant.115.clone.lane_tab) | copy-start | bytes 786436
  45.6 0.9 copy-start.2
  53.3 4.2 %collective-permute-start.6 = (f32[10,80,128]{2,1,0:T(8,128)S(1)}, f32[10,80,128]{2,1,0:T(8,128)S(1)}, u32[]{:S(2)}, u32[]{:S(2)}) collective-permute-start(f32[10,80,128]{2,1,0:T(8,128)S(1)} %get-tuple-element.35), channel_id=1, source_target_pairs={{0,16},{16,0},{32,48},{48,32},{64,80},{80,64},{96,112},{112,96},{1... | collective-permute-start | bytes 1228808 | tf_op jit(solution)/shard_map/ppermute | solution.py:445
  57.5 0.6 copy-start.3
  62.0 1.4 %collective-permute-start.7 = (f32[16,16,128]{2,1,0:T(8,128)S(1)}, f32[16,16,128]{2,1,0:T(8,128)S(1)}, u32[]{:S(2)}, u32[]{:S(2)}) collective-permute-start(f32[16,16,128]{2,1,0:T(8,128)S(1)} %get-tuple-element.39), channel_id=1, source_target_pairs={{0,16},{16,0},{32,48},{48,32},{64,80},{80,64},{96,112},{112,96},{1... | collective-permute-start | bytes 393224 | tf_op jit(solution)/shard_map/ppermute | solution.py:445
  97.0 5.2 %collective-permute-start.8 = (f32[16,16,128]{2,1,0:T(8,128)S(1)}, f32[16,16,128]{2,1,0:T(8,128)S(1)}, u32[]{:S(2)}, u32[]{:S(2)}) collective-permute-start(f32[16,16,128]{2,1,0:T(8,128)S(1)} %all_to_all.22.mine), channel_id=1, source_target_pairs={{0,16},{16,0},{32,48},{48,32},{64,80},{80,64},{96,112},{112,96},{1... | collective-permute-start | bytes 393224 | tf_op jit(solution)/shard_map/ppermute | solution.py:445

commit v7 on v6

--- a/solution.py
+++ b/solution.py
@@ -70,18 +70,19 @@
 
 def lane_table():
     t = toeplitz()
-    table = np.zeros((2 * LANES, 2 * LANES))
-    y = np.arange(PIX)
-    sign = (-1.0) ** (y[:, None] - y[None, :])
-    for group in range(WINDOW // PIX):
-        rows = slice(group * PIX, (group + 1) * PIX)
-        after = slice(LANES + group * PIX, LANES + (group + 1) * PIX)
-        table[rows, rows] = 4.0 * t.T
-        table[after, rows] = -8.0 * sign
-        table[rows, after] = -8.0 * sign
-    first = table.astype(jnp.bfloat16)
-    second = (table - first.astype(np.float64)).astype(jnp.bfloat16)
-    return np.concatenate([first, second])
+    row = lax.broadcasted_iota(jnp.int32, (LANES, LANES), 0)
+    column = lax.broadcasted_iota(jnp.int32, (LANES, LANES), 1)
+    same = (lax.shift_right_logical(row, 3) == lax.shift_right_logical(column, 3)) & (row < WINDOW)
+    ahead_by = jnp.where(same, column - row, LANES)
+    value = jnp.zeros((LANES, LANES), jnp.float32)
+    for d in range(1, PIX):
+        for step in (d, -d):
+            value = jnp.where(ahead_by == step, jnp.float32(4.0 * t[max(step, 0), max(-step, 0)]), value)
+    sign = jnp.where(same, jnp.where((ahead_by & 1) == 0, -8.0, 8.0), 0.0).astype(jnp.bfloat16)
+    main, rest = parts(value, 2)
+    left = jnp.concatenate([main, sign], axis=0)
+    right = jnp.concatenate([sign, jnp.zeros_like(sign)], axis=0)
+    return jnp.concatenate([left, right], axis=1), rest
 
 
 def group_table():
@@ -273,10 +274,11 @@
     lax.fori_loop(0, STEPS, step, 0)
 
 
-def spot_kernel(flags, here, there, lane_tab, recon, keep, send, flat_out, sums):
+def spot_kernel(flags, here, there, recon, keep, send, flat_out, sums, lane_tab, lane_rest):
     side = flags[0]
     sums[...] = jnp.zeros_like(sums)
     weights = [ahead(d) for d in range(1, 5)]
+    lane_tab[...], lane_rest[...] = lane_table()
 
     def spots(t):
         sine, cosine = sincos(here[t] + there[t])
@@ -284,10 +286,10 @@
         s1, s2 = parts(sine, 2)
         head = jnp.concatenate([c1, s1], axis=1)
         tail = jnp.concatenate([c2, s2], axis=1)
-        first = jnp.dot(jnp.concatenate([head, tail]), lane_tab[: 2 * LANES], preferred_element_type=jnp.float32)
-        second = jnp.dot(head, lane_tab[2 * LANES :], preferred_element_type=jnp.float32)
-        along = first[:80] + first[80:] + second
-        z_y = sine * along[:, :LANES] + cosine * along[:, LANES:]
+        first = jnp.dot(jnp.concatenate([head, tail]), lane_tab[...], preferred_element_type=jnp.float32)
+        second = jnp.dot(c1, lane_rest[...], preferred_element_type=jnp.float32)
+        along = first[:80] + first[80:]
+        z_y = sine * (along[:, :LANES] + second) + cosine * along[:, LANES:]
 
         c3 = cosine.reshape(10, PIX, LANES)
         s3 = sine.reshape(10, PIX, LANES)
@@ -408,11 +410,15 @@
     return pl.pallas_call(
         spot_kernel,
         out_shape=(slab, slab, jax.ShapeDtypeStruct((16, FLAT_PAD), jnp.float32)),
-        in_specs=[smem()] + [vmem()] * 4,
+        in_specs=[smem()] + [vmem()] * 3,
         out_specs=(vmem(),) * 3,
-        scratch_shapes=[pltpu.VMEM((20, 16, LANES), jnp.float32)],
+        scratch_shapes=[
+            pltpu.VMEM((20, 16, LANES), jnp.float32),
+            pltpu.VMEM((2 * LANES, 2 * LANES), jnp.bfloat16),
+            pltpu.VMEM((LANES, LANES), jnp.bfloat16),
+        ],
         compiler_params=pltpu.CompilerParams(vmem_limit_bytes=16 << 20),
-    )(flags, here, there, jnp.asarray(lane_table()), recon)
+    )(flags, here, there, recon)
 
 
 def finish(core, mine, other):
@@ -482,9 +488,10 @@
 
     side = (layer % 2).reshape(1)
     place = jnp.stack([layer % 2, layer // 2 % 4, half])
-    payload, partner = lax.optimization_barrier((pack(low, core, high, meta), partner))
+    payload = pack(low, core, high, meta)
+    _, later = lax.optimization_barrier((payload, place))
     mine = exchange(payload, groups_by(lambda zh, x, c, y, zl: (c, y, zl)))
-    *news, recon = lax.optimization_barrier((*hand(place, new_rows(half), partner), recon))
+    news = list(hand(later, new_rows(half), partner))
     for d in range(1, 4):
         along = [(i, i // 8 * 8 + (i % 8 + 2 * d) % 8) for i in range(16)]
         news[d] = lax.ppermute(news[d], "layer", along)

time: 104 us -> 114 us (1.096)
  waiting for transfers between devices: 9.3 us -> 16.8 us
  blocking collectives: 33.4 us -> 36.6 us
  starting transfers between devices: 29.7 us -> 32.5 us
  local copies, waits for them, and re-layouts: 12.4 us -> 9.94 us
    ppermute x3, waiting for transfers between devices: 0.01 us -> 3.97 us  [local(): news[d] = lax.ppermute(news[d], 'layer', along)]
    all_to_all x3, blocking collectives: 33.4 us -> 36.6 us  [exchange(): lax.all_to_all(blocks, ('layer', 'sub'), 0, 0, tiled=True, axis_index_gro...]
    all_to_all x1, starting transfers between devices: 5.18 us -> 7.95 us  [exchange(): lax.all_to_all(blocks, ('layer', 'sub'), 0, 0, tiled=True, axis_index_gro...]
    unnamed x10 -> x4, local copies, waits for them, and re-layouts: 2.15 us -> 0.01 us
    ppermute x1, waiting for transfers between devices: 3.8 us -> 5.8 us  [local(): lax.ppermute(new_rows(1 - half), 'layer', [(i, i ^ 8) for i in range(16)])]
    ppermute x1, waiting for transfers between devices: 3.02 us -> 4.58 us  [local(): lax.ppermute(strip(jnp.where(owner == count - 1, PUP_TURN - 1, PUP_TURN))...]
    ppermute x3, starting transfers between devices: 7.52 us -> 6.24 us  [to_other_core(): return lax.ppermute(block, 'layer', [(i, i ^ 1) for i in range(16)])]
  transfers between devices with their start and end apart: 10 -> 10, of which waited for: 5 -> 7; matrix products, arithmetic and copies ran while one was open for 12% -> 10% of each run, Pallas kernels for 3% -> 2%
where the time goes in v7:
time: 114 us
  blocking collectives  36.6 us (32%)
  starting transfers between devices  32.5 us (29%)
  waiting for transfers between devices  16.8 us (15%)
  Pallas kernels  14.9 us (13%)
  local copies, waits for them, and re-layouts  9.94 us (9%)
  other arithmetic  2.34 us (2%)
    all_to_all x3, blocking collectives, exchange(): lax.all_to_all(blocks, ('layer', 'sub'), 0, 0, tiled=True, axis_index_gro...  36.6 us
    all_to_all x1, starting transfers between devices, exchange(): lax.all_to_all(blocks, ('layer', 'sub'), 0, 0, tiled=True, axis_index_gro...  7.95 us
    ppermute x1, starting transfers between devices, local(): lax.ppermute(strip(jnp.where(owner == 0, PUP_TURN + 1, PUP_TURN)), 'sub',...  7.7 us
    pallas_call x1, Pallas kernels, partial_phases(): pl.pallas_call(sum_kernel, out_shape=(half, half), in_specs=[smem()] + [v...  6.83 us
    reshape x1, local copies, waits for them, and re-layouts, local(): matrix = jnp.transpose(recon, (0, 2, 3, 1, 4)).reshape(FLAT, ACTS)  6.33 us
    ppermute x3, starting transfers between devices, to_other_core(): return lax.ppermute(block, 'layer', [(i, i ^ 1) for i in range(16)])  6.24 us
    ppermute x1, waiting for transfers between devices, local(): lax.ppermute(new_rows(1 - half), 'layer', [(i, i ^ 8) for i in range(16)])  5.8 us
    ppermute x1, starting transfers between devices, local(): lax.ppermute(new_rows(1 - half), 'layer', [(i, i ^ 8) for i in range(16)])  5.36 us
  transfers between devices with their start and end apart: 10, of which 7 were waited for; matrix products, arithmetic and copies ran while one was open for 10% of the time, Pallas kernels for 2%

profile of v7, /device:TPU:1, one launch (start us, length us, event | category | flops | bytes accessed | tf_op | source)
XLA Modules:
  0.0 113.9 jit_solution(9733801659069431779)
XLA Ops:
  0.6 0.0 copy-start
  0.6 0.0 copy-start.1
  0.7 1.0 dynamic-slice_bitcast_fusion.2
  1.7 7.7 %collective-permute-start.1 = (f32[40,768]{1,0:T(8,128)S(1)}, f32[40,768]{1,0:T(8,128)S(1)}, u32[]{:S(2)}, u32[]{:S(2)}) collective-permute-start(f32[40,768]{1,0:T(8,128)S(1)} %get-tuple-element.28), channel_id=1, source_target_pairs={{1,0},{2,1},{3,2},{4,3},{5,4},{6,5},{7,6},{8,7},{9,8},{10,9},{11,1... | collective-permute-start | bytes 368648 | tf_op jit(solution)/shard_map/ppermute | solution.py:473
  9.4 0.0 collective-permute-start
  9.4 0.7 add_select_fusion
  10.1 0.7 fusion.5
  10.8 0.9 slice_bitcast_fusion.core
  11.7 0.7 fusion.6
  12.4 0.1 add_convert_fusion.meta
  12.5 0.0 collective-permute-done.1.high
  12.5 4.6 %collective-permute-done.low = f32[40,768]{1,0:T(8,128)S(1)} collective-permute-done((f32[40,768]{1,0:T(8,128)S(1)}, f32[40,768]{1,0:T(8,128)S(1)}, u32[]{:S(2)}, u32[]{:S(2)}) %collective-permute-start) | collective-permute-done | bytes 122912 | tf_op jit(solution)/shard_map/ppermute | solution.py:472
  17.0 1.4 %shard_map.86 = f32[8,152,128]{2,1,0:T(8,128)} custom-call(f32[40,768]{1,0:T(8,128)S(1)} %collective-permute-done.low, f32[40,768]{1,0:T(8,128)S(1)} %slice_bitcast_fusion.core, f32[40,768]{1,0:T(8,128)S(1)} %collective-permute-done.1.high, f32[8,128]{1,0:T(8,128)S(1)} %add_convert_fusion.meta), custom_call_target="tpu_custom_call" | custom-call | tf_op jit(solution)/shard_map/pallas_call | solution.py:372
  18.4 7.9 %all-to-all-start = ((f32[8,152,128]{2,1,0:T(8,128)}), f32[8,152,128]{2,1,0:T(8,128)}, u32[]{:S(2)}, u32[]{:S(2)}) async-start(f32[8,152,128]{2,1,0:T(8,128)} %shard_map.86), calls=%async_computation | async-start | bytes 1245184 | tf_op jit(solution)/shard_map/all_to_all | solution.py:443
  26.4 0.0 copy-done
  26.4 0.7 dynamic-slice_bitcast_fusion
  27.1 5.4 %collective-permute-start.2 = (f32[80,512]{1,0:T(8,128)}, f32[80,512]{1,0:T(8,128)}, u32[]{:S(2)}, u32[]{:S(2)}) collective-permute-start(f32[80,512]{1,0:T(8,128)} %get-tuple-element.30), channel_id=1, source_target_pairs={{0,128},{16,144},{32,160},{48,176},{64,192},{80,208},{96,224},{112... | collective-permute-start | bytes 491528 | tf_op jit(solution)/shard_map/ppermute | solution.py:475
  32.5 0.0 copy-done.1
  32.5 0.1 reshape.94
  32.5 6.3 %reshape.92.recon = bf16[300,5376]{1,0:T(8,128)(2,1)S(1)} reshape(bf16[6,5,5,2,5376]{4,3,2,1,0:T(2,128)(2,1)} %bitcast.50) | data formatting | bytes 6451200 | tf_op jit(solution)/shard_map/reshape | solution.py:498
  38.9 0.1 pad_add_fusion.1.place
  39.0 5.8 %collective-permute-done.2.partner = f32[80,512]{1,0:T(8,128)} collective-permute-done((f32[80,512]{1,0:T(8,128)}, f32[80,512]{1,0:T(8,128)}, u32[]{:S(2)}, u32[]{:S(2)}) %collective-permute-start.2) | collective-permute-done | bytes 163872 | tf_op jit(solution)/shard_map/ppermute | solution.py:475
  44.8 2.0 %shard_map.87 = (f32[208,128]{1,0:T(8,128)S(1)}, f32[208,128]{1,0:T(8,128)}, f32[208,128]{1,0:T(8,128)}, f32[208,128]{1,0:T(8,128)}) custom-call(s32[3]{0:T(128)S(1)} %pad_add_fusion.1.place, f32[80,512]{1,0:T(8,128)S(1)} %get-tuple-element.31.own, f32[80,512]{1,0:T(8,128)} %collective-permute-done.2.partner), custom_call_target="tpu_custom_call" | custom-call | tf_op jit(solution)/shard_map/pallas_call | solution.py:382
  46.7 1.6 %collective-permute-start.3 = (f32[208,128]{1,0:T(8,128)}, f32[208,128]{1,0:T(8,128)S(1)}, u32[]{:S(2)}, u32[]{:S(2)}) collective-permute-start(f32[208,128]{1,0:T(8,128)} %get-tuple-element.19), channel_id=1, source_target_pairs={{0,32},{16,48},{32,64},{48,80},{64,96},{80,112},{96,0},{112,16},{1... | collective-permute-start | bytes 319496 | tf_op jit(solution)/shard_map/ppermute | solution.py:497
  48.4 2.4 %collective-permute-start.4 = (f32[208,128]{1,0:T(8,128)}, f32[208,128]{1,0:T(8,128)}, u32[]{:S(2)}, u32[]{:S(2)}) collective-permute-start(f32[208,128]{1,0:T(8,128)} %get-tuple-element.20), channel_id=1, source_target_pairs={{0,64},{16,80},{32,96},{48,112},{64,0},{80,16},{96,32},{112,48},{1... | collective-permute-start | bytes 319496 | tf_op jit(solution)/shard_map/ppermute | solution.py:497
  50.8 1.2 %collective-permute-start.5 = (f32[208,128]{1,0:T(8,128)}, f32[208,128]{1,0:T(8,128)}, u32[]{:S(2)}, u32[]{:S(2)}) collective-permute-start(f32[208,128]{1,0:T(8,128)} %get-tuple-element.21), channel_id=1, source_target_pairs={{0,96},{16,112},{32,0},{48,16},{64,32},{80,48},{96,64},{112,80},{1... | collective-permute-start | bytes 319496 | tf_op jit(solution)/shard_map/ppermute | solution.py:497
  52.0 0.1 pad_add_fusion.flags
  52.1 0.0 all-to-all-done.mine
  52.1 0.0 collective-permute-done.3.new_1
  52.1 2.9 %collective-permute-done.4.new_2 = f32[208,128]{1,0:T(8,128)} collective-permute-done((f32[208,128]{1,0:T(8,128)}, f32[208,128]{1,0:T(8,128)}, u32[]{:S(2)}, u32[]{:S(2)}) %collective-permute-start.4) | collective-permute-done | bytes 106528 | tf_op jit(solution)/shard_map/ppermute | solution.py:497
  55.0 1.0 collective-permute-done.5.new_3
  56.1 6.8 %shard_map.88 = (f32[10,80,128]{2,1,0:T(8,128)S(1)}, f32[10,80,128]{2,1,0:T(8,128)S(1)}) custom-call(s32[3]{0:T(128)S(1)} %pad_add_fusion.1.place, f32[8,152,128]{2,1,0:T(8,128)} %all-to-all-done.mine, f32[208,128]{1,0:T(8,128)S(1)} %get-tuple-element.18.new_0, f32[208,128]{1,0:T(8,128)S(1)} %collective-permute-done.3.new_1, ...), custom_call_target="tpu_custom_call" | custom-call | tf_op jit(solution)/shard_map/pallas_call | solution.py:393
  62.9 1.5 %collective-permute-start.6 = (f32[10,80,128]{2,1,0:T(8,128)S(1)}, f32[10,80,128]{2,1,0:T(8,128)S(1)}, u32[]{:S(2)}, u32[]{:S(2)}) collective-permute-start(f32[10,80,128]{2,1,0:T(8,128)S(1)} %get-tuple-element.23), channel_id=1, source_target_pairs={{0,16},{16,0},{32,48},{48,32},{64,80},{80,64},{96,112},{112,96},{1... | collective-permute-start | bytes 1228808 | tf_op jit(solution)/shard_map/ppermute | solution.py:451
  64.4 1.4 %collective-permute-done.6.there = f32[10,80,128]{2,1,0:T(8,128)S(1)} collective-permute-done((f32[10,80,128]{2,1,0:T(8,128)S(1)}, f32[10,80,128]{2,1,0:T(8,128)S(1)}, u32[]{:S(2)}, u32[]{:S(2)}) %collective-permute-start.6) | collective-permute-done | bytes 409632 | tf_op jit(solution)/shard_map/ppermute | solution.py:451
  65.8 3.9 %shard_map.89 = (f32[16,16,128]{2,1,0:T(8,128)S(1)}, f32[16,16,128]{2,1,0:T(8,128)S(1)}, f32[16,384]{1,0:T(8,128)S(1)}) custom-call(s32[26]{0:T(128)S(1)} %pad_add_fusion.flags, f32[10,80,128]{2,1,0:T(8,128)S(1)} %get-tuple-element.22.here, f32[10,80,128]{2,1,0:T(8,128)S(1)} %collective-permute-done.6.there, bf16[300,5376]{1,0:T(8,128)(2,1)S(1)} %reshape.92.recon), custom_call_target="tpu_custom_call" | custom-call | tf_op jit(solution)/shard_map/pallas_call | solution.py:410
  69.7 0.5 collective-permute-start.7
  70.2 1.0 collective-permute-done.7
  71.2 14.1 %all_to_all.20 = f32[16,16,128]{2,1,0:T(8,128)S(1)} all-to-all(f32[16,16,128]{2,1,0:T(8,128)S(1)} %add.100), channel_id=1, replica_groups={{0,4,8,12,32,36,40,44,64,68,72,76,96,100,104,108},{1,5,9,13,33,37,41,45..., dimensions={0} | all-to-all | bytes 262144 | tf_op jit(solution)/shard_map/all_to_all | solution.py:443
  85.3 12.3 %all_to_all.21 = f32[8,16,128]{2,1,0:T(8,128)S(1)} all-to-all(f32[8,16,128]{2,1,0:T(8,128)S(1)} %broadcast_in_dim.9), channel_id=1, replica_groups={{0,1,2,3,128,129,130,131},{4,5,6,7,132,133,134,135},{8,9,10,11,136,137,..., dimensions={0} | all-to-all | bytes 131072 | tf_op jit(solution)/shard_map/all_to_all | solution.py:443
  97.7 10.2 %all_to_all.22.mine = f32[16,16,128]{2,1,0:T(8,128)S(1)} all-to-all(f32[16,16,128]{2,1,0:T(8,128)S(1)} %broadcast_in_dim.18), channel_id=1, replica_groups={{0,4,8,12,32,36,40,44,64,68,72,76,96,100,104,108},{1,5,9,13,33,37,41,45..., dimensions={0} | all-to-all | bytes 262144 | tf_op jit(solution)/shard_map/all_to_all | solution.py:443
  107.9 4.3 %collective-permute-start.8 = (f32[16,16,128]{2,1,0:T(8,128)S(1)}, f32[16,16,128]{2,1,0:T(8,128)S(1)}, u32[]{:S(2)}, u32[]{:S(2)}) collective-permute-start(f32[16,16,128]{2,1,0:T(8,128)S(1)} %all_to_all.22.mine), channel_id=1, source_target_pairs={{0,16},{16,0},{32,48},{48,32},{64,80},{80,64},{96,112},{112,96},{1... | collective-permute-start | bytes 393224 | tf_op jit(solution)/shard_map/ppermute | solution.py:451
  112.1 0.1 copy.17
  112.2 0.8 reshape.99
  113.0 0.1 collective-permute-done.8.other
  113.1 0.8 shard_map.90
  (5 shorter events, 0.1 us)
Async XLA Ops:
  0.6 25.8 %copy-start = (f32[10,1,2048,8]{2,3,1,0:T(8,128)S(1)}, f32[10,1,2048,8]{2,3,1,0:T(8,128)}, u32[]{:S(2)}) copy-start(f32[10,1,2048,8]{2,3,1,0:T(8,128)} %param.8) | copy-start | bytes 1966084
  0.6 31.8 %copy-start.1 = (s32[5,5]{1,0:T(8,128)S(1)}, s32[5,5]{1,0:T(8,128)}, u32[]{:S(2)}) copy-start(s32[5,5]{1,0:T(8,128)} %param.12) | copy-start | bytes 304
  1.7 10.8 %collective-permute-start.1 = (f32[40,768]{1,0:T(8,128)S(1)}, f32[40,768]{1,0:T(8,128)S(1)}, u32[]{:S(2)}, u32[]{:S(2)}) collective-permute-start(f32[40,768]{1,0:T(8,128)S(1)} %get-tuple-element.28), channel_id=1, source_target_pairs={{1,0},{2,1},{3,2},{4,3},{5,4},{6,5},{7,6},{8,7},{9,8},{10,9},{11,1... | collective-permute-start | bytes 368648 | tf_op jit(solution)/shard_map/ppermute | solution.py:473
  9.4 7.6 %collective-permute-start = (f32[40,768]{1,0:T(8,128)S(1)}, f32[40,768]{1,0:T(8,128)S(1)}, u32[]{:S(2)}, u32[]{:S(2)}) collective-permute-start(f32[40,768]{1,0:T(8,128)S(1)} %get-tuple-element.29), channel_id=1, source_target_pairs={{0,1},{1,2},{2,3},{3,4},{4,5},{5,6},{6,7},{7,8},{8,9},{9,10},{10,1... | collective-permute-start | bytes 368648 | tf_op jit(solution)/shard_map/ppermute | solution.py:472
  18.4 33.6 %all-to-all-start = ((f32[8,152,128]{2,1,0:T(8,128)}), f32[8,152,128]{2,1,0:T(8,128)}, u32[]{:S(2)}, u32[]{:S(2)}) async-start(f32[8,152,128]{2,1,0:T(8,128)} %shard_map.86), calls=%async_computation | async-start | bytes 1245184 | tf_op jit(solution)/shard_map/all_to_all | solution.py:443
  27.1 17.7 %collective-permute-start.2 = (f32[80,512]{1,0:T(8,128)}, f32[80,512]{1,0:T(8,128)}, u32[]{:S(2)}, u32[]{:S(2)}) collective-permute-start(f32[80,512]{1,0:T(8,128)} %get-tuple-element.30), channel_id=1, source_target_pairs={{0,128},{16,144},{32,160},{48,176},{64,192},{80,208},{96,224},{112... | collective-permute-start | bytes 491528 | tf_op jit(solution)/shard_map/ppermute | solution.py:475
  46.7 5.4 %collective-permute-start.3 = (f32[208,128]{1,0:T(8,128)}, f32[208,128]{1,0:T(8,128)S(1)}, u32[]{:S(2)}, u32[]{:S(2)}) collective-permute-start(f32[208,128]{1,0:T(8,128)} %get-tuple-element.19), channel_id=1, source_target_pairs={{0,32},{16,48},{32,64},{48,80},{64,96},{80,112},{96,0},{112,16},{1... | collective-permute-start | bytes 319496 | tf_op jit(solution)/shard_map/ppermute | solution.py:497
  48.4 6.7 %collective-permute-start.4 = (f32[208,128]{1,0:T(8,128)}, f32[208,128]{1,0:T(8,128)}, u32[]{:S(2)}, u32[]{:S(2)}) collective-permute-start(f32[208,128]{1,0:T(8,128)} %get-tuple-element.20), channel_id=1, source_target_pairs={{0,64},{16,80},{32,96},{48,112},{64,0},{80,16},{96,32},{112,48},{1... | collective-permute-start | bytes 319496 | tf_op jit(solution)/shard_map/ppermute | solution.py:497
  50.8 5.3 %collective-permute-start.5 = (f32[208,128]{1,0:T(8,128)}, f32[208,128]{1,0:T(8,128)}, u32[]{:S(2)}, u32[]{:S(2)}) collective-permute-start(f32[208,128]{1,0:T(8,128)} %get-tuple-element.21), channel_id=1, source_target_pairs={{0,96},{16,112},{32,0},{48,16},{64,32},{80,48},{96,64},{112,80},{1... | collective-permute-start | bytes 319496 | tf_op jit(solution)/shard_map/ppermute | solution.py:497
  62.9 2.9 %collective-permute-start.6 = (f32[10,80,128]{2,1,0:T(8,128)S(1)}, f32[10,80,128]{2,1,0:T(8,128)S(1)}, u32[]{:S(2)}, u32[]{:S(2)}) collective-permute-start(f32[10,80,128]{2,1,0:T(8,128)S(1)} %get-tuple-element.23), channel_id=1, source_target_pairs={{0,16},{16,0},{32,48},{48,32},{64,80},{80,64},{96,112},{112,96},{1... | collective-permute-start | bytes 1228808 | tf_op jit(solution)/shard_map/ppermute | solution.py:451
  69.7 1.4 %collective-permute-start.7 = (f32[16,16,128]{2,1,0:T(8,128)S(1)}, f32[16,16,128]{2,1,0:T(8,128)S(1)}, u32[]{:S(2)}, u32[]{:S(2)}) collective-permute-start(f32[16,16,128]{2,1,0:T(8,128)S(1)} %get-tuple-element.27), channel_id=1, source_target_pairs={{0,16},{16,0},{32,48},{48,32},{64,80},{80,64},{96,112},{112,96},{1... | collective-permute-start | bytes 393224 | tf_op jit(solution)/shard_map/ppermute | solution.py:451
  107.9 5.2 %collective-permute-start.8 = (f32[16,16,128]{2,1,0:T(8,128)S(1)}, f32[16,16,128]{2,1,0:T(8,128)S(1)}, u32[]{:S(2)}, u32[]{:S(2)}) collective-permute-start(f32[16,16,128]{2,1,0:T(8,128)S(1)} %all_to_all.22.mine), channel_id=1, source_target_pairs={{0,16},{16,0},{32,48},{48,32},{64,80},{80,64},{96,112},{112,96},{1... | collective-permute-start | bytes 393224 | tf_op jit(solution)/shard_map/ppermute | solution.py:451

commit v8 on v7

--- a/solution.py
+++ b/solution.py
@@ -165,7 +165,9 @@
             out[m, WINDOW + r * PIX : WINDOW + (r + 1) * PIX, :] = joined
 
 
-def hand_kernel(place, own, partner, *outs):
+def hand_kernel(place, own, partner, own_target, *outs):
+    *outs, leaving = outs
+    outs = [outs[3], *outs[:3]]
     lane = lane_index((PIX, LANES))
 
     def window(ref, first, count, start):
@@ -192,6 +194,10 @@
                     piece = window(ref, first, PIX, start + LANES - q * REST_LANES)
                     joined = piece if joined is None else jnp.where(lane < q * REST_LANES, joined, piece)
                 out[base + UPDATES + r * PIX : base + UPDATES + (r + 1) * PIX, :] = joined
+        if d == 0:
+            copy = pltpu.make_async_copy(out, own_target, leaving)
+            copy.start()
+    copy.wait()
 
 
 def sincos(x):
@@ -383,7 +389,8 @@
         hand_kernel,
         out_shape=(jax.ShapeDtypeStruct((2 * NEW_PAYLOAD, LANES), jnp.float32),) * 4,
         in_specs=[smem(), vmem(), vmem()],
-        out_specs=(vmem(),) * 4,
+        out_specs=(pl.BlockSpec(memory_space=pl.ANY),) + (vmem(),) * 3,
+        scratch_shapes=[pltpu.VMEM((2 * NEW_PAYLOAD, LANES), jnp.float32), pltpu.SemaphoreType.DMA(())],
         compiler_params=pltpu.CompilerParams(vmem_limit_bytes=8 << 20),
     )(place, own, partner)
 
@@ -488,16 +495,16 @@
 
     side = (layer % 2).reshape(1)
     place = jnp.stack([layer % 2, layer // 2 % 4, half])
-    payload = pack(low, core, high, meta)
-    _, later = lax.optimization_barrier((payload, place))
+    flags = jnp.concatenate([side, valid.reshape(-1)])
+    payload, partner, flags = lax.optimization_barrier((pack(low, core, high, meta), partner, flags))
     mine = exchange(payload, groups_by(lambda zh, x, c, y, zl: (c, y, zl)))
-    news = list(hand(later, new_rows(half), partner))
+    news = list(hand(place, new_rows(half), partner))
+    *news[1:], recon = lax.optimization_barrier((*news[1:], recon))
     for d in range(1, 4):
         along = [(i, i // 8 * 8 + (i % 8 + 2 * d) % 8) for i in range(16)]
         news[d] = lax.ppermute(news[d], "layer", along)
     matrix = jnp.transpose(recon, (0, 2, 3, 1, 4)).reshape(FLAT, ACTS)
-    flags = jnp.concatenate([side, valid.reshape(-1)])
-    mine, matrix, flags = lax.optimization_barrier((mine, matrix, flags))
+    mine, matrix = lax.optimization_barrier((mine, matrix))
     here, there = partial_phases(place, mine, news)
     keep, send, flat = slopes_and_products(flags, here, to_other_core(there), matrix)
 

time: 114 us -> 102 us (0.89)
  waiting for transfers between devices: 16.8 us -> 8.74 us
  blocking collectives: 36.6 us -> 33.8 us
  starting transfers between devices: 32.5 us -> 29.9 us
    ppermute x3, waiting for transfers between devices: 3.97 us -> 0.28 us  [local(): news[d] = lax.ppermute(news[d], 'layer', along)]
    all_to_all x3, blocking collectives: 36.6 us -> 33.8 us  [exchange(): lax.all_to_all(blocks, ('layer', 'sub'), 0, 0, tiled=True, axis_index_gro...]
    all_to_all x1, starting transfers between devices: 7.95 us -> 5.18 us  [exchange(): lax.all_to_all(blocks, ('layer', 'sub'), 0, 0, tiled=True, axis_index_gro...]
    ppermute x1, waiting for transfers between devices: 4.58 us -> 2.18 us  [local(): lax.ppermute(strip(jnp.where(owner == count - 1, PUP_TURN - 1, PUP_TURN))...]
    ppermute x1, waiting for transfers between devices: 5.8 us -> 3.8 us  [local(): lax.ppermute(new_rows(1 - half), 'layer', [(i, i ^ 8) for i in range(16)])]
    ppermute x3, starting transfers between devices: 6.24 us -> 7.59 us  [to_other_core(): return lax.ppermute(block, 'layer', [(i, i ^ 1) for i in range(16)])]
  transfers between devices with their start and end apart: 10 -> 10, of which waited for: 7 -> 6; matrix products, arithmetic and copies ran while one was open for 10% -> 12% of each run, Pallas kernels for 2% -> 3%
where the time goes in v8:
time: 102 us; the launch traced here: 101 us
  blocking collectives  33.8 us (33%)
  starting transfers between devices  29.9 us (29%)
  Pallas kernels  14.8 us (15%)
  local copies, waits for them, and re-layouts  10.9 us (11%)
  waiting for transfers between devices  8.74 us (9%)
  other arithmetic  2.33 us (2%)
    all_to_all x3, blocking collectives, exchange(): lax.all_to_all(blocks, ('layer', 'sub'), 0, 0, tiled=True, axis_index_gro...  33.8 us
    ppermute x1, starting transfers between devices, local(): lax.ppermute(strip(jnp.where(owner == 0, PUP_TURN + 1, PUP_TURN)), 'sub',...  7.7 us
    ppermute x3, starting transfers between devices, to_other_core(): return lax.ppermute(block, 'layer', [(i, i ^ 1) for i in range(16)])  7.59 us
    pallas_call x1, Pallas kernels, partial_phases(): pl.pallas_call(sum_kernel, out_shape=(half, half), in_specs=[smem()] + [v...  6.83 us
    reshape x1, local copies, waits for them, and re-layouts, local(): matrix = jnp.transpose(recon, (0, 2, 3, 1, 4)).reshape(FLAT, ACTS)  6.33 us
    all_to_all x1, starting transfers between devices, exchange(): lax.all_to_all(blocks, ('layer', 'sub'), 0, 0, tiled=True, axis_index_gro...  5.18 us
    ppermute x3, starting transfers between devices, local(): news[d] = lax.ppermute(news[d], 'layer', along)  5.11 us
    ppermute x1, starting transfers between devices, local(): lax.ppermute(new_rows(1 - half), 'layer', [(i, i ^ 8) for i in range(16)])  4.3 us
  transfers between devices with their start and end apart: 10, of which 6 were waited for; matrix products, arithmetic and copies ran while one was open for 12% of the time, Pallas kernels for 3%

profile of v8, /device:TPU:1, one launch (start us, length us, event | category | flops | bytes accessed | tf_op | source)
XLA Modules:
  0.0 101.2 jit_solution(14658041155704479332)
XLA Ops:
  0.6 1.0 dynamic-slice_bitcast_fusion.2
  1.6 7.7 %collective-permute-start.1 = (f32[40,768]{1,0:T(8,128)S(1)}, f32[40,768]{1,0:T(8,128)S(1)}, u32[]{:S(2)}, u32[]{:S(2)}) collective-permute-start(f32[40,768]{1,0:T(8,128)S(1)} %get-tuple-element.38), channel_id=1, source_target_pairs={{1,0},{2,1},{3,2},{4,3},{5,4},{6,5},{7,6},{8,7},{9,8},{10,9},{11,1... | collective-permute-start | bytes 368648 | tf_op jit(solution)/shard_map/ppermute | solution.py:480
  9.3 0.0 collective-permute-start
  9.3 1.0 %dynamic-slice_bitcast_fusion = (f32[80,512]{1,0:T(8,128)S(1)}, f32[80,512]{1,0:T(8,128)S(1)}) fusion(f32[10,1,2048,8]{2,3,1,0:T(8,128)} %param.8, s32[]{:T(128)S(6)} %select_n.62, s32[]{:T(128)S(6)} %select_n.58), kind=kLoop, calls=%fused_computation | loop fusion | bytes 655368 | tf_op jit(solution)/shard_map/reshape | solution.py:471
  10.4 4.3 %collective-permute-start.2 = (f32[80,512]{1,0:T(8,128)S(1)}, f32[80,512]{1,0:T(8,128)S(1)}, u32[]{:S(2)}, u32[]{:S(2)}) collective-permute-start(f32[80,512]{1,0:T(8,128)S(1)} %get-tuple-element.41), channel_id=1, source_target_pairs={{0,128},{16,144},{32,160},{48,176},{64,192},{80,208},{96,224},{112... | collective-permute-start | bytes 491528 | tf_op jit(solution)/shard_map/ppermute | solution.py:482
  14.7 0.8 reshape.95
  15.4 0.7 add_select_fusion
  16.1 0.7 fusion.5
  16.8 0.9 slice_bitcast_fusion.core
  17.7 0.7 fusion.6
  18.4 0.1 pad_add_fusion.flags
  18.5 0.1 add_convert_fusion.meta
  18.5 0.0 collective-permute-done.1.high
  18.5 2.2 %collective-permute-done.low = f32[40,768]{1,0:T(8,128)S(1)} collective-permute-done((f32[40,768]{1,0:T(8,128)S(1)}, f32[40,768]{1,0:T(8,128)S(1)}, u32[]{:S(2)}, u32[]{:S(2)}) %collective-permute-start) | collective-permute-done | bytes 122912 | tf_op jit(solution)/shard_map/ppermute | solution.py:479
  20.7 1.4 %shard_map.86 = f32[8,152,128]{2,1,0:T(8,128)} custom-call(f32[40,768]{1,0:T(8,128)S(1)} %collective-permute-done.low, f32[40,768]{1,0:T(8,128)S(1)} %slice_bitcast_fusion.core, f32[40,768]{1,0:T(8,128)S(1)} %collective-permute-done.1.high, f32[8,128]{1,0:T(8,128)S(1)} %add_convert_fusion.meta), custom_call_target="tpu_custom_call" | custom-call | tf_op jit(solution)/shard_map/pallas_call | solution.py:378
  22.1 3.8 %collective-permute-done.2.partner = f32[80,512]{1,0:T(8,128)S(1)} collective-permute-done((f32[80,512]{1,0:T(8,128)S(1)}, f32[80,512]{1,0:T(8,128)S(1)}, u32[]{:S(2)}, u32[]{:S(2)}) %collective-permute-start.2) | collective-permute-done | bytes 163872 | tf_op jit(solution)/shard_map/ppermute | solution.py:482
  25.9 5.2 %all-to-all-start = ((f32[8,152,128]{2,1,0:T(8,128)}), f32[8,152,128]{2,1,0:T(8,128)}, u32[]{:S(2)}, u32[]{:S(2)}) async-start(f32[8,152,128]{2,1,0:T(8,128)} %shard_map.86), calls=%async_computation | async-start | bytes 1245184 | tf_op jit(solution)/shard_map/all_to_all | solution.py:450
  31.1 0.1 pad_add_fusion.1.place
  31.2 1.9 %shard_map.87 = (f32[208,128]{1,0:T(8,128)S(1)}, f32[208,128]{1,0:T(8,128)}, f32[208,128]{1,0:T(8,128)}, f32[208,128]{1,0:T(8,128)}) custom-call(s32[3]{0:T(128)S(1)} %pad_add_fusion.1.place, f32[80,512]{1,0:T(8,128)S(1)} %get-tuple-element.40.own, f32[80,512]{1,0:T(8,128)S(1)} %collective-permute-done.2.partner), custom_call_target="tpu_custom_call" | custom-call | tf_op jit(solution)/shard_map/pallas_call | solution.py:388
  33.1 1.5 %collective-permute-start.3 = (f32[208,128]{1,0:T(8,128)}, f32[208,128]{1,0:T(8,128)S(1)}, u32[]{:S(2)}, u32[]{:S(2)}) collective-permute-start(f32[208,128]{1,0:T(8,128)} %get-tuple-element.29), channel_id=1, source_target_pairs={{0,32},{16,48},{32,64},{48,80},{64,96},{80,112},{96,0},{112,16},{1... | collective-permute-start | bytes 319496 | tf_op jit(solution)/shard_map/ppermute | solution.py:505
  34.6 2.4 %collective-permute-start.4 = (f32[208,128]{1,0:T(8,128)}, f32[208,128]{1,0:T(8,128)}, u32[]{:S(2)}, u32[]{:S(2)}) collective-permute-start(f32[208,128]{1,0:T(8,128)} %get-tuple-element.30), channel_id=1, source_target_pairs={{0,64},{16,80},{32,96},{48,112},{64,0},{80,16},{96,32},{112,48},{1... | collective-permute-start | bytes 319496 | tf_op jit(solution)/shard_map/ppermute | solution.py:505
  37.0 1.2 %collective-permute-start.5 = (f32[208,128]{1,0:T(8,128)}, f32[208,128]{1,0:T(8,128)}, u32[]{:S(2)}, u32[]{:S(2)}) collective-permute-start(f32[208,128]{1,0:T(8,128)} %get-tuple-element.31), channel_id=1, source_target_pairs={{0,96},{16,112},{32,0},{48,16},{64,32},{80,48},{96,64},{112,80},{1... | collective-permute-start | bytes 319496 | tf_op jit(solution)/shard_map/ppermute | solution.py:505
  38.2 6.3 %reshape.98.recon = bf16[300,5376]{1,0:T(8,128)(2,1)S(1)} reshape(bf16[6,5,5,2,5376]{4,3,2,1,0:T(2,128)(2,1)} %bitcast.50) | data formatting | bytes 6451200 | tf_op jit(solution)/shard_map/reshape | solution.py:506
  44.6 0.0 all-to-all-done.mine
  44.6 0.0 collective-permute-done.3.new_1
  44.6 0.0 collective-permute-done.4.new_2
  44.6 0.3 collective-permute-done.5.new_3
  44.9 6.8 %shard_map.88 = (f32[10,80,128]{2,1,0:T(8,128)S(1)}, f32[10,80,128]{2,1,0:T(8,128)S(1)}) custom-call(s32[3]{0:T(128)S(1)} %pad_add_fusion.1.place, f32[8,152,128]{2,1,0:T(8,128)} %all-to-all-done.mine, f32[208,128]{1,0:T(8,128)S(1)} %get-tuple-element.28.new_0, f32[208,128]{1,0:T(8,128)S(1)} %collective-permute-done.3.new_1, ...), custom_call_target="tpu_custom_call" | custom-call | tf_op jit(solution)/shard_map/pallas_call | solution.py:400
  51.7 2.9 %collective-permute-start.6 = (f32[10,80,128]{2,1,0:T(8,128)S(1)}, f32[10,80,128]{2,1,0:T(8,128)S(1)}, u32[]{:S(2)}, u32[]{:S(2)}) collective-permute-start(f32[10,80,128]{2,1,0:T(8,128)S(1)} %get-tuple-element.33), channel_id=1, source_target_pairs={{0,16},{16,0},{32,48},{48,32},{64,80},{80,64},{96,112},{112,96},{1... | collective-permute-start | bytes 1228808 | tf_op jit(solution)/shard_map/ppermute | solution.py:458
  54.6 1.4 %collective-permute-done.6.there = f32[10,80,128]{2,1,0:T(8,128)S(1)} collective-permute-done((f32[10,80,128]{2,1,0:T(8,128)S(1)}, f32[10,80,128]{2,1,0:T(8,128)S(1)}, u32[]{:S(2)}, u32[]{:S(2)}) %collective-permute-start.6) | collective-permute-done | bytes 409632 | tf_op jit(solution)/shard_map/ppermute | solution.py:458
  55.9 3.9 %shard_map.89 = (f32[16,16,128]{2,1,0:T(8,128)S(1)}, f32[16,16,128]{2,1,0:T(8,128)S(1)}, f32[16,384]{1,0:T(8,128)S(1)}) custom-call(s32[26]{0:T(128)S(1)} %pad_add_fusion.flags, f32[10,80,128]{2,1,0:T(8,128)S(1)} %get-tuple-element.32.here, f32[10,80,128]{2,1,0:T(8,128)S(1)} %collective-permute-done.6.there, bf16[300,5376]{1,0:T(8,128)(2,1)S(1)} %reshape.98.recon), custom_call_target="tpu_custom_call" | custom-call | tf_op jit(solution)/shard_map/pallas_call | solution.py:417
  59.9 0.5 collective-permute-start.7
  60.3 1.0 collective-permute-done.7
  61.3 9.7 %all_to_all.20 = f32[16,16,128]{2,1,0:T(8,128)S(1)} all-to-all(f32[16,16,128]{2,1,0:T(8,128)S(1)} %add.100), channel_id=1, replica_groups={{0,4,8,12,32,36,40,44,64,68,72,76,96,100,104,108},{1,5,9,13,33,37,41,45..., dimensions={0} | all-to-all | bytes 262144 | tf_op jit(solution)/shard_map/all_to_all | solution.py:450
  71.1 13.9 %all_to_all.21 = f32[8,16,128]{2,1,0:T(8,128)S(1)} all-to-all(f32[8,16,128]{2,1,0:T(8,128)S(1)} %broadcast_in_dim.9), channel_id=1, replica_groups={{0,1,2,3,128,129,130,131},{4,5,6,7,132,133,134,135},{8,9,10,11,136,137,..., dimensions={0} | all-to-all | bytes 131072 | tf_op jit(solution)/shard_map/all_to_all | solution.py:450
  85.0 10.2 %all_to_all.22.mine = f32[16,16,128]{2,1,0:T(8,128)S(1)} all-to-all(f32[16,16,128]{2,1,0:T(8,128)S(1)} %broadcast_in_dim.18), channel_id=1, replica_groups={{0,4,8,12,32,36,40,44,64,68,72,76,96,100,104,108},{1,5,9,13,33,37,41,45..., dimensions={0} | all-to-all | bytes 262144 | tf_op jit(solution)/shard_map/all_to_all | solution.py:450
  95.2 4.3 %collective-permute-start.8 = (f32[16,16,128]{2,1,0:T(8,128)S(1)}, f32[16,16,128]{2,1,0:T(8,128)S(1)}, u32[]{:S(2)}, u32[]{:S(2)}) collective-permute-start(f32[16,16,128]{2,1,0:T(8,128)S(1)} %all_to_all.22.mine), channel_id=1, source_target_pairs={{0,16},{16,0},{32,48},{48,32},{64,80},{80,64},{96,112},{112,96},{1... | collective-permute-start | bytes 393224 | tf_op jit(solution)/shard_map/ppermute | solution.py:458
  99.5 0.1 copy.17
  99.6 0.8 reshape.99
  100.4 0.1 collective-permute-done.8.other
  100.5 0.8 shard_map.90
  (5 shorter events, 0.1 us)
Async XLA Ops:
  1.6 16.9 %collective-permute-start.1 = (f32[40,768]{1,0:T(8,128)S(1)}, f32[40,768]{1,0:T(8,128)S(1)}, u32[]{:S(2)}, u32[]{:S(2)}) collective-permute-start(f32[40,768]{1,0:T(8,128)S(1)} %get-tuple-element.38), channel_id=1, source_target_pairs={{1,0},{2,1},{3,2},{4,3},{5,4},{6,5},{7,6},{8,7},{9,8},{10,9},{11,1... | collective-permute-start | bytes 368648 | tf_op jit(solution)/shard_map/ppermute | solution.py:480
  9.3 11.4 %collective-permute-start = (f32[40,768]{1,0:T(8,128)S(1)}, f32[40,768]{1,0:T(8,128)S(1)}, u32[]{:S(2)}, u32[]{:S(2)}) collective-permute-start(f32[40,768]{1,0:T(8,128)S(1)} %get-tuple-element.39), channel_id=1, source_target_pairs={{0,1},{1,2},{2,3},{3,4},{4,5},{5,6},{6,7},{7,8},{8,9},{9,10},{10,1... | collective-permute-start | bytes 368648 | tf_op jit(solution)/shard_map/ppermute | solution.py:479
  10.4 15.6 %collective-permute-start.2 = (f32[80,512]{1,0:T(8,128)S(1)}, f32[80,512]{1,0:T(8,128)S(1)}, u32[]{:S(2)}, u32[]{:S(2)}) collective-permute-start(f32[80,512]{1,0:T(8,128)S(1)} %get-tuple-element.41), channel_id=1, source_target_pairs={{0,128},{16,144},{32,160},{48,176},{64,192},{80,208},{96,224},{112... | collective-permute-start | bytes 491528 | tf_op jit(solution)/shard_map/ppermute | solution.py:482
  25.9 18.6 %all-to-all-start = ((f32[8,152,128]{2,1,0:T(8,128)}), f32[8,152,128]{2,1,0:T(8,128)}, u32[]{:S(2)}, u32[]{:S(2)}) async-start(f32[8,152,128]{2,1,0:T(8,128)} %shard_map.86), calls=%async_computation | async-start | bytes 1245184 | tf_op jit(solution)/shard_map/all_to_all | solution.py:450
  33.1 11.5 %collective-permute-start.3 = (f32[208,128]{1,0:T(8,128)}, f32[208,128]{1,0:T(8,128)S(1)}, u32[]{:S(2)}, u32[]{:S(2)}) collective-permute-start(f32[208,128]{1,0:T(8,128)} %get-tuple-element.29), channel_id=1, source_target_pairs={{0,32},{16,48},{32,64},{48,80},{64,96},{80,112},{96,0},{112,16},{1... | collective-permute-start | bytes 319496 | tf_op jit(solution)/shard_map/ppermute | solution.py:505
  34.6 9.9 %collective-permute-start.4 = (f32[208,128]{1,0:T(8,128)}, f32[208,128]{1,0:T(8,128)}, u32[]{:S(2)}, u32[]{:S(2)}) collective-permute-start(f32[208,128]{1,0:T(8,128)} %get-tuple-element.30), channel_id=1, source_target_pairs={{0,64},{16,80},{32,96},{48,112},{64,0},{80,16},{96,32},{112,48},{1... | collective-permute-start | bytes 319496 | tf_op jit(solution)/shard_map/ppermute | solution.py:505
  37.0 7.8 %collective-permute-start.5 = (f32[208,128]{1,0:T(8,128)}, f32[208,128]{1,0:T(8,128)}, u32[]{:S(2)}, u32[]{:S(2)}) collective-permute-start(f32[208,128]{1,0:T(8,128)} %get-tuple-element.31), channel_id=1, source_target_pairs={{0,96},{16,112},{32,0},{48,16},{64,32},{80,48},{96,64},{112,80},{1... | collective-permute-start | bytes 319496 | tf_op jit(solution)/shard_map/ppermute | solution.py:505
  51.7 4.2 %collective-permute-start.6 = (f32[10,80,128]{2,1,0:T(8,128)S(1)}, f32[10,80,128]{2,1,0:T(8,128)S(1)}, u32[]{:S(2)}, u32[]{:S(2)}) collective-permute-start(f32[10,80,128]{2,1,0:T(8,128)S(1)} %get-tuple-element.33), channel_id=1, source_target_pairs={{0,16},{16,0},{32,48},{48,32},{64,80},{80,64},{96,112},{112,96},{1... | collective-permute-start | bytes 1228808 | tf_op jit(solution)/shard_map/ppermute | solution.py:458
  59.9 1.4 %collective-permute-start.7 = (f32[16,16,128]{2,1,0:T(8,128)S(1)}, f32[16,16,128]{2,1,0:T(8,128)S(1)}, u32[]{:S(2)}, u32[]{:S(2)}) collective-permute-start(f32[16,16,128]{2,1,0:T(8,128)S(1)} %get-tuple-element.37), channel_id=1, source_target_pairs={{0,16},{16,0},{32,48},{48,32},{64,80},{80,64},{96,112},{112,96},{1... | collective-permute-start | bytes 393224 | tf_op jit(solution)/shard_map/ppermute | solution.py:458
  95.2 5.2 %collective-permute-start.8 = (f32[16,16,128]{2,1,0:T(8,128)S(1)}, f32[16,16,128]{2,1,0:T(8,128)S(1)}, u32[]{:S(2)}, u32[]{:S(2)}) collective-permute-start(f32[16,16,128]{2,1,0:T(8,128)S(1)} %all_to_all.22.mine), channel_id=1, source_target_pairs={{0,16},{16,0},{32,48},{48,32},{64,80},{80,64},{96,112},{112,96},{1... | collective-permute-start | bytes 393224 | tf_op jit(solution)/shard_map/ppermute | solution.py:458

commit v9 on v8

--- a/solution.py
+++ b/solution.py
@@ -268,16 +268,15 @@
                 window = state[l, pl.ds(meta[l, g, META_LANE + t], 40), :]
                 total = total + pltpu.roll(window, meta[l, g, TURN_LANE + t], 1)
             acc.append(total)
-        for out, block in ((keep, side), (send, 1 - side)):
-            for k in range(2):
-                placed = [
-                    pltpu.roll(acc[3 * k + j], lax.rem(LANES + 40 * j - 40 * block, LANES), 1) for j in range(3)
-                ]
-                joined = jnp.where(lane < 40, placed[0], jnp.where(lane < 80, placed[1], placed[2]))
-                out[t, k * 40 : (k + 1) * 40, :] = joined
+        for k in range(2):
+            one, two, three = acc[3 * k : 3 * k + 3]
+            near = jnp.where(lane < 40, one, jnp.where(lane < 80, pltpu.roll(two, 40, 1), pltpu.roll(three, 80, 1)))
+            far = jnp.where(lane < 40, pltpu.roll(one, LANES - 40, 1), jnp.where(lane < 80, two, pltpu.roll(three, 40, 1)))
+            keep[t, k * 40 : (k + 1) * 40, :] = jnp.where(side == 0, near, far)
+            send[t, k * 40 : (k + 1) * 40, :] = jnp.where(side == 0, far, near)
         return carry
 
-    lax.fori_loop(0, STEPS, step, 0)
+    lax.fori_loop(0, STEPS, step, 0, unroll=2)
 
 
 def spot_kernel(flags, here, there, recon, keep, send, flat_out, sums, lane_tab, lane_rest):

time: 102 us -> 101 us (level)
  no operation moved by 1% of the time
where the time goes in v9:
time: 101 us
  blocking collectives  33.8 us (33%)
  starting transfers between devices  29.9 us (30%)
  Pallas kernels  14.2 us (14%)
  local copies, waits for them, and re-layouts  10.9 us (11%)
  waiting for transfers between devices  8.74 us (9%)
  other arithmetic  2.33 us (2%)
    all_to_all x3, blocking collectives, exchange(): lax.all_to_all(blocks, ('layer', 'sub'), 0, 0, tiled=True, axis_index_gro...  33.8 us
    ppermute x1, starting transfers between devices, local(): lax.ppermute(strip(jnp.where(owner == 0, PUP_TURN + 1, PUP_TURN)), 'sub',...  7.7 us
    ppermute x3, starting transfers between devices, to_other_core(): return lax.ppermute(block, 'layer', [(i, i ^ 1) for i in range(16)])  7.59 us
    reshape x1, local copies, waits for them, and re-layouts, local(): matrix = jnp.transpose(recon, (0, 2, 3, 1, 4)).reshape(FLAT, ACTS)  6.33 us
    pallas_call x1, Pallas kernels, partial_phases(): pl.pallas_call(sum_kernel, out_shape=(half, half), in_specs=[smem()] + [v...  6.19 us
    all_to_all x1, starting transfers between devices, exchange(): lax.all_to_all(blocks, ('layer', 'sub'), 0, 0, tiled=True, axis_index_gro...  5.18 us
    ppermute x3, starting transfers between devices, local(): news[d] = lax.ppermute(news[d], 'layer', along)  5.11 us
    ppermute x1, starting transfers between devices, local(): lax.ppermute(new_rows(1 - half), 'layer', [(i, i ^ 8) for i in range(16)])  4.3 us
  transfers between devices with their start and end apart: 10, of which 6 were waited for; matrix products, arithmetic and copies ran while one was open for 12% of the time, Pallas kernels for 3%

profile of v9, /device:TPU:1, one launch (start us, length us, event | category | flops | bytes accessed | tf_op | source)
XLA Modules:
  0.0 100.6 jit_solution(786026746167498017)
XLA Ops:
  0.6 1.0 dynamic-slice_bitcast_fusion.2
  1.6 7.7 %collective-permute-start.1 = (f32[40,768]{1,0:T(8,128)S(1)}, f32[40,768]{1,0:T(8,128)S(1)}, u32[]{:S(2)}, u32[]{:S(2)}) collective-permute-start(f32[40,768]{1,0:T(8,128)S(1)} %get-tuple-element.38), channel_id=1, source_target_pairs={{1,0},{2,1},{3,2},{4,3},{5,4},{6,5},{7,6},{8,7},{9,8},{10,9},{11,1... | collective-permute-start | bytes 368648 | tf_op jit(solution)/shard_map/ppermute | solution.py:479
  9.3 0.0 collective-permute-start
  9.3 1.0 %dynamic-slice_bitcast_fusion = (f32[80,512]{1,0:T(8,128)S(1)}, f32[80,512]{1,0:T(8,128)S(1)}) fusion(f32[10,1,2048,8]{2,3,1,0:T(8,128)} %param.8, s32[]{:T(128)S(6)} %select_n.62, s32[]{:T(128)S(6)} %select_n.58), kind=kLoop, calls=%fused_computation | loop fusion | bytes 655368 | tf_op jit(solution)/shard_map/reshape | solution.py:470
  10.4 4.3 %collective-permute-start.2 = (f32[80,512]{1,0:T(8,128)S(1)}, f32[80,512]{1,0:T(8,128)S(1)}, u32[]{:S(2)}, u32[]{:S(2)}) collective-permute-start(f32[80,512]{1,0:T(8,128)S(1)} %get-tuple-element.41), channel_id=1, source_target_pairs={{0,128},{16,144},{32,160},{48,176},{64,192},{80,208},{96,224},{112... | collective-permute-start | bytes 491528 | tf_op jit(solution)/shard_map/ppermute | solution.py:481
  14.7 0.8 reshape.95
  15.4 0.7 add_select_fusion
  16.1 0.7 fusion.5
  16.8 0.9 slice_bitcast_fusion.core
  17.7 0.7 fusion.6
  18.4 0.1 pad_add_fusion.flags
  18.5 0.1 add_convert_fusion.meta
  18.5 0.0 collective-permute-done.1.high
  18.5 2.2 %collective-permute-done.low = f32[40,768]{1,0:T(8,128)S(1)} collective-permute-done((f32[40,768]{1,0:T(8,128)S(1)}, f32[40,768]{1,0:T(8,128)S(1)}, u32[]{:S(2)}, u32[]{:S(2)}) %collective-permute-start) | collective-permute-done | bytes 122912 | tf_op jit(solution)/shard_map/ppermute | solution.py:478
  20.7 1.4 %shard_map.86 = f32[8,152,128]{2,1,0:T(8,128)} custom-call(f32[40,768]{1,0:T(8,128)S(1)} %collective-permute-done.low, f32[40,768]{1,0:T(8,128)S(1)} %slice_bitcast_fusion.core, f32[40,768]{1,0:T(8,128)S(1)} %collective-permute-done.1.high, f32[8,128]{1,0:T(8,128)S(1)} %add_convert_fusion.meta), custom_call_target="tpu_custom_call" | custom-call | tf_op jit(solution)/shard_map/pallas_call | solution.py:377
  22.1 3.8 %collective-permute-done.2.partner = f32[80,512]{1,0:T(8,128)S(1)} collective-permute-done((f32[80,512]{1,0:T(8,128)S(1)}, f32[80,512]{1,0:T(8,128)S(1)}, u32[]{:S(2)}, u32[]{:S(2)}) %collective-permute-start.2) | collective-permute-done | bytes 163872 | tf_op jit(solution)/shard_map/ppermute | solution.py:481
  25.9 5.2 %all-to-all-start = ((f32[8,152,128]{2,1,0:T(8,128)}), f32[8,152,128]{2,1,0:T(8,128)}, u32[]{:S(2)}, u32[]{:S(2)}) async-start(f32[8,152,128]{2,1,0:T(8,128)} %shard_map.86), calls=%async_computation | async-start | bytes 1245184 | tf_op jit(solution)/shard_map/all_to_all | solution.py:449
  31.1 0.1 pad_add_fusion.1.place
  31.2 1.9 %shard_map.87 = (f32[208,128]{1,0:T(8,128)S(1)}, f32[208,128]{1,0:T(8,128)}, f32[208,128]{1,0:T(8,128)}, f32[208,128]{1,0:T(8,128)}) custom-call(s32[3]{0:T(128)S(1)} %pad_add_fusion.1.place, f32[80,512]{1,0:T(8,128)S(1)} %get-tuple-element.40.own, f32[80,512]{1,0:T(8,128)S(1)} %collective-permute-done.2.partner), custom_call_target="tpu_custom_call" | custom-call | tf_op jit(solution)/shard_map/pallas_call | solution.py:387
  33.1 1.5 %collective-permute-start.3 = (f32[208,128]{1,0:T(8,128)}, f32[208,128]{1,0:T(8,128)S(1)}, u32[]{:S(2)}, u32[]{:S(2)}) collective-permute-start(f32[208,128]{1,0:T(8,128)} %get-tuple-element.29), channel_id=1, source_target_pairs={{0,32},{16,48},{32,64},{48,80},{64,96},{80,112},{96,0},{112,16},{1... | collective-permute-start | bytes 319496 | tf_op jit(solution)/shard_map/ppermute | solution.py:504
  34.6 2.4 %collective-permute-start.4 = (f32[208,128]{1,0:T(8,128)}, f32[208,128]{1,0:T(8,128)}, u32[]{:S(2)}, u32[]{:S(2)}) collective-permute-start(f32[208,128]{1,0:T(8,128)} %get-tuple-element.30), channel_id=1, source_target_pairs={{0,64},{16,80},{32,96},{48,112},{64,0},{80,16},{96,32},{112,48},{1... | collective-permute-start | bytes 319496 | tf_op jit(solution)/shard_map/ppermute | solution.py:504
  37.0 1.2 %collective-permute-start.5 = (f32[208,128]{1,0:T(8,128)}, f32[208,128]{1,0:T(8,128)}, u32[]{:S(2)}, u32[]{:S(2)}) collective-permute-start(f32[208,128]{1,0:T(8,128)} %get-tuple-element.31), channel_id=1, source_target_pairs={{0,96},{16,112},{32,0},{48,16},{64,32},{80,48},{96,64},{112,80},{1... | collective-permute-start | bytes 319496 | tf_op jit(solution)/shard_map/ppermute | solution.py:504
  38.2 6.3 %reshape.98.recon = bf16[300,5376]{1,0:T(8,128)(2,1)S(1)} reshape(bf16[6,5,5,2,5376]{4,3,2,1,0:T(2,128)(2,1)} %bitcast.50) | data formatting | bytes 6451200 | tf_op jit(solution)/shard_map/reshape | solution.py:505
  44.6 0.0 all-to-all-done.mine
  44.6 0.0 collective-permute-done.3.new_1
  44.6 0.0 collective-permute-done.4.new_2
  44.6 0.3 collective-permute-done.5.new_3
  44.9 6.2 %shard_map.88 = (f32[10,80,128]{2,1,0:T(8,128)S(1)}, f32[10,80,128]{2,1,0:T(8,128)S(1)}) custom-call(s32[3]{0:T(128)S(1)} %pad_add_fusion.1.place, f32[8,152,128]{2,1,0:T(8,128)} %all-to-all-done.mine, f32[208,128]{1,0:T(8,128)S(1)} %get-tuple-element.28.new_0, f32[208,128]{1,0:T(8,128)S(1)} %collective-permute-done.3.new_1, ...), custom_call_target="tpu_custom_call" | custom-call | tf_op jit(solution)/shard_map/pallas_call | solution.py:399
  51.1 2.9 %collective-permute-start.6 = (f32[10,80,128]{2,1,0:T(8,128)S(1)}, f32[10,80,128]{2,1,0:T(8,128)S(1)}, u32[]{:S(2)}, u32[]{:S(2)}) collective-permute-start(f32[10,80,128]{2,1,0:T(8,128)S(1)} %get-tuple-element.33), channel_id=1, source_target_pairs={{0,16},{16,0},{32,48},{48,32},{64,80},{80,64},{96,112},{112,96},{1... | collective-permute-start | bytes 1228808 | tf_op jit(solution)/shard_map/ppermute | solution.py:457
  53.9 1.4 %collective-permute-done.6.there = f32[10,80,128]{2,1,0:T(8,128)S(1)} collective-permute-done((f32[10,80,128]{2,1,0:T(8,128)S(1)}, f32[10,80,128]{2,1,0:T(8,128)S(1)}, u32[]{:S(2)}, u32[]{:S(2)}) %collective-permute-start.6) | collective-permute-done | bytes 409632 | tf_op jit(solution)/shard_map/ppermute | solution.py:457
  55.3 3.9 %shard_map.89 = (f32[16,16,128]{2,1,0:T(8,128)S(1)}, f32[16,16,128]{2,1,0:T(8,128)S(1)}, f32[16,384]{1,0:T(8,128)S(1)}) custom-call(s32[26]{0:T(128)S(1)} %pad_add_fusion.flags, f32[10,80,128]{2,1,0:T(8,128)S(1)} %get-tuple-element.32.here, f32[10,80,128]{2,1,0:T(8,128)S(1)} %collective-permute-done.6.there, bf16[300,5376]{1,0:T(8,128)(2,1)S(1)} %reshape.98.recon), custom_call_target="tpu_custom_call" | custom-call | tf_op jit(solution)/shard_map/pallas_call | solution.py:416
  59.2 0.5 collective-permute-start.7
  59.7 1.0 collective-permute-done.7
  60.7 9.7 %all_to_all.20 = f32[16,16,128]{2,1,0:T(8,128)S(1)} all-to-all(f32[16,16,128]{2,1,0:T(8,128)S(1)} %add.100), channel_id=1, replica_groups={{0,4,8,12,32,36,40,44,64,68,72,76,96,100,104,108},{1,5,9,13,33,37,41,45..., dimensions={0} | all-to-all | bytes 262144 | tf_op jit(solution)/shard_map/all_to_all | solution.py:449
  70.5 13.9 %all_to_all.21 = f32[8,16,128]{2,1,0:T(8,128)S(1)} all-to-all(f32[8,16,128]{2,1,0:T(8,128)S(1)} %broadcast_in_dim.9), channel_id=1, replica_groups={{0,1,2,3,128,129,130,131},{4,5,6,7,132,133,134,135},{8,9,10,11,136,137,..., dimensions={0} | all-to-all | bytes 131072 | tf_op jit(solution)/shard_map/all_to_all | solution.py:449
  84.4 10.2 %all_to_all.22.mine = f32[16,16,128]{2,1,0:T(8,128)S(1)} all-to-all(f32[16,16,128]{2,1,0:T(8,128)S(1)} %broadcast_in_dim.18), channel_id=1, replica_groups={{0,4,8,12,32,36,40,44,64,68,72,76,96,100,104,108},{1,5,9,13,33,37,41,45..., dimensions={0} | all-to-all | bytes 262144 | tf_op jit(solution)/shard_map/all_to_all | solution.py:449
  94.6 4.3 %collective-permute-start.8 = (f32[16,16,128]{2,1,0:T(8,128)S(1)}, f32[16,16,128]{2,1,0:T(8,128)S(1)}, u32[]{:S(2)}, u32[]{:S(2)}) collective-permute-start(f32[16,16,128]{2,1,0:T(8,128)S(1)} %all_to_all.22.mine), channel_id=1, source_target_pairs={{0,16},{16,0},{32,48},{48,32},{64,80},{80,64},{96,112},{112,96},{1... | collective-permute-start | bytes 393224 | tf_op jit(solution)/shard_map/ppermute | solution.py:457
  98.8 0.1 copy.17
  99.0 0.8 reshape.99
  99.7 0.1 collective-permute-done.8.other
  99.8 0.8 shard_map.90
  (5 shorter events, 0.1 us)
Async XLA Ops:
  1.6 16.9 %collective-permute-start.1 = (f32[40,768]{1,0:T(8,128)S(1)}, f32[40,768]{1,0:T(8,128)S(1)}, u32[]{:S(2)}, u32[]{:S(2)}) collective-permute-start(f32[40,768]{1,0:T(8,128)S(1)} %get-tuple-element.38), channel_id=1, source_target_pairs={{1,0},{2,1},{3,2},{4,3},{5,4},{6,5},{7,6},{8,7},{9,8},{10,9},{11,1... | collective-permute-start | bytes 368648 | tf_op jit(solution)/shard_map/ppermute | solution.py:479
  9.3 11.4 %collective-permute-start = (f32[40,768]{1,0:T(8,128)S(1)}, f32[40,768]{1,0:T(8,128)S(1)}, u32[]{:S(2)}, u32[]{:S(2)}) collective-permute-start(f32[40,768]{1,0:T(8,128)S(1)} %get-tuple-element.39), channel_id=1, source_target_pairs={{0,1},{1,2},{2,3},{3,4},{4,5},{5,6},{6,7},{7,8},{8,9},{9,10},{10,1... | collective-permute-start | bytes 368648 | tf_op jit(solution)/shard_map/ppermute | solution.py:478
  10.4 15.6 %collective-permute-start.2 = (f32[80,512]{1,0:T(8,128)S(1)}, f32[80,512]{1,0:T(8,128)S(1)}, u32[]{:S(2)}, u32[]{:S(2)}) collective-permute-start(f32[80,512]{1,0:T(8,128)S(1)} %get-tuple-element.41), channel_id=1, source_target_pairs={{0,128},{16,144},{32,160},{48,176},{64,192},{80,208},{96,224},{112... | collective-permute-start | bytes 491528 | tf_op jit(solution)/shard_map/ppermute | solution.py:481
  25.9 18.6 %all-to-all-start = ((f32[8,152,128]{2,1,0:T(8,128)}), f32[8,152,128]{2,1,0:T(8,128)}, u32[]{:S(2)}, u32[]{:S(2)}) async-start(f32[8,152,128]{2,1,0:T(8,128)} %shard_map.86), calls=%async_computation | async-start | bytes 1245184 | tf_op jit(solution)/shard_map/all_to_all | solution.py:449
  33.1 11.5 %collective-permute-start.3 = (f32[208,128]{1,0:T(8,128)}, f32[208,128]{1,0:T(8,128)S(1)}, u32[]{:S(2)}, u32[]{:S(2)}) collective-permute-start(f32[208,128]{1,0:T(8,128)} %get-tuple-element.29), channel_id=1, source_target_pairs={{0,32},{16,48},{32,64},{48,80},{64,96},{80,112},{96,0},{112,16},{1... | collective-permute-start | bytes 319496 | tf_op jit(solution)/shard_map/ppermute | solution.py:504
  34.6 9.9 %collective-permute-start.4 = (f32[208,128]{1,0:T(8,128)}, f32[208,128]{1,0:T(8,128)}, u32[]{:S(2)}, u32[]{:S(2)}) collective-permute-start(f32[208,128]{1,0:T(8,128)} %get-tuple-element.30), channel_id=1, source_target_pairs={{0,64},{16,80},{32,96},{48,112},{64,0},{80,16},{96,32},{112,48},{1... | collective-permute-start | bytes 319496 | tf_op jit(solution)/shard_map/ppermute | solution.py:504
  37.0 7.8 %collective-permute-start.5 = (f32[208,128]{1,0:T(8,128)}, f32[208,128]{1,0:T(8,128)}, u32[]{:S(2)}, u32[]{:S(2)}) collective-permute-start(f32[208,128]{1,0:T(8,128)} %get-tuple-element.31), channel_id=1, source_target_pairs={{0,96},{16,112},{32,0},{48,16},{64,32},{80,48},{96,64},{112,80},{1... | collective-permute-start | bytes 319496 | tf_op jit(solution)/shard_map/ppermute | solution.py:504
  51.1 4.3 %collective-permute-start.6 = (f32[10,80,128]{2,1,0:T(8,128)S(1)}, f32[10,80,128]{2,1,0:T(8,128)S(1)}, u32[]{:S(2)}, u32[]{:S(2)}) collective-permute-start(f32[10,80,128]{2,1,0:T(8,128)S(1)} %get-tuple-element.33), channel_id=1, source_target_pairs={{0,16},{16,0},{32,48},{48,32},{64,80},{80,64},{96,112},{112,96},{1... | collective-permute-start | bytes 1228808 | tf_op jit(solution)/shard_map/ppermute | solution.py:457
  59.2 1.4 %collective-permute-start.7 = (f32[16,16,128]{2,1,0:T(8,128)S(1)}, f32[16,16,128]{2,1,0:T(8,128)S(1)}, u32[]{:S(2)}, u32[]{:S(2)}) collective-permute-start(f32[16,16,128]{2,1,0:T(8,128)S(1)} %get-tuple-element.37), channel_id=1, source_target_pairs={{0,16},{16,0},{32,48},{48,32},{64,80},{80,64},{96,112},{112,96},{1... | collective-permute-start | bytes 393224 | tf_op jit(solution)/shard_map/ppermute | solution.py:457
  94.6 5.2 %collective-permute-start.8 = (f32[16,16,128]{2,1,0:T(8,128)S(1)}, f32[16,16,128]{2,1,0:T(8,128)S(1)}, u32[]{:S(2)}, u32[]{:S(2)}) collective-permute-start(f32[16,16,128]{2,1,0:T(8,128)S(1)} %all_to_all.22.mine), channel_id=1, source_target_pairs={{0,16},{16,0},{32,48},{48,32},{64,80},{80,64},{96,112},{112,96},{1... | collective-permute-start | bytes 393224 | tf_op jit(solution)/shard_map/ppermute | solution.py:457

commit v10 on v9

--- a/solution.py
+++ b/solution.py
@@ -276,7 +276,7 @@
             send[t, k * 40 : (k + 1) * 40, :] = jnp.where(side == 0, far, near)
         return carry
 
-    lax.fori_loop(0, STEPS, step, 0, unroll=2)
+    lax.fori_loop(0, STEPS, step, 0, unroll=5)
 
 
 def spot_kernel(flags, here, there, recon, keep, send, flat_out, sums, lane_tab, lane_rest):
@@ -317,7 +317,7 @@
         spots(t)
         return carry
 
-    lax.fori_loop(0, STEPS, step, 0, unroll=2)
+    lax.fori_loop(0, STEPS, step, 0, unroll=5)
 
     units = 20
     stacked = jnp.concatenate(parts(sums[...].reshape(units * 16, LANES), 3))

time: 101 us -> 101 us (level)
  no operation moved by 1% of the time
where the time goes in v10:
time: 101 us; the launch traced here: 100 us
  blocking collectives  33.8 us (33%)
  starting transfers between devices  29.9 us (30%)
  Pallas kernels  13.6 us (13%)
  local copies, waits for them, and re-layouts  10.9 us (11%)
  waiting for transfers between devices  8.74 us (9%)
  other arithmetic  2.33 us (2%)
    all_to_all x3, blocking collectives, exchange(): lax.all_to_all(blocks, ('layer', 'sub'), 0, 0, tiled=True, axis_index_gro...  33.8 us
    ppermute x1, starting transfers between devices, local(): lax.ppermute(strip(jnp.where(owner == 0, PUP_TURN + 1, PUP_TURN)), 'sub',...  7.7 us
    ppermute x3, starting transfers between devices, to_other_core(): return lax.ppermute(block, 'layer', [(i, i ^ 1) for i in range(16)])  7.58 us
    reshape x1, local copies, waits for them, and re-layouts, local(): matrix = jnp.transpose(recon, (0, 2, 3, 1, 4)).reshape(FLAT, ACTS)  6.33 us
    pallas_call x1, Pallas kernels, partial_phases(): pl.pallas_call(sum_kernel, out_shape=(half, half), in_specs=[smem()] + [v...  5.99 us
    all_to_all x1, starting transfers between devices, exchange(): lax.all_to_all(blocks, ('layer', 'sub'), 0, 0, tiled=True, axis_index_gro...  5.18 us
    ppermute x3, starting transfers between devices, local(): news[d] = lax.ppermute(news[d], 'layer', along)  5.11 us
    ppermute x1, starting transfers between devices, local(): lax.ppermute(new_rows(1 - half), 'layer', [(i, i ^ 8) for i in range(16)])  4.3 us
  transfers between devices with their start and end apart: 10, of which 6 were waited for; matrix products, arithmetic and copies ran while one was open for 12% of the time, Pallas kernels for 3%

profile of v10, /device:TPU:1, one launch (start us, length us, event | category | flops | bytes accessed | tf_op | source)
XLA Modules:
  0.0 100.0 jit_solution(1825667511188258883)
XLA Ops:
  0.6 1.0 dynamic-slice_bitcast_fusion.2
  1.6 7.7 %collective-permute-start.1 = (f32[40,768]{1,0:T(8,128)S(1)}, f32[40,768]{1,0:T(8,128)S(1)}, u32[]{:S(2)}, u32[]{:S(2)}) collective-permute-start(f32[40,768]{1,0:T(8,128)S(1)} %get-tuple-element.38), channel_id=1, source_target_pairs={{1,0},{2,1},{3,2},{4,3},{5,4},{6,5},{7,6},{8,7},{9,8},{10,9},{11,1... | collective-permute-start | bytes 368648 | tf_op jit(solution)/shard_map/ppermute | solution.py:479
  9.3 0.0 collective-permute-start
  9.3 1.0 %dynamic-slice_bitcast_fusion = (f32[80,512]{1,0:T(8,128)S(1)}, f32[80,512]{1,0:T(8,128)S(1)}) fusion(f32[10,1,2048,8]{2,3,1,0:T(8,128)} %param.8, s32[]{:T(128)S(6)} %select_n.62, s32[]{:T(128)S(6)} %select_n.58), kind=kLoop, calls=%fused_computation | loop fusion | bytes 655368 | tf_op jit(solution)/shard_map/reshape | solution.py:470
  10.4 4.3 %collective-permute-start.2 = (f32[80,512]{1,0:T(8,128)S(1)}, f32[80,512]{1,0:T(8,128)S(1)}, u32[]{:S(2)}, u32[]{:S(2)}) collective-permute-start(f32[80,512]{1,0:T(8,128)S(1)} %get-tuple-element.41), channel_id=1, source_target_pairs={{0,128},{16,144},{32,160},{48,176},{64,192},{80,208},{96,224},{112... | collective-permute-start | bytes 491528 | tf_op jit(solution)/shard_map/ppermute | solution.py:481
  14.7 0.8 reshape.95
  15.4 0.7 add_select_fusion
  16.1 0.7 fusion.5
  16.8 0.9 slice_bitcast_fusion.core
  17.7 0.7 fusion.6
  18.4 0.1 pad_add_fusion.flags
  18.5 0.1 add_convert_fusion.meta
  18.5 0.0 collective-permute-done.1.high
  18.5 2.2 %collective-permute-done.low = f32[40,768]{1,0:T(8,128)S(1)} collective-permute-done((f32[40,768]{1,0:T(8,128)S(1)}, f32[40,768]{1,0:T(8,128)S(1)}, u32[]{:S(2)}, u32[]{:S(2)}) %collective-permute-start) | collective-permute-done | bytes 122912 | tf_op jit(solution)/shard_map/ppermute | solution.py:478
  20.7 1.4 %shard_map.86 = f32[8,152,128]{2,1,0:T(8,128)} custom-call(f32[40,768]{1,0:T(8,128)S(1)} %collective-permute-done.low, f32[40,768]{1,0:T(8,128)S(1)} %slice_bitcast_fusion.core, f32[40,768]{1,0:T(8,128)S(1)} %collective-permute-done.1.high, f32[8,128]{1,0:T(8,128)S(1)} %add_convert_fusion.meta), custom_call_target="tpu_custom_call" | custom-call | tf_op jit(solution)/shard_map/pallas_call | solution.py:377
  22.1 3.8 %collective-permute-done.2.partner = f32[80,512]{1,0:T(8,128)S(1)} collective-permute-done((f32[80,512]{1,0:T(8,128)S(1)}, f32[80,512]{1,0:T(8,128)S(1)}, u32[]{:S(2)}, u32[]{:S(2)}) %collective-permute-start.2) | collective-permute-done | bytes 163872 | tf_op jit(solution)/shard_map/ppermute | solution.py:481
  25.9 5.2 %all-to-all-start = ((f32[8,152,128]{2,1,0:T(8,128)}), f32[8,152,128]{2,1,0:T(8,128)}, u32[]{:S(2)}, u32[]{:S(2)}) async-start(f32[8,152,128]{2,1,0:T(8,128)} %shard_map.86), calls=%async_computation | async-start | bytes 1245184 | tf_op jit(solution)/shard_map/all_to_all | solution.py:449
  31.1 0.1 pad_add_fusion.1.place
  31.2 1.9 %shard_map.87 = (f32[208,128]{1,0:T(8,128)S(1)}, f32[208,128]{1,0:T(8,128)}, f32[208,128]{1,0:T(8,128)}, f32[208,128]{1,0:T(8,128)}) custom-call(s32[3]{0:T(128)S(1)} %pad_add_fusion.1.place, f32[80,512]{1,0:T(8,128)S(1)} %get-tuple-element.40.own, f32[80,512]{1,0:T(8,128)S(1)} %collective-permute-done.2.partner), custom_call_target="tpu_custom_call" | custom-call | tf_op jit(solution)/shard_map/pallas_call | solution.py:387
  33.1 1.5 %collective-permute-start.3 = (f32[208,128]{1,0:T(8,128)}, f32[208,128]{1,0:T(8,128)S(1)}, u32[]{:S(2)}, u32[]{:S(2)}) collective-permute-start(f32[208,128]{1,0:T(8,128)} %get-tuple-element.29), channel_id=1, source_target_pairs={{0,32},{16,48},{32,64},{48,80},{64,96},{80,112},{96,0},{112,16},{1... | collective-permute-start | bytes 319496 | tf_op jit(solution)/shard_map/ppermute | solution.py:504
  34.6 2.4 %collective-permute-start.4 = (f32[208,128]{1,0:T(8,128)}, f32[208,128]{1,0:T(8,128)}, u32[]{:S(2)}, u32[]{:S(2)}) collective-permute-start(f32[208,128]{1,0:T(8,128)} %get-tuple-element.30), channel_id=1, source_target_pairs={{0,64},{16,80},{32,96},{48,112},{64,0},{80,16},{96,32},{112,48},{1... | collective-permute-start | bytes 319496 | tf_op jit(solution)/shard_map/ppermute | solution.py:504
  37.0 1.2 %collective-permute-start.5 = (f32[208,128]{1,0:T(8,128)}, f32[208,128]{1,0:T(8,128)}, u32[]{:S(2)}, u32[]{:S(2)}) collective-permute-start(f32[208,128]{1,0:T(8,128)} %get-tuple-element.31), channel_id=1, source_target_pairs={{0,96},{16,112},{32,0},{48,16},{64,32},{80,48},{96,64},{112,80},{1... | collective-permute-start | bytes 319496 | tf_op jit(solution)/shard_map/ppermute | solution.py:504
  38.2 6.3 %reshape.98.recon = bf16[300,5376]{1,0:T(8,128)(2,1)S(1)} reshape(bf16[6,5,5,2,5376]{4,3,2,1,0:T(2,128)(2,1)} %bitcast.50) | data formatting | bytes 6451200 | tf_op jit(solution)/shard_map/reshape | solution.py:505
  44.6 0.0 all-to-all-done.mine
  44.6 0.0 collective-permute-done.3.new_1
  44.6 0.0 collective-permute-done.4.new_2
  44.6 0.3 collective-permute-done.5.new_3
  44.9 6.0 %shard_map.88 = (f32[10,80,128]{2,1,0:T(8,128)S(1)}, f32[10,80,128]{2,1,0:T(8,128)S(1)}) custom-call(s32[3]{0:T(128)S(1)} %pad_add_fusion.1.place, f32[8,152,128]{2,1,0:T(8,128)} %all-to-all-done.mine, f32[208,128]{1,0:T(8,128)S(1)} %get-tuple-element.28.new_0, f32[208,128]{1,0:T(8,128)S(1)} %collective-permute-done.3.new_1, ...), custom_call_target="tpu_custom_call" | custom-call | tf_op jit(solution)/shard_map/pallas_call | solution.py:399
  50.9 2.9 %collective-permute-start.6 = (f32[10,80,128]{2,1,0:T(8,128)S(1)}, f32[10,80,128]{2,1,0:T(8,128)S(1)}, u32[]{:S(2)}, u32[]{:S(2)}) collective-permute-start(f32[10,80,128]{2,1,0:T(8,128)S(1)} %get-tuple-element.33), channel_id=1, source_target_pairs={{0,16},{16,0},{32,48},{48,32},{64,80},{80,64},{96,112},{112,96},{1... | collective-permute-start | bytes 1228808 | tf_op jit(solution)/shard_map/ppermute | solution.py:457
  53.7 1.4 %collective-permute-done.6.there = f32[10,80,128]{2,1,0:T(8,128)S(1)} collective-permute-done((f32[10,80,128]{2,1,0:T(8,128)S(1)}, f32[10,80,128]{2,1,0:T(8,128)S(1)}, u32[]{:S(2)}, u32[]{:S(2)}) %collective-permute-start.6) | collective-permute-done | bytes 409632 | tf_op jit(solution)/shard_map/ppermute | solution.py:457
  55.1 3.5 %shard_map.89 = (f32[16,16,128]{2,1,0:T(8,128)S(1)}, f32[16,16,128]{2,1,0:T(8,128)S(1)}, f32[16,384]{1,0:T(8,128)S(1)}) custom-call(s32[26]{0:T(128)S(1)} %pad_add_fusion.flags, f32[10,80,128]{2,1,0:T(8,128)S(1)} %get-tuple-element.32.here, f32[10,80,128]{2,1,0:T(8,128)S(1)} %collective-permute-done.6.there, bf16[300,5376]{1,0:T(8,128)(2,1)S(1)} %reshape.98.recon), custom_call_target="tpu_custom_call" | custom-call | tf_op jit(solution)/shard_map/pallas_call | solution.py:416
  58.6 0.5 collective-permute-start.7
  59.1 1.0 collective-permute-done.7
  60.1 9.7 %all_to_all.20 = f32[16,16,128]{2,1,0:T(8,128)S(1)} all-to-all(f32[16,16,128]{2,1,0:T(8,128)S(1)} %add.100), channel_id=1, replica_groups={{0,4,8,12,32,36,40,44,64,68,72,76,96,100,104,108},{1,5,9,13,33,37,41,45..., dimensions={0} | all-to-all | bytes 262144 | tf_op jit(solution)/shard_map/all_to_all | solution.py:449
  69.8 13.9 %all_to_all.21 = f32[8,16,128]{2,1,0:T(8,128)S(1)} all-to-all(f32[8,16,128]{2,1,0:T(8,128)S(1)} %broadcast_in_dim.9), channel_id=1, replica_groups={{0,1,2,3,128,129,130,131},{4,5,6,7,132,133,134,135},{8,9,10,11,136,137,..., dimensions={0} | all-to-all | bytes 131072 | tf_op jit(solution)/shard_map/all_to_all | solution.py:449
  83.8 10.2 %all_to_all.22.mine = f32[16,16,128]{2,1,0:T(8,128)S(1)} all-to-all(f32[16,16,128]{2,1,0:T(8,128)S(1)} %broadcast_in_dim.18), channel_id=1, replica_groups={{0,4,8,12,32,36,40,44,64,68,72,76,96,100,104,108},{1,5,9,13,33,37,41,45..., dimensions={0} | all-to-all | bytes 262144 | tf_op jit(solution)/shard_map/all_to_all | solution.py:449
  94.0 4.3 %collective-permute-start.8 = (f32[16,16,128]{2,1,0:T(8,128)S(1)}, f32[16,16,128]{2,1,0:T(8,128)S(1)}, u32[]{:S(2)}, u32[]{:S(2)}) collective-permute-start(f32[16,16,128]{2,1,0:T(8,128)S(1)} %all_to_all.22.mine), channel_id=1, source_target_pairs={{0,16},{16,0},{32,48},{48,32},{64,80},{80,64},{96,112},{112,96},{1... | collective-permute-start | bytes 393224 | tf_op jit(solution)/shard_map/ppermute | solution.py:457
  98.2 0.1 copy.17
  98.3 0.8 reshape.99
  99.1 0.1 collective-permute-done.8.other
  99.2 0.8 shard_map.90
  (5 shorter events, 0.1 us)
Async XLA Ops:
  1.6 16.9 %collective-permute-start.1 = (f32[40,768]{1,0:T(8,128)S(1)}, f32[40,768]{1,0:T(8,128)S(1)}, u32[]{:S(2)}, u32[]{:S(2)}) collective-permute-start(f32[40,768]{1,0:T(8,128)S(1)} %get-tuple-element.38), channel_id=1, source_target_pairs={{1,0},{2,1},{3,2},{4,3},{5,4},{6,5},{7,6},{8,7},{9,8},{10,9},{11,1... | collective-permute-start | bytes 368648 | tf_op jit(solution)/shard_map/ppermute | solution.py:479
  9.3 11.4 %collective-permute-start = (f32[40,768]{1,0:T(8,128)S(1)}, f32[40,768]{1,0:T(8,128)S(1)}, u32[]{:S(2)}, u32[]{:S(2)}) collective-permute-start(f32[40,768]{1,0:T(8,128)S(1)} %get-tuple-element.39), channel_id=1, source_target_pairs={{0,1},{1,2},{2,3},{3,4},{4,5},{5,6},{6,7},{7,8},{8,9},{9,10},{10,1... | collective-permute-start | bytes 368648 | tf_op jit(solution)/shard_map/ppermute | solution.py:478
  10.4 15.6 %collective-permute-start.2 = (f32[80,512]{1,0:T(8,128)S(1)}, f32[80,512]{1,0:T(8,128)S(1)}, u32[]{:S(2)}, u32[]{:S(2)}) collective-permute-start(f32[80,512]{1,0:T(8,128)S(1)} %get-tuple-element.41), channel_id=1, source_target_pairs={{0,128},{16,144},{32,160},{48,176},{64,192},{80,208},{96,224},{112... | collective-permute-start | bytes 491528 | tf_op jit(solution)/shard_map/ppermute | solution.py:481
  25.9 18.6 %all-to-all-start = ((f32[8,152,128]{2,1,0:T(8,128)}), f32[8,152,128]{2,1,0:T(8,128)}, u32[]{:S(2)}, u32[]{:S(2)}) async-start(f32[8,152,128]{2,1,0:T(8,128)} %shard_map.86), calls=%async_computation | async-start | bytes 1245184 | tf_op jit(solution)/shard_map/all_to_all | solution.py:449
  33.1 11.5 %collective-permute-start.3 = (f32[208,128]{1,0:T(8,128)}, f32[208,128]{1,0:T(8,128)S(1)}, u32[]{:S(2)}, u32[]{:S(2)}) collective-permute-start(f32[208,128]{1,0:T(8,128)} %get-tuple-element.29), channel_id=1, source_target_pairs={{0,32},{16,48},{32,64},{48,80},{64,96},{80,112},{96,0},{112,16},{1... | collective-permute-start | bytes 319496 | tf_op jit(solution)/shard_map/ppermute | solution.py:504
  34.6 9.9 %collective-permute-start.4 = (f32[208,128]{1,0:T(8,128)}, f32[208,128]{1,0:T(8,128)}, u32[]{:S(2)}, u32[]{:S(2)}) collective-permute-start(f32[208,128]{1,0:T(8,128)} %get-tuple-element.30), channel_id=1, source_target_pairs={{0,64},{16,80},{32,96},{48,112},{64,0},{80,16},{96,32},{112,48},{1... | collective-permute-start | bytes 319496 | tf_op jit(solution)/shard_map/ppermute | solution.py:504
  37.0 7.8 %collective-permute-start.5 = (f32[208,128]{1,0:T(8,128)}, f32[208,128]{1,0:T(8,128)}, u32[]{:S(2)}, u32[]{:S(2)}) collective-permute-start(f32[208,128]{1,0:T(8,128)} %get-tuple-element.31), channel_id=1, source_target_pairs={{0,96},{16,112},{32,0},{48,16},{64,32},{80,48},{96,64},{112,80},{1... | collective-permute-start | bytes 319496 | tf_op jit(solution)/shard_map/ppermute | solution.py:504
  50.9 4.2 %collective-permute-start.6 = (f32[10,80,128]{2,1,0:T(8,128)S(1)}, f32[10,80,128]{2,1,0:T(8,128)S(1)}, u32[]{:S(2)}, u32[]{:S(2)}) collective-permute-start(f32[10,80,128]{2,1,0:T(8,128)S(1)} %get-tuple-element.33), channel_id=1, source_target_pairs={{0,16},{16,0},{32,48},{48,32},{64,80},{80,64},{96,112},{112,96},{1... | collective-permute-start | bytes 1228808 | tf_op jit(solution)/shard_map/ppermute | solution.py:457
  58.6 1.4 %collective-permute-start.7 = (f32[16,16,128]{2,1,0:T(8,128)S(1)}, f32[16,16,128]{2,1,0:T(8,128)S(1)}, u32[]{:S(2)}, u32[]{:S(2)}) collective-permute-start(f32[16,16,128]{2,1,0:T(8,128)S(1)} %get-tuple-element.37), channel_id=1, source_target_pairs={{0,16},{16,0},{32,48},{48,32},{64,80},{80,64},{96,112},{112,96},{1... | collective-permute-start | bytes 393224 | tf_op jit(solution)/shard_map/ppermute | solution.py:457
  94.0 5.2 %collective-permute-start.8 = (f32[16,16,128]{2,1,0:T(8,128)S(1)}, f32[16,16,128]{2,1,0:T(8,128)S(1)}, u32[]{:S(2)}, u32[]{:S(2)}) collective-permute-start(f32[16,16,128]{2,1,0:T(8,128)S(1)} %all_to_all.22.mine), channel_id=1, source_target_pairs={{0,16},{16,0},{32,48},{48,32},{64,80},{80,64},{96,112},{112,96},{1... | collective-permute-start | bytes 393224 | tf_op jit(solution)/shard_map/ppermute | solution.py:457
